TPU v7x, 512 devices: a whole 4x4x16 slice. The times are simulated.
512 devices in a mesh: row: 16 (over z), col: 4 (over x_hi, core), layer: 8 (over x_lo, y).
Axes of the slice: x: 4 (x_hi: 2, x_lo: 2; x = x_hi * 2 + x_lo), y: 4, z: 16, core: 2. Of those that a mesh axis runs over, the one named last changes fastest.
Arguments:
- blocks: float32 [4096, 128, 128], P(('row', 'col', 'layer')), may hold values from -0.6 to 0.6
- block_ids: int32 [4096, 2], P(('row', 'col', 'layer')), may hold values from -1 to 1535, as said below
- out_ids: int32 [4096, 2], P(('row', 'col')), may hold values from -1 to 1535, as said below
Outputs:
- products: float32 [4096, 128, 128], P(('row', 'col', 'layer'))
Inputs may be any that keep to these rules, and one draw needn't show every extreme that they name: `block_ids`: each row is the (block row, block column) of one slot, or (-1, -1) for an empty slot. The device at index (r, c, l) of (row, col, layer) holds blocks whose row is r modulo 16 and whose column is c * 8 + l modulo 4 * 8. Each row group r has between 1 and 4 block rows in use, and each column class has exactly 2 block columns in use; a device holds every block where its row group's rows in use meet its class's columns, each once, in no set order, and its other slots are empty. Some 4 + 1 row groups in a row (wrapping around) have 4 rows in use. `out_ids`: the 64 rows for the index pair (r, c) of (row, col) list, in no set order, each pair (i, j) once where i is a block row in use of row group r and j one of row group (r + 4 c + m) modulo 16 for some m < 4; the remaining rows are (-1, -1).
All inputs are finite; a program needn't handle non-finite values.
Results may differ from a plain program's by a relative error of at most 0.0003.
Values sent between devices are 32-bit elements; how exact they have to be, the bound alone decides.
No kernel may reach another device: no remote copies, remote signals or barrier semaphores. Data moves between devices by JAX's collectives and lax.ppermute only.
A program may use at most 64 MiB of HBM per device.

v0:
```python
import jax
import jax.numpy as jnp
from jax import lax
from jax.sharding import PartitionSpec as P

NB = 1536
ROWS_G = 4


HIGH = lax.Precision.HIGHEST


def shifted(value, axis, steps):
    count = lax.axis_size(axis)
    pairs = [(source, (source + steps) % count) for source in range(count)]
    return lax.ppermute(value, axis, pairs)


def arrange(panel_blocks, panel_coords, row_total):
    slot_total = panel_blocks.shape[0]
    width = panel_blocks.shape[1]
    per_row = slot_total // row_total
    row_ids = panel_coords[:, 0]
    col_ids = panel_coords[:, 1]
    slot_range = jnp.arange(slot_total, dtype=jnp.int32)
    sort_key = jnp.where(row_ids >= 0, row_ids * NB + col_ids, 2**30 + slot_range)
    rank_of = jnp.sum((sort_key[None, :] < sort_key[:, None]).astype(jnp.int32), axis=1)
    gather_order = jnp.sum(
        jnp.where(rank_of[None, :] == slot_range[:, None], slot_range[None, :], 0), axis=1
    )
    ordered = jnp.take(panel_blocks, gather_order, axis=0)
    row_heads = jnp.take(row_ids, gather_order)[::per_row]
    shaped = ordered.reshape(row_total, per_row, width, width).transpose(0, 2, 1, 3)
    shaped = shaped.reshape(row_total, width, per_row * width)
    shaped = jnp.where((row_heads >= 0)[:, None, None], shaped, jnp.float32(0.0))
    return (shaped.reshape(row_total * width, per_row * width), row_heads)


def locate(targets, heads):
    hits = (targets[:, None] == heads[None, :]) & (targets[:, None] >= 0)
    found = jnp.any(hits, axis=1)
    head_range = jnp.arange(heads.shape[0], dtype=jnp.int32)
    where_at = jnp.sum(jnp.where(hits, head_range[None, :], 0), axis=1)
    return (where_at, found)


def shards(blocks, block_ids, out_ids):
    row_count = lax.axis_size("row")
    col_count = lax.axis_size("col")
    stride = row_count // col_count
    col_index = lax.axis_index("col")
    width = blocks.shape[1]
    left_blocks, left_coords = (
        lax.all_gather(blocks, "col", axis=0, tiled=True),
        lax.all_gather(block_ids, "col", axis=0, tiled=True),
    )
    base_blocks, base_coords = (left_blocks, left_coords)
    far_blocks, far_coords = (left_blocks, left_coords)
    for offset in range(1, col_count):
        far_blocks, far_coords = shifted((far_blocks, far_coords), "row", row_count - stride)
        chosen = col_index == offset
        base_blocks = jnp.where(chosen, far_blocks, base_blocks)
        base_coords = jnp.where(chosen, far_coords, base_coords)
    block_list = [base_blocks]
    coord_list = [base_coords]
    for offset in range(1, stride):
        far_blocks, far_coords = shifted((block_list[-1], coord_list[-1]), "row", row_count - 1)
        block_list.append(far_blocks)
        coord_list.append(far_coords)
    stack_blocks = jnp.stack(block_list, axis=0)
    stack_coords = jnp.stack(coord_list, axis=0)
    left_dense, left_heads = arrange(left_blocks, left_coords, ROWS_G)
    right_dense, right_heads = jax.vmap(
        lambda stack_piece, coord_piece: arrange(stack_piece, coord_piece, ROWS_G)
    )(stack_blocks, stack_coords)
    right_dense = right_dense.reshape(-1, right_dense.shape[-1])
    right_heads = right_heads.reshape(-1)
    right_total = right_heads.shape[0]
    partial_all = lax.dot_general(
        left_dense,
        right_dense,
        (((1,), (1,)), ((), ())),
        precision=HIGH,
        preferred_element_type=jnp.float32,
    )
    tiled = (
        partial_all.reshape(ROWS_G, width, right_total, width)
        .transpose(0, 2, 1, 3)
        .reshape(ROWS_G * right_total, width, width)
    )
    left_at, left_found = locate(out_ids[:, 0], left_heads)
    right_at, right_found = locate(out_ids[:, 1], right_heads)
    picked = jnp.take(tiled, left_at * right_total + right_at, axis=0)
    picked = jnp.where((left_found & right_found)[:, None, None], picked, jnp.float32(0.0))
    return lax.psum_scatter(picked, "layer", scatter_dimension=0, tiled=True)


def solution(mesh):
    return jax.shard_map(
        shards,
        mesh=mesh,
        in_specs=(
            P(("row", "col", "layer"), None, None),
            P(("row", "col", "layer"), None),
            P(("row", "col"), None),
        ),
        out_specs=P(("row", "col", "layer"), None, None),
        check_vma=False,
    )
```

profile of v0, /device:TPU:1, one launch (start us, length us, event | category | flops | bytes accessed | tf_op | source)
XLA Modules:
  0.0 921.1 jit_solution(10634318678526448864)
XLA Ops:
  7.3 42.2 %all-gather.3.cloned.1.call-done = f32[32,128,128]{2,1,0:T(8,128)} async-done(((f32[8,128,128]{2,1,0:T(8,128)}), f32[32,128,128]{2,1,0:T(8,128)}) %all-gather.3.cloned.1.call-update) | async-done | bytes 2097168 | tf_op jit(solution)/shard_map/all_gather | solution.py:54
  49.5 8.1 collective-permute-start.6
  57.6 283.4 %collective-permute-done.6 = f32[32,128,128]{2,1,0:T(8,128)S(1)} collective-permute-done((f32[32,128,128]{2,1,0:T(8,128)}, f32[32,128,128]{2,1,0:T(8,128)S(1)}, u32[]{:S(2)}, u32[]{:S(2)}) %collective-permute-start.6) | collective-permute-done | bytes 2097184 | tf_op jit(solution)/shard_map/ppermute | solution.py:16
  342.3 9.6 %collective-permute-start.7 = (f32[32,128,128]{2,1,0:T(8,128)S(1)}, f32[32,128,128]{2,1,0:T(8,128)S(1)}, u32[]{:S(2)}, u32[]{:S(2)}) collective-permute-start(f32[32,128,128]{2,1,0:T(8,128)S(1)} %collective-permute-done.6), channel_id=1, source_target_pairs={{0,384},{32,416},{64,448},{96,480},{128,0},{160,32},{192,64},{224,... | collective-permute-start | bytes 6291464 | tf_op jit(solution)/shard_map/ppermute | solution.py:16
  351.9 178.9 %collective-permute-done.7 = f32[32,128,128]{2,1,0:T(8,128)S(1)} collective-permute-done((f32[32,128,128]{2,1,0:T(8,128)S(1)}, f32[32,128,128]{2,1,0:T(8,128)S(1)}, u32[]{:S(2)}, u32[]{:S(2)}) %collective-permute-start.7) | collective-permute-done | bytes 2097184 | tf_op jit(solution)/shard_map/ppermute | solution.py:16
  532.8 68.6 %collective-permute-done.8 = f32[32,128,128]{2,1,0:T(8,128)} collective-permute-done((f32[32,128,128]{2,1,0:T(8,128)S(1)}, f32[32,128,128]{2,1,0:T(8,128)}, u32[]{:S(2)}, u32[]{:S(2)}) %collective-permute-start.8) | collective-permute-done | bytes 2097184 | tf_op jit(solution)/shard_map/ppermute | solution.py:16
  605.7 12.6 %all-gather = s32[4,8,2]{1,2,0:T(2,128)S(1)} all-gather(s32[1,8,2]{1,2,0:T(2,128)S(1)} %bitcast.72), channel_id=1, replica_groups=mesh['row'=16,'col'=4,'layer'=8] {'col'}, dimensions={0}, use_global_device_ids=true | all-gather | bytes 320 | tf_op jit(solution)/shard_map/all_gather | solution.py:55
  618.4 6.9 collective-permute-start
  625.7 21.0 %collective-permute-done.9 = f32[32,128,128]{2,1,0:T(8,128)} collective-permute-done((f32[32,128,128]{2,1,0:T(8,128)S(1)}, f32[32,128,128]{2,1,0:T(8,128)}, u32[]{:S(2)}, u32[]{:S(2)}) %collective-permute-start.9) | collective-permute-done | bytes 2097184 | tf_op jit(solution)/shard_map/ppermute | solution.py:16
  646.7 8.3 collective-permute-start.10
  655.7 5.2 collective-permute-done
  663.0 47.3 %collective-permute-done.1 = s32[32,2]{0,1:T(2,128)S(1)} collective-permute-done((s32[32,2]{0,1:T(2,128)S(1)}, s32[32,2]{0,1:T(2,128)S(1)}, u32[]{:S(2)}, u32[]{:S(2)}) %collective-permute-start.1) | collective-permute-done | bytes 288 | tf_op jit(solution)/shard_map/ppermute | solution.py:16
  712.2 6.3 collective-permute-done.2
  727.2 4.5 collective-permute-start.5
  732.4 5.0 collective-permute-start.11
  747.0 28.7 %collective-permute-done.11 = f32[32,128,128]{2,1,0:T(8,128)} collective-permute-done((f32[32,128,128]{2,1,0:T(8,128)}, f32[32,128,128]{2,1,0:T(8,128)}, u32[]{:S(2)}, u32[]{:S(2)}) %collective-permute-start.11) | collective-permute-done | bytes 2097184 | tf_op jit(solution)/shard_map/ppermute | solution.py:16
  775.7 5.9 pad_maximum_fusion
  781.6 7.7 gather_fusion.4
  793.5 9.7 %copy.27 = f32[4,4,128,8,128]{4,3,2,1,0:T(8,128)} copy(f32[4,4,128,8,128]{4,2,3,1,0:T(8,128)S(1)} %select_bitcast_fusion) | data formatting | bytes 16777216 | tf_op jit(solution)/shard_map/vmap(jit(_where))/select_n | solution.py:35
  803.2 9.3 %reshape.227 = f32[16,128,1024,1]{2,1,0,3:T(8,128)} reshape(f32[4,4,128,8,128]{4,3,2,1,0:T(8,128)} %copy.27) | data formatting | bytes 16777216 | tf_op jit(solution)/shard_map/vmap(jit(_where))/select_n | solution.py:35
  812.5 17.6 %fusion = f32[4,128,16,128]{3,1,2,0:T(8,128)} fusion(f32[16,128,1024,1]{2,1,0,3:T(8,128)} %reshape.227, f32[4,128,1024,1]{2,1,0,3:T(8,128)S(1)} %reshape.226), kind=kOutput, calls=%fused_computation.8 | convolution fusion | flops 12884901888 | bytes 14680064 | tf_op jit(solution)/shard_map/dot_general | solution.py:79
  830.1 4.9 gather_fusion.2
  835.0 4.6 select_select_fusion
  839.7 74.6 %reduce-scatter.2.cloned.1.call-done = f32[8,128,128]{2,1,0:T(8,128)} async-done(((f32[64,128,128]{2,1,0:T(8,128)}), f32[8,128,128]{2,1,0:T(8,128)}) %reduce-scatter.2.cloned.1.call-update) | async-done | bytes 524304 | tf_op jit(solution)/shard_map/reduce_scatter | solution.py:95
  (71 shorter events, 36.6 us)
Async XLA Ops:
  6.5 43.0 %all-gather.3.cloned.1.call-start = ((), (), s32[]{:S(2)}) async-start(), calls=%async_computation.1 | async-start | bytes 2621440 | tf_op jit(solution)/shard_map/all_gather | solution.py:54
  7.3 907.0 %reduce-scatter.2.cloned.1.call-start = ((), (), s32[]{:S(2)}) async-start(), calls=%async_computation.2 | async-start | bytes 4718592 | tf_op jit(solution)/shard_map/reduce_scatter | solution.py:95
  49.5 291.5 %collective-permute-start.6 = (f32[32,128,128]{2,1,0:T(8,128)}, f32[32,128,128]{2,1,0:T(8,128)S(1)}, u32[]{:S(2)}, u32[]{:S(2)}) collective-permute-start(f32[32,128,128]{2,1,0:T(8,128)} %all-gather.3.cloned.1.call-done), channel_id=1, source_target_pairs={{0,384},{32,416},{64,448},{96,480},{128,0},{160,32},{192,64},{224,... | collective-permute-start | bytes 6291464 | tf_op jit(solution)/shard_map/ppermute | solution.py:16
  341.0 1.3 copy-start.1
  342.3 188.5 %collective-permute-start.7 = (f32[32,128,128]{2,1,0:T(8,128)S(1)}, f32[32,128,128]{2,1,0:T(8,128)S(1)}, u32[]{:S(2)}, u32[]{:S(2)}) collective-permute-start(f32[32,128,128]{2,1,0:T(8,128)S(1)} %collective-permute-done.6), channel_id=1, source_target_pairs={{0,384},{32,416},{64,448},{96,480},{128,0},{160,32},{192,64},{224,... | collective-permute-start | bytes 6291464 | tf_op jit(solution)/shard_map/ppermute | solution.py:16
  530.8 1.9 copy-start.2
  530.8 70.6 %collective-permute-start.8 = (f32[32,128,128]{2,1,0:T(8,128)S(1)}, f32[32,128,128]{2,1,0:T(8,128)}, u32[]{:S(2)}, u32[]{:S(2)}) collective-permute-start(f32[32,128,128]{2,1,0:T(8,128)S(1)} %collective-permute-done.7), channel_id=1, source_target_pairs={{0,384},{32,416},{64,448},{96,480},{128,0},{160,32},{192,64},{224,... | collective-permute-start | bytes 6291464 | tf_op jit(solution)/shard_map/ppermute | solution.py:16
  532.8 73.0 %copy-start.4 = (s32[8,2]{0,1:T(2,128)S(1)}, s32[8,2]{0,1:T(2,128)}, u32[]{:S(2)}) copy-start(s32[8,2]{0,1:T(2,128)} %param.4) | copy-start | bytes 196
  532.8 92.9 %copy-start.3 = (s32[64,2]{0,1:T(2,128)S(1)}, s32[64,2]{0,1:T(2,128)}, u32[]{:S(2)}) copy-start(s32[64,2]{0,1:T(2,128)} %param.5) | copy-start | bytes 1540
  603.8 128.6 %copy-start = (f32[32,128,128]{2,1,0:T(8,128)}, f32[32,128,128]{2,1,0:T(8,128)S(1)}, u32[]{:S(2)}) copy-start(f32[32,128,128]{2,1,0:T(8,128)S(1)} %select_select_fusion.1) | copy-start | bytes 6291460
  603.8 42.9 %collective-permute-start.9 = (f32[32,128,128]{2,1,0:T(8,128)S(1)}, f32[32,128,128]{2,1,0:T(8,128)}, u32[]{:S(2)}, u32[]{:S(2)}) collective-permute-start(f32[32,128,128]{2,1,0:T(8,128)S(1)} %select_select_fusion.1), channel_id=1, source_target_pairs={{0,480},{32,0},{64,32},{96,64},{128,96},{160,128},{192,160},{224,1... | collective-permute-start | bytes 6291464 | tf_op jit(solution)/shard_map/ppermute | solution.py:16
  618.4 42.6 %collective-permute-start = (s32[32,2]{0,1:T(2,128)S(1)}, s32[32,2]{0,1:T(2,128)S(1)}, u32[]{:S(2)}, u32[]{:S(2)}) collective-permute-start(s32[32,2]{0,1:T(2,128)S(1)} %reshape.225), channel_id=1, source_target_pairs={{0,384},{32,416},{64,448},{96,480},{128,0},{160,32},{192,64},{224,... | collective-permute-start | bytes 776 | tf_op jit(solution)/shard_map/ppermute | solution.py:16
  646.7 85.7 %collective-permute-start.10 = (f32[32,128,128]{2,1,0:T(8,128)}, f32[32,128,128]{2,1,0:T(8,128)}, u32[]{:S(2)}, u32[]{:S(2)}) collective-permute-start(f32[32,128,128]{2,1,0:T(8,128)} %collective-permute-done.9), channel_id=1, source_target_pairs={{0,480},{32,0},{64,32},{96,64},{128,96},{160,128},{192,160},{224,1... | collective-permute-start | bytes 6291464 | tf_op jit(solution)/shard_map/ppermute | solution.py:16
  661.0 49.3 %collective-permute-start.1 = (s32[32,2]{0,1:T(2,128)S(1)}, s32[32,2]{0,1:T(2,128)S(1)}, u32[]{:S(2)}, u32[]{:S(2)}) collective-permute-start(s32[32,2]{0,1:T(2,128)S(1)} %collective-permute-done), channel_id=1, source_target_pairs={{0,384},{32,416},{64,448},{96,480},{128,0},{160,32},{192,64},{224,... | collective-permute-start | bytes 776 | tf_op jit(solution)/shard_map/ppermute | solution.py:16
  710.2 8.2 collective-permute-start.2
  718.5 4.3 collective-permute-start.3
  722.8 4.4 collective-permute-start.4
  727.2 5.2 collective-permute-start.5
  732.4 43.3 %collective-permute-start.11 = (f32[32,128,128]{2,1,0:T(8,128)}, f32[32,128,128]{2,1,0:T(8,128)}, u32[]{:S(2)}, u32[]{:S(2)}) collective-permute-start(f32[32,128,128]{2,1,0:T(8,128)} %collective-permute-done.10), channel_id=1, source_target_pairs={{0,480},{32,0},{64,32},{96,64},{128,96},{160,128},{192,160},{224,1... | collective-permute-start | bytes 6291464 | tf_op jit(solution)/shard_map/ppermute | solution.py:16
Sparse Core Ops, SparseCore 0:
  9.5 39.9 all-gather.2
  839.8 74.4 reduce-scatter.1
where the time goes:
time: 922 us; the launch traced here: 921 us
  waiting for transfers between devices  760 us (82%)
  starting transfers between devices  55.6 us (6%)
  local copies, waits for them, and re-layouts  42.5 us (5%)
  other arithmetic  18.6 us (2%)
  matrix products  17.6 us (2%)
  between operations  13.7 us (1%)
  blocking collectives  12.6 us (1%)
    ppermute x12, waiting for transfers between devices, shifted(): return lax.ppermute(value, axis, pairs)  643 us
    reduce_scatter x1, waiting for transfers between devices, shards(): return lax.psum_scatter(picked, 'layer', scatter_dimension=0, tiled=True)  74.6 us
    ppermute x12, starting transfers between devices, shifted(): return lax.ppermute(value, axis, pairs)  55.6 us
    all_gather x1, waiting for transfers between devices, shards(): lax.all_gather(blocks, 'col', axis=0, tiled=True)  42.2 us
    select_n x4, local copies, waits for them, and re-layouts, arrange(): jnp.where((row_heads >= 0)[:, None, None], shaped, jnp.float32(0.0))  23.3 us
  transfers between devices with their start and end apart: 14, of which 13 were waited for; matrix products, arithmetic and copies ran while one was open for 1% of the time, Pallas kernels for 0%

commit v1 on v0

v1 whole, which is shorter than its diff:
```python
import functools

import jax
import jax.numpy as jnp
import numpy as np
from jax import lax
from jax.experimental import pallas as pl
from jax.experimental.pallas import tpu as pltpu
from jax.sharding import Mesh
from jax.sharding import PartitionSpec as P

NB = 1536
NZ = 16
AXES = ("z", "xhi", "core", "xlo", "y")
LEFT = (0, -4, 4, 1)
RIGHT = (0, 0, -4, -3)
YA, YB, XA, XB = range(4)
ORDERS = {
    (0, 0): (YA, XA, YB, XB),
    (0, 1): (XA, YB, XB, YA),
    (1, 0): (YB, XB, YA, XA),
    (1, 1): (XB, YA, XA, YB),
}


def flat(z, xhi, core, xlo, y):
    return (((z % NZ * 2 + xhi) * 2 + core) * 2 + xlo) * 4 + y


def coords():
    for z in range(NZ):
        for xhi in range(2):
            for core in range(2):
                for xlo in range(2):
                    for y in range(4):
                        yield z, xhi, core, xlo, y


def send(value, target):
    pairs = []
    for at in coords():
        to = target(*at)
        if to is not None:
            pairs.append((flat(*at), flat(*to)))
    return lax.ppermute(value, AXES, pairs)


def other_core(z, xhi, core, xlo, y):
    return z, xhi, 1 - core, xlo, y


def ring_z(z, xhi, core, xlo, y):
    return (z - 1 if core == 0 else z + 1), xhi, core, xlo, y


def across(dim, x, y):
    if dim == YA:
        return x, y ^ 1
    if dim == YB:
        return x, (3 - y)
    if dim == XA:
        return x ^ 1, y
    return 3 - x, y


def plane_step(half, step):
    def target(z, xhi, core, xlo, y):
        x, ny = across(ORDERS[core, half][step], xhi * 2 + xlo, y)
        return z, x // 2, core, x % 2, ny

    return target


def home(chunk, same):
    def target(z, xhi, core, xlo, y):
        c = ((0, 3), (1, 2))[chunk][xhi]
        if (core == c % 2) != same:
            return None
        return z + LEFT[c], xhi, c % 2, xlo, y

    return target


def dest_table():
    table = np.zeros((2, 16, 2, 16), np.int32)
    for core in range(2):
        for x in range(4):
            for y in range(4):
                for half in range(2):
                    for index in range(16):
                        nx, ny = x, y
                        for step in range(4):
                            if index >> (3 - step) & 1:
                                nx, ny = across(ORDERS[core, half][step], nx, ny)
                        table[core, x * 4 + y, half, index] = nx * 4 + ny
    return table.reshape(-1)


def sort_kernel(ids_ref, blocks_ref, out_ref, sems):
    count = blocks_ref.shape[0]
    keys = []
    for s in range(count):
        row = ids_ref[2 * s]
        keys.append(jnp.where(row >= 0, row * NB + ids_ref[2 * s + 1], 2**30 + s))
    copies = []
    for s in range(count):
        rank = jnp.int32(0)
        for o in range(count):
            if o != s:
                rank = rank + jnp.where(keys[o] < keys[s], 1, 0)
        copies.append(pltpu.make_async_copy(blocks_ref.at[s], out_ref.at[rank], sems.at[s]))
    for copy in copies:
        copy.start()
    for copy in copies:
        copy.wait()


def sort_blocks(block_ids, blocks):
    return pl.pallas_call(
        sort_kernel,
        out_shape=jax.ShapeDtypeStruct(blocks.shape, blocks.dtype),
        in_specs=[
            pl.BlockSpec(memory_space=pltpu.SMEM),
            pl.BlockSpec(memory_space=pl.ANY),
        ],
        out_specs=pl.BlockSpec(memory_space=pl.ANY),
        scratch_shapes=[pltpu.SemaphoreType.DMA((blocks.shape[0],))],
        name="sort_blocks",
    )(block_ids.reshape(-1), blocks)


def chunk_kernel(chunk, reach, where_ref, codes_ref, table_ref, *refs):
    panels = refs[: 2 + 4 * reach]
    keep0, send0, keep1, send1, hi_ref, lo_ref = refs[2 + 4 * reach :]
    core = where_ref[0]
    place = where_ref[1]

    def put(panel, row, quarter):
        for rho in range(4):
            for col in range(2):
                x = panel[2 * rho + col]
                hi = x.astype(jnp.bfloat16)
                lo = (x - hi.astype(jnp.float32)).astype(jnp.bfloat16)
                at = ((row + 4) * 4 + rho) * 2 + quarter
                hi_ref[at, :, col * 128 : (col + 1) * 128] = hi
                lo_ref[at, :, col * 128 : (col + 1) * 128] = lo

    put(panels[0], 0, core)
    put(panels[1], 0, 1 - core)
    for k in range(1, reach + 1):
        mine_a, mine_b, their_a, their_b = panels[4 * k - 2 : 4 * k + 2]
        ahead = jnp.where(core == 0, k, -k)
        put(mine_a, ahead, core)
        put(mine_b, ahead, 1 - core)
        put(their_a, -ahead, 1 - core)
        put(their_b, -ahead, core)

    lists = ((0, 3), (1, 2))[chunk]

    def product(left, right):
        total = None
        for quarter in range(2):
            lh = hi_ref[left * 2 + quarter]
            ll = lo_ref[left * 2 + quarter]
            rh = hi_ref[right * 2 + quarter]
            rl = lo_ref[right * 2 + quarter]
            for a, b in ((lh, rh), (lh, rl), (ll, rh)):
                term = lax.dot_general(
                    a, b, (((1,), (1,)), ((), ())), preferred_element_type=jnp.float32
                )
                total = term if total is None else total + term
        return total

    for half, (kept, sent) in enumerate(((keep0, send0), (keep1, send1))):
        for side, out in enumerate((kept, sent)):

            def body(index, carry, half=half, side=side, out=out):
                spot = index // 2
                dest = table_ref[(core * 16 + place) * 32 + half * 16 + side * 8 + spot]
                far = dest // 8
                layer = dest % 8
                slot = layer * 8 + core * 4 + half * 2 + index % 2
                code = codes_ref[jnp.where(far == 0, lists[0], lists[1]) * 64 + slot]
                good = code >= 0
                code = jnp.maximum(code, 0)
                left_row = jnp.where(far == 0, LEFT[lists[0]], LEFT[lists[1]])
                right_row = jnp.where(far == 0, RIGHT[lists[0]], RIGHT[lists[1]])
                left = (left_row + 4) * 4 + code // 16
                right = (right_row + 4) * 4 + code % 16
                out[index] = jnp.where(good, product(left, right), jnp.float32(0.0))
                return carry

            lax.fori_loop(0, 16, body, 0, unroll=2)


def chunk_products(chunk, reach, where, codes, table, panels):
    piece = jax.ShapeDtypeStruct((16, 128, 128), jnp.float32)
    vmem = pl.BlockSpec(memory_space=pltpu.VMEM)
    smem = pl.BlockSpec(memory_space=pltpu.SMEM)
    return pl.pallas_call(
        functools.partial(chunk_kernel, chunk, reach),
        out_shape=[piece] * 4,
        in_specs=[smem] * 3 + [vmem] * len(panels),
        out_specs=[vmem] * 4,
        scratch_shapes=[
            pltpu.VMEM((72, 128, 256), jnp.bfloat16),
            pltpu.VMEM((72, 128, 256), jnp.bfloat16),
        ],
        compiler_params=pltpu.CompilerParams(vmem_limit_bytes=40 << 20),
        name=f"products_{chunk}",
    )(where, codes, table, *panels)


def slot_codes(out_ids, row, col):
    i = out_ids[:, 0]
    j = out_ids[:, 1]
    good = (i >= 0) & (j >= 0)
    same_j = (j[None, :] == j[:, None]) & good[None, :]
    same_i = (i[None, :] == i[:, None]) & good[None, :]
    group = lax.rem(j, NZ)
    left = jnp.sum((same_j & (i[None, :] < i[:, None])).astype(jnp.int32), axis=1)
    right = jnp.sum(
        (same_i & (group[None, :] == group[:, None]) & (j[None, :] < j[:, None])).astype(jnp.int32),
        axis=1,
    )
    step = lax.rem(group - row - 4 * col + 8 * NZ, NZ)
    return jnp.where(good, left * 16 + step * 4 + right, -1)


def halve(keeps, sends):
    for step in range(4):
        received = [send(sends[h], plane_step(h, step)) for h in range(2)]
        if step == 3:
            return [keeps[h] + received[h] for h in range(2)]
        mid = keeps[0].shape[0] // 2
        sends = [keeps[h][mid:] + received[h][mid:] for h in range(2)]
        keeps = [keeps[h][:mid] + received[h][:mid] for h in range(2)]


def bring_home(chunk, halves):
    part = jnp.concatenate(halves, axis=0)
    return send(part, home(chunk, True)), send(part, home(chunk, False))


def shards(blocks, block_ids, out_ids):
    z = lax.axis_index("z")
    xhi = lax.axis_index("xhi")
    core = lax.axis_index("core")
    x = xhi * 2 + lax.axis_index("xlo")
    where = jnp.stack([core, x * 4 + lax.axis_index("y")]).astype(jnp.int32)
    table = jnp.asarray(dest_table())

    mine_a = [sort_blocks(block_ids, blocks)]
    mine_b = [send(mine_a[0], other_core)]
    their_a, their_b = [None], [None]
    for k in range(1, 5):
        mine_a.append(send(mine_a[-1], ring_z))
        mine_b.append(send(mine_b[-1], ring_z))
        their_a.append(send(mine_a[k], other_core))
        their_b.append(send(mine_b[k], other_core))

    codes = slot_codes(out_ids, z, xhi * 2 + core)

    def to_place(z, xhi, core, xlo, y):
        return z - LEFT[xhi * 2 + core], xhi, core, xlo, y

    codes = lax.all_gather(send(codes, to_place), ("xhi", "core"), axis=0, tiled=True)

    def panels(reach):
        out = [mine_a[0], mine_b[0]]
        for k in range(1, reach + 1):
            out += [mine_a[k], mine_b[k], their_a[k], their_b[k]]
        return out

    results = []
    for chunk, reach in ((0, 3), (1, 4)):
        keep0, send0, keep1, send1 = chunk_products(chunk, reach, where, codes, table, panels(reach))
        results.append(bring_home(chunk, halve([keep0, keep1], [send0, send1])))
    same = jnp.where(core == xhi, results[0][0], results[1][0])
    cross = jnp.where(core == xhi, results[0][1], results[1][1])
    first = jnp.where(core == 0, same, cross)
    second = jnp.where(core == 0, cross, same)
    layers = jnp.concatenate([first, second], axis=0)
    return layers


def solution(mesh):
    fine = Mesh(mesh.devices.reshape(16, 2, 2, 2, 4), AXES)
    return jax.shard_map(
        shards,
        mesh=fine,
        in_specs=(P(AXES, None, None), P(AXES, None), P(("z", "xhi", "core"), None)),
        out_specs=P(AXES, None, None),
        check_vma=False,
    )
```

time: 922 us -> 241 us (0.26)
  the two profiles are of different devices: /device:TPU:1 before, /device:TPU:12 now
where the time goes in v1:
time: 241 us; the launch traced here: 240 us
  starting transfers between devices  124 us (51%)
  Pallas kernels  49.2 us (20%)
  waiting for transfers between devices  48.7 us (20%)
  local copies, waits for them, and re-layouts  8.28 us (3%)
  blocking collectives  5.78 us (2%)
    ppermute x38, starting transfers between devices, send(): return lax.ppermute(value, AXES, pairs)  124 us
    ppermute x38, waiting for transfers between devices, send(): return lax.ppermute(value, AXES, pairs)  48.7 us
    pallas_call x2, Pallas kernels, chunk_products(): pl.pallas_call(functools.partial(chunk_kernel, chunk, reach), out_shape=[...  31.5 us
    pallas_call x1, Pallas kernels, sort_blocks(): pl.pallas_call(sort_kernel, out_shape=jax.ShapeDtypeStruct(blocks.shape,...  17.7 us
    unnamed x24, local copies, waits for them, and re-layouts  7.63 us
    unnamed x1, blocking collectives  5.78 us
  transfers between devices with their start and end apart: 38, of which 9 were waited for; matrix products, arithmetic and copies ran while one was open for 1% of the time, Pallas kernels for 13%

profile of v1, /device:TPU:12, one launch (start us, length us, event | category | flops | bytes accessed | tf_op | source)
XLA Modules:
  0.0 239.6 jit_solution(3597174283282430047)
XLA Ops:
  1.4 17.7 %sort_blocks.1.refs_0_ = f32[8,128,128]{2,1,0:T(8,128)} custom-call(s32[16]{0:T(128)} %reshape.32.ids_ref, f32[8,128,128]{2,1,0:T(8,128)} %blocks_ref.1), custom_call_target="tpu_custom_call" | custom-call | tf_op jit(solution)/shard_map/sort_blocks/pallas_call | solution.py:119
  21.1 11.4 %collective-permute-start.2 = (f32[8,128,128]{2,1,0:T(8,128)}, f32[8,128,128]{2,1,0:T(8,128)S(1)}, u32[]{:S(2)}, u32[]{:S(2)}) collective-permute-start(f32[8,128,128]{2,1,0:T(8,128)} %sort_blocks.1.refs_0_), channel_id=1, source_target_pairs={{0,480},{1,481},{2,482},{3,483},{4,484},{5,485},{6,486},{7,487},{8... | collective-permute-start | bytes 1572872 | tf_op jit(solution)/shard_map/ppermute | solution.py:45
  36.1 3.4 %collective-permute-done.2.refs_2_ = f32[8,128,128]{2,1,0:T(8,128)S(1)} collective-permute-done((f32[8,128,128]{2,1,0:T(8,128)}, f32[8,128,128]{2,1,0:T(8,128)S(1)}, u32[]{:S(2)}, u32[]{:S(2)}) %collective-permute-start.2) | collective-permute-done | bytes 524320 | tf_op jit(solution)/shard_map/ppermute | solution.py:45
  39.5 5.5 %collective-permute-start.6 = (f32[8,128,128]{2,1,0:T(8,128)S(1)}, f32[8,128,128]{2,1,0:T(8,128)S(1)}, u32[]{:S(2)}, u32[]{:S(2)}) collective-permute-start(f32[8,128,128]{2,1,0:T(8,128)S(1)} %collective-permute-done.2.refs_2_), channel_id=1, source_target_pairs={{0,480},{1,481},{2,482},{3,483},{4,484},{5,485},{6,486},{7,487},{8... | collective-permute-start | bytes 1572872 | tf_op jit(solution)/shard_map/ppermute | solution.py:45
  45.0 5.6 %collective-permute-start.7 = (f32[8,128,128]{2,1,0:T(8,128)S(1)}, f32[8,128,128]{2,1,0:T(8,128)S(1)}, u32[]{:S(2)}, u32[]{:S(2)}) collective-permute-start(f32[8,128,128]{2,1,0:T(8,128)S(1)} %collective-permute-done.3.refs_3_), channel_id=1, source_target_pairs={{0,480},{1,481},{2,482},{3,483},{4,484},{5,485},{6,486},{7,487},{8... | collective-permute-start | bytes 1572872 | tf_op jit(solution)/shard_map/ppermute | solution.py:45
  52.8 4.5 %collective-permute-start.10 = (f32[8,128,128]{2,1,0:T(8,128)S(1)}, f32[8,128,128]{2,1,0:T(8,128)}, u32[]{:S(2)}, u32[]{:S(2)}) collective-permute-start(f32[8,128,128]{2,1,0:T(8,128)S(1)} %collective-permute-done.6.refs_6_), channel_id=1, source_target_pairs={{0,480},{1,481},{2,482},{3,483},{4,484},{5,485},{6,486},{7,487},{8... | collective-permute-start | bytes 1572872 | tf_op jit(solution)/shard_map/ppermute | solution.py:45
  57.3 5.6 %collective-permute-start.11 = (f32[8,128,128]{2,1,0:T(8,128)S(1)}, f32[8,128,128]{2,1,0:T(8,128)}, u32[]{:S(2)}, u32[]{:S(2)}) collective-permute-start(f32[8,128,128]{2,1,0:T(8,128)S(1)} %collective-permute-done.7.refs_7_), channel_id=1, source_target_pairs={{0,480},{1,481},{2,482},{3,483},{4,484},{5,485},{6,486},{7,487},{8... | collective-permute-start | bytes 1572872 | tf_op jit(solution)/shard_map/ppermute | solution.py:45
  62.9 5.5 %collective-permute-start = (s32[64]{0:T(128)S(1)}, s32[64]{0:T(128)S(1)}, u32[]{:S(2)}, u32[]{:S(2)}) collective-permute-start(s32[64]{0:T(128)S(1)} %fusion.11), channel_id=1, source_target_pairs={{0,0},{1,1},{2,2},{3,3},{4,4},{5,5},{6,6},{7,7},{8,136},{9,137},{1... | collective-permute-start | bytes 776 | tf_op jit(solution)/shard_map/ppermute | solution.py:45
  88.6 5.8 %all-reduce.codes_ref = s32[256]{0:T(256)S(1)} all-reduce(s32[256]{0:T(256)S(1)} %dynamic-update-slice), channel_id=1, replica_groups=mesh['z'=16,'xhi'=2,'core'=2,'xlo'=2,'y'=4] {'xhi','core'}, use_global_device_ids=true, to_apply=%add | all-reduce | flops 256 | bytes 2048
  97.5 15.5 %products_0.1 = (f32[16,128,128]{2,1,0:T(8,128)S(1)}, f32[16,128,128]{2,1,0:T(8,128)S(1)}, f32[16,128,128]{2,1,0:T(8,128)S(1)}, f32[16,128,128]{2,1,0:T(8,128)S(1)}) custom-call(s32[2]{0:T(128)S(1)} %pad_add_fusion.where_ref, s32[256]{0:T(256)S(1)} %all-reduce.codes_ref, s32[1024]{0:T(1024)S(1)} %copy-done.8, f32[8,128,128]{2,1,0:T(8,128)S(1)} %copy-done, ...), custom_call_target="tpu_custom_call" | custom-call | tf_op jit(solution)/shard_map/products_0/pallas_call | solution.py:200
  119.7 3.1 %collective-permute-start.18 = (f32[16,128,128]{2,1,0:T(8,128)S(1)}, f32[16,128,128]{2,1,0:T(8,128)S(1)}, u32[]{:S(2)}, u32[]{:S(2)}) collective-permute-start(f32[16,128,128]{2,1,0:T(8,128)S(1)} %get-tuple-element.16), channel_id=1, source_target_pairs={{0,4},{1,5},{2,6},{3,7},{4,0},{5,1},{6,2},{7,3},{8,28},{9,29},{10,... | collective-permute-start | bytes 3145736 | tf_op jit(solution)/shard_map/ppermute | solution.py:45
  122.9 16.0 %products_1.1 = (f32[16,128,128]{2,1,0:T(8,128)S(1)}, f32[16,128,128]{2,1,0:T(8,128)S(1)}, f32[16,128,128]{2,1,0:T(8,128)S(1)}, f32[16,128,128]{2,1,0:T(8,128)S(1)}) custom-call(s32[2]{0:T(128)S(1)} %pad_add_fusion.where_ref, s32[256]{0:T(256)S(1)} %all-reduce.codes_ref, s32[1024]{0:T(1024)S(1)} %copy-done.8, f32[8,128,128]{2,1,0:T(8,128)S(1)} %copy-done.1, ...), custom_call_target="tpu_custom_call" | custom-call | tf_op jit(solution)/shard_map/products_1/pallas_call | solution.py:200
  138.9 3.5 %collective-permute-start.27 = (f32[16,128,128]{2,1,0:T(8,128)S(1)}, f32[16,128,128]{2,1,0:T(8,128)S(1)}, u32[]{:S(2)}, u32[]{:S(2)}) collective-permute-start(f32[16,128,128]{2,1,0:T(8,128)S(1)} %get-tuple-element.18), channel_id=1, source_target_pairs={{0,1},{1,0},{2,3},{3,2},{4,5},{5,4},{6,7},{7,6},{8,11},{9,10},{10,... | collective-permute-start | bytes 3145736 | tf_op jit(solution)/shard_map/ppermute | solution.py:45
  148.6 3.5 %collective-permute-start.19 = (f32[8,128,128]{2,1,0:T(8,128)S(1)}, f32[8,128,128]{2,1,0:T(8,128)S(1)}, u32[]{:S(2)}, u32[]{:S(2)}) collective-permute-start(f32[8,128,128]{2,1,0:T(8,128)S(1)} %get-tuple-element.30), channel_id=1, source_target_pairs={{0,3},{1,2},{2,1},{3,0},{4,7},{5,6},{6,5},{7,4},{8,9},{9,8},{10,11... | collective-permute-start | bytes 1572872 | tf_op jit(solution)/shard_map/ppermute | solution.py:45
  152.0 6.2 %collective-permute-done.27 = f32[16,128,128]{2,1,0:T(8,128)S(1)} collective-permute-done((f32[16,128,128]{2,1,0:T(8,128)S(1)}, f32[16,128,128]{2,1,0:T(8,128)S(1)}, u32[]{:S(2)}, u32[]{:S(2)}) %collective-permute-start.27) | collective-permute-done | bytes 1048608 | tf_op jit(solution)/shard_map/ppermute | solution.py:45
  160.3 4.4 %collective-permute-done.15 = f32[8,128,128]{2,1,0:T(8,128)S(1)} collective-permute-done((f32[8,128,128]{2,1,0:T(8,128)S(1)}, f32[8,128,128]{2,1,0:T(8,128)S(1)}, u32[]{:S(2)}, u32[]{:S(2)}) %collective-permute-start.15) | collective-permute-done | bytes 524320 | tf_op jit(solution)/shard_map/ppermute | solution.py:45
  164.8 3.5 %collective-permute-start.16 = (f32[4,128,128]{2,1,0:T(8,128)S(1)}, f32[4,128,128]{2,1,0:T(8,128)S(1)}, u32[]{:S(2)}, u32[]{:S(2)}) collective-permute-start(f32[4,128,128]{2,1,0:T(8,128)S(1)} %get-tuple-element.38), channel_id=1, source_target_pairs={{0,3},{1,2},{2,1},{3,0},{4,7},{5,6},{6,5},{7,4},{8,9},{9,8},{10,11... | collective-permute-start | bytes 786440 | tf_op jit(solution)/shard_map/ppermute | solution.py:45
  173.5 3.3 %collective-permute-start.17 = (f32[2,128,128]{2,1,0:T(8,128)S(1)}, f32[2,128,128]{2,1,0:T(8,128)S(1)}, u32[]{:S(2)}, u32[]{:S(2)}) collective-permute-start(f32[2,128,128]{2,1,0:T(8,128)S(1)} %slice_add_fusion.22), channel_id=1, source_target_pairs={{0,20},{1,21},{2,22},{3,23},{4,16},{5,17},{6,18},{7,19},{8,12},{9,... | collective-permute-start | bytes 393224 | tf_op jit(solution)/shard_map/ppermute | solution.py:45
  176.8 3.6 %collective-permute-start.21 = (f32[2,128,128]{2,1,0:T(8,128)S(1)}, f32[2,128,128]{2,1,0:T(8,128)S(1)}, u32[]{:S(2)}, u32[]{:S(2)}) collective-permute-start(f32[2,128,128]{2,1,0:T(8,128)S(1)} %slice_add_fusion.20), channel_id=1, source_target_pairs={{0,1},{1,0},{2,3},{3,2},{4,5},{5,4},{6,7},{7,6},{8,11},{9,10},{10,... | collective-permute-start | bytes 393224 | tf_op jit(solution)/shard_map/ppermute | solution.py:45
  180.5 3.2 %collective-permute-done.21 = f32[2,128,128]{2,1,0:T(8,128)S(1)} collective-permute-done((f32[2,128,128]{2,1,0:T(8,128)S(1)}, f32[2,128,128]{2,1,0:T(8,128)S(1)}, u32[]{:S(2)}, u32[]{:S(2)}) %collective-permute-start.21) | collective-permute-done | bytes 131104 | tf_op jit(solution)/shard_map/ppermute | solution.py:45
  183.7 4.0 %collective-permute-start.29 = (f32[4,128,128]{2,1,0:T(8,128)S(1)}, f32[4,128,128]{2,1,0:T(8,128)S(1)}, u32[]{:S(2)}, u32[]{:S(2)}) collective-permute-start(f32[4,128,128]{2,1,0:T(8,128)S(1)} %get-tuple-element.34), channel_id=1, source_target_pairs={{0,3},{1,2},{2,1},{3,0},{4,7},{5,6},{6,5},{7,4},{8,9},{9,8},{10,11... | collective-permute-start | bytes 786440 | tf_op jit(solution)/shard_map/ppermute | solution.py:45
  191.1 6.7 %collective-permute-start.36 = (f32[4,128,128]{2,1,0:T(8,128)S(1)}, f32[4,128,128]{2,1,0:T(8,128)S(1)}, u32[]{:S(2)}, u32[]{:S(2)}) collective-permute-start(f32[4,128,128]{2,1,0:T(8,128)S(1)} %pad_maximum_fusion.1), channel_id=1, source_target_pairs={{8,0},{9,1},{10,2},{11,3},{12,4},{13,5},{14,6},{15,7},{16,56},{17,... | collective-permute-start | bytes 786440 | tf_op jit(solution)/shard_map/ppermute | solution.py:45
  206.8 5.8 %collective-permute-start.35 = (f32[4,128,128]{2,1,0:T(8,128)S(1)}, f32[4,128,128]{2,1,0:T(8,128)S(1)}, u32[]{:S(2)}, u32[]{:S(2)}) collective-permute-start(f32[4,128,128]{2,1,0:T(8,128)S(1)} %pad_maximum_fusion.2), channel_id=1, source_target_pairs={{8,392},{9,393},{10,394},{11,395},{12,396},{13,397},{14,398},{15,3... | collective-permute-start | bytes 786440 | tf_op jit(solution)/shard_map/ppermute | solution.py:45
  213.9 23.0 %collective-permute-done.35 = f32[4,128,128]{2,1,0:T(8,128)S(1)} collective-permute-done((f32[4,128,128]{2,1,0:T(8,128)S(1)}, f32[4,128,128]{2,1,0:T(8,128)S(1)}, u32[]{:S(2)}, u32[]{:S(2)}) %collective-permute-start.35) | collective-permute-done | bytes 262176 | tf_op jit(solution)/shard_map/ppermute | solution.py:45
  (107 shorter events, 68.2 us)
Async XLA Ops:
  19.1 13.3 %collective-permute-start.1 = (f32[8,128,128]{2,1,0:T(8,128)}, f32[8,128,128]{2,1,0:T(8,128)S(1)}, u32[]{:S(2)}, u32[]{:S(2)}) collective-permute-start(f32[8,128,128]{2,1,0:T(8,128)} %sort_blocks.1.refs_0_), channel_id=1, source_target_pairs={{0,8},{1,9},{2,10},{3,11},{4,12},{5,13},{6,14},{7,15},{8,0},{9,1},... | collective-permute-start | bytes 1572872 | tf_op jit(solution)/shard_map/ppermute | solution.py:45
  21.1 18.4 %collective-permute-start.2 = (f32[8,128,128]{2,1,0:T(8,128)}, f32[8,128,128]{2,1,0:T(8,128)S(1)}, u32[]{:S(2)}, u32[]{:S(2)}) collective-permute-start(f32[8,128,128]{2,1,0:T(8,128)} %sort_blocks.1.refs_0_), channel_id=1, source_target_pairs={{0,480},{1,481},{2,482},{3,483},{4,484},{5,485},{6,486},{7,487},{8... | collective-permute-start | bytes 1572872 | tf_op jit(solution)/shard_map/ppermute | solution.py:45
  39.5 13.3 %collective-permute-start.6 = (f32[8,128,128]{2,1,0:T(8,128)S(1)}, f32[8,128,128]{2,1,0:T(8,128)S(1)}, u32[]{:S(2)}, u32[]{:S(2)}) collective-permute-start(f32[8,128,128]{2,1,0:T(8,128)S(1)} %collective-permute-done.2.refs_2_), channel_id=1, source_target_pairs={{0,480},{1,481},{2,482},{3,483},{4,484},{5,485},{6,486},{7,487},{8... | collective-permute-start | bytes 1572872 | tf_op jit(solution)/shard_map/ppermute | solution.py:45
  50.8 23.3 %collective-permute-start.4 = (f32[8,128,128]{2,1,0:T(8,128)S(1)}, f32[8,128,128]{2,1,0:T(8,128)S(1)}, u32[]{:S(2)}, u32[]{:S(2)}) collective-permute-start(f32[8,128,128]{2,1,0:T(8,128)S(1)} %collective-permute-done.2.refs_2_), channel_id=1, source_target_pairs={{0,8},{1,9},{2,10},{3,11},{4,12},{5,13},{6,14},{7,15},{8,0},{9,1},... | collective-permute-start | bytes 1572872 | tf_op jit(solution)/shard_map/ppermute | solution.py:45
  52.8 23.8 %collective-permute-start.10 = (f32[8,128,128]{2,1,0:T(8,128)S(1)}, f32[8,128,128]{2,1,0:T(8,128)}, u32[]{:S(2)}, u32[]{:S(2)}) collective-permute-start(f32[8,128,128]{2,1,0:T(8,128)S(1)} %collective-permute-done.6.refs_6_), channel_id=1, source_target_pairs={{0,480},{1,481},{2,482},{3,483},{4,484},{5,485},{6,486},{7,487},{8... | collective-permute-start | bytes 1572872 | tf_op jit(solution)/shard_map/ppermute | solution.py:45
  57.3 21.2 %collective-permute-start.11 = (f32[8,128,128]{2,1,0:T(8,128)S(1)}, f32[8,128,128]{2,1,0:T(8,128)}, u32[]{:S(2)}, u32[]{:S(2)}) collective-permute-start(f32[8,128,128]{2,1,0:T(8,128)S(1)} %collective-permute-done.7.refs_7_), channel_id=1, source_target_pairs={{0,480},{1,481},{2,482},{3,483},{4,484},{5,485},{6,486},{7,487},{8... | collective-permute-start | bytes 1572872 | tf_op jit(solution)/shard_map/ppermute | solution.py:45
  74.2 20.2 %collective-permute-start.9 = (f32[8,128,128]{2,1,0:T(8,128)S(1)}, f32[8,128,128]{2,1,0:T(8,128)}, u32[]{:S(2)}, u32[]{:S(2)}) collective-permute-start(f32[8,128,128]{2,1,0:T(8,128)S(1)} %collective-permute-done.7.refs_7_), channel_id=1, source_target_pairs={{0,8},{1,9},{2,10},{3,11},{4,12},{5,13},{6,14},{7,15},{8,0},{9,1},... | collective-permute-start | bytes 1572872 | tf_op jit(solution)/shard_map/ppermute | solution.py:45
  76.6 17.8 %collective-permute-start.12 = (f32[8,128,128]{2,1,0:T(8,128)}, f32[8,128,128]{2,1,0:T(8,128)}, u32[]{:S(2)}, u32[]{:S(2)}) collective-permute-start(f32[8,128,128]{2,1,0:T(8,128)} %collective-permute-done.10.refs_10_), channel_id=1, source_target_pairs={{0,8},{1,9},{2,10},{3,11},{4,12},{5,13},{6,14},{7,15},{8,0},{9,1},... | collective-permute-start | bytes 1572872 | tf_op jit(solution)/shard_map/ppermute | solution.py:45
  78.5 15.9 %collective-permute-start.13 = (f32[8,128,128]{2,1,0:T(8,128)}, f32[8,128,128]{2,1,0:T(8,128)}, u32[]{:S(2)}, u32[]{:S(2)}) collective-permute-start(f32[8,128,128]{2,1,0:T(8,128)} %collective-permute-done.11.refs_11_), channel_id=1, source_target_pairs={{0,8},{1,9},{2,10},{3,11},{4,12},{5,13},{6,14},{7,15},{8,0},{9,1},... | collective-permute-start | bytes 1572872 | tf_op jit(solution)/shard_map/ppermute | solution.py:45
  81.8 33.6 %collective-permute-start.23 = (f32[8,128,128]{2,1,0:T(8,128)}, f32[8,128,128]{2,1,0:T(8,128)}, u32[]{:S(2)}, u32[]{:S(2)}) collective-permute-start(f32[8,128,128]{2,1,0:T(8,128)} %collective-permute-done.10.refs_10_), channel_id=1, source_target_pairs={{0,480},{1,481},{2,482},{3,483},{4,484},{5,485},{6,486},{7,487},{8... | collective-permute-start | bytes 1572872 | tf_op jit(solution)/shard_map/ppermute | solution.py:45
  84.5 32.8 %collective-permute-start.24 = (f32[8,128,128]{2,1,0:T(8,128)}, f32[8,128,128]{2,1,0:T(8,128)}, u32[]{:S(2)}, u32[]{:S(2)}) collective-permute-start(f32[8,128,128]{2,1,0:T(8,128)} %collective-permute-done.11.refs_11_), channel_id=1, source_target_pairs={{0,480},{1,481},{2,482},{3,483},{4,484},{5,485},{6,486},{7,487},{8... | collective-permute-start | bytes 1572872 | tf_op jit(solution)/shard_map/ppermute | solution.py:45
  113.0 32.2 %collective-permute-start.14 = (f32[16,128,128]{2,1,0:T(8,128)S(1)}, f32[16,128,128]{2,1,0:T(8,128)S(1)}, u32[]{:S(2)}, u32[]{:S(2)}) collective-permute-start(f32[16,128,128]{2,1,0:T(8,128)S(1)} %get-tuple-element.14), channel_id=1, source_target_pairs={{0,1},{1,0},{2,3},{3,2},{4,5},{5,4},{6,7},{7,6},{8,11},{9,10},{10,... | collective-permute-start | bytes 3145736 | tf_op jit(solution)/shard_map/ppermute | solution.py:45
  119.7 28.7 %collective-permute-start.18 = (f32[16,128,128]{2,1,0:T(8,128)S(1)}, f32[16,128,128]{2,1,0:T(8,128)S(1)}, u32[]{:S(2)}, u32[]{:S(2)}) collective-permute-start(f32[16,128,128]{2,1,0:T(8,128)S(1)} %get-tuple-element.16), channel_id=1, source_target_pairs={{0,4},{1,5},{2,6},{3,7},{4,0},{5,1},{6,2},{7,3},{8,28},{9,29},{10,... | collective-permute-start | bytes 3145736 | tf_op jit(solution)/shard_map/ppermute | solution.py:45
  138.9 19.3 %collective-permute-start.27 = (f32[16,128,128]{2,1,0:T(8,128)S(1)}, f32[16,128,128]{2,1,0:T(8,128)S(1)}, u32[]{:S(2)}, u32[]{:S(2)}) collective-permute-start(f32[16,128,128]{2,1,0:T(8,128)S(1)} %get-tuple-element.18), channel_id=1, source_target_pairs={{0,1},{1,0},{2,3},{3,2},{4,5},{5,4},{6,7},{7,6},{8,11},{9,10},{10,... | collective-permute-start | bytes 3145736 | tf_op jit(solution)/shard_map/ppermute | solution.py:45
  142.4 28.5 %collective-permute-start.31 = (f32[16,128,128]{2,1,0:T(8,128)S(1)}, f32[16,128,128]{2,1,0:T(8,128)S(1)}, u32[]{:S(2)}, u32[]{:S(2)}) collective-permute-start(f32[16,128,128]{2,1,0:T(8,128)S(1)} %get-tuple-element.20), channel_id=1, source_target_pairs={{0,4},{1,5},{2,6},{3,7},{4,0},{5,1},{6,2},{7,3},{8,28},{9,29},{10,... | collective-permute-start | bytes 3145736 | tf_op jit(solution)/shard_map/ppermute | solution.py:45
  145.3 19.4 %collective-permute-start.15 = (f32[8,128,128]{2,1,0:T(8,128)S(1)}, f32[8,128,128]{2,1,0:T(8,128)S(1)}, u32[]{:S(2)}, u32[]{:S(2)}) collective-permute-start(f32[8,128,128]{2,1,0:T(8,128)S(1)} %get-tuple-element.28), channel_id=1, source_target_pairs={{0,4},{1,5},{2,6},{3,7},{4,0},{5,1},{6,2},{7,3},{8,28},{9,29},{10,... | collective-permute-start | bytes 1572872 | tf_op jit(solution)/shard_map/ppermute | solution.py:45
  148.6 19.7 %collective-permute-start.19 = (f32[8,128,128]{2,1,0:T(8,128)S(1)}, f32[8,128,128]{2,1,0:T(8,128)S(1)}, u32[]{:S(2)}, u32[]{:S(2)}) collective-permute-start(f32[8,128,128]{2,1,0:T(8,128)S(1)} %get-tuple-element.30), channel_id=1, source_target_pairs={{0,3},{1,2},{2,1},{3,0},{4,7},{5,6},{6,5},{7,4},{8,9},{9,8},{10,11... | collective-permute-start | bytes 1572872 | tf_op jit(solution)/shard_map/ppermute | solution.py:45
  158.4 25.3 %collective-permute-start.28 = (f32[8,128,128]{2,1,0:T(8,128)S(1)}, f32[8,128,128]{2,1,0:T(8,128)S(1)}, u32[]{:S(2)}, u32[]{:S(2)}) collective-permute-start(f32[8,128,128]{2,1,0:T(8,128)S(1)} %get-tuple-element.24), channel_id=1, source_target_pairs={{0,4},{1,5},{2,6},{3,7},{4,0},{5,1},{6,2},{7,3},{8,28},{9,29},{10,... | collective-permute-start | bytes 1572872 | tf_op jit(solution)/shard_map/ppermute | solution.py:45
  171.1 16.6 %collective-permute-start.32 = (f32[8,128,128]{2,1,0:T(8,128)S(1)}, f32[8,128,128]{2,1,0:T(8,128)S(1)}, u32[]{:S(2)}, u32[]{:S(2)}) collective-permute-start(f32[8,128,128]{2,1,0:T(8,128)S(1)} %get-tuple-element.26), channel_id=1, source_target_pairs={{0,3},{1,2},{2,1},{3,0},{4,7},{5,6},{6,5},{7,4},{8,9},{9,8},{10,11... | collective-permute-start | bytes 1572872 | tf_op jit(solution)/shard_map/ppermute | solution.py:45
  183.7 14.1 %collective-permute-start.29 = (f32[4,128,128]{2,1,0:T(8,128)S(1)}, f32[4,128,128]{2,1,0:T(8,128)S(1)}, u32[]{:S(2)}, u32[]{:S(2)}) collective-permute-start(f32[4,128,128]{2,1,0:T(8,128)S(1)} %get-tuple-element.34), channel_id=1, source_target_pairs={{0,3},{1,2},{2,1},{3,0},{4,7},{5,6},{6,5},{7,4},{8,9},{9,8},{10,11... | collective-permute-start | bytes 786440 | tf_op jit(solution)/shard_map/ppermute | solution.py:45
  190.4 23.4 %collective-permute-start.22 = (f32[4,128,128]{2,1,0:T(8,128)S(1)}, f32[4,128,128]{2,1,0:T(8,128)S(1)}, u32[]{:S(2)}, u32[]{:S(2)}) collective-permute-start(f32[4,128,128]{2,1,0:T(8,128)S(1)} %pad_maximum_fusion.1), channel_id=1, source_target_pairs={{0,0},{1,1},{2,2},{3,3},{4,4},{5,5},{6,6},{7,7},{24,56},{25,57},{2... | collective-permute-start | bytes 786440 | tf_op jit(solution)/shard_map/ppermute | solution.py:45
  191.1 22.8 %collective-permute-start.36 = (f32[4,128,128]{2,1,0:T(8,128)S(1)}, f32[4,128,128]{2,1,0:T(8,128)S(1)}, u32[]{:S(2)}, u32[]{:S(2)}) collective-permute-start(f32[4,128,128]{2,1,0:T(8,128)S(1)} %pad_maximum_fusion.1), channel_id=1, source_target_pairs={{8,0},{9,1},{10,2},{11,3},{12,4},{13,5},{14,6},{15,7},{16,56},{17,... | collective-permute-start | bytes 786440 | tf_op jit(solution)/shard_map/ppermute | solution.py:45
  206.8 30.0 %collective-permute-start.35 = (f32[4,128,128]{2,1,0:T(8,128)S(1)}, f32[4,128,128]{2,1,0:T(8,128)S(1)}, u32[]{:S(2)}, u32[]{:S(2)}) collective-permute-start(f32[4,128,128]{2,1,0:T(8,128)S(1)} %pad_maximum_fusion.2), channel_id=1, source_target_pairs={{8,392},{9,393},{10,394},{11,395},{12,396},{13,397},{14,398},{15,3... | collective-permute-start | bytes 786440 | tf_op jit(solution)/shard_map/ppermute | solution.py:45
  212.5 26.2 %collective-permute-start.37 = (f32[4,128,128]{2,1,0:T(8,128)S(1)}, f32[4,128,128]{2,1,0:T(8,128)S(1)}, u32[]{:S(2)}, u32[]{:S(2)}) collective-permute-start(f32[4,128,128]{2,1,0:T(8,128)S(1)} %pad_maximum_fusion.2), channel_id=1, source_target_pairs={{0,392},{1,393},{2,394},{3,395},{4,396},{5,397},{6,398},{7,399},{2... | collective-permute-start | bytes 786440 | tf_op jit(solution)/shard_map/ppermute | solution.py:45
  (24 other events, 215.2 us)

commit v2 on v1

--- a/solution.py
+++ b/solution.py
@@ -96,23 +96,18 @@
     return table.reshape(-1)
 
 
-def sort_kernel(ids_ref, blocks_ref, out_ref, sems):
+def sort_kernel(ids_ref, blocks_ref, out_ref):
     count = blocks_ref.shape[0]
     keys = []
     for s in range(count):
-        row = ids_ref[2 * s]
-        keys.append(jnp.where(row >= 0, row * NB + ids_ref[2 * s + 1], 2**30 + s))
-    copies = []
+        row = ids_ref[0, s]
+        keys.append(jnp.where(row >= 0, row * NB + ids_ref[1, s], 2**30 + s))
     for s in range(count):
         rank = jnp.int32(0)
         for o in range(count):
             if o != s:
                 rank = rank + jnp.where(keys[o] < keys[s], 1, 0)
-        copies.append(pltpu.make_async_copy(blocks_ref.at[s], out_ref.at[rank], sems.at[s]))
-    for copy in copies:
-        copy.start()
-    for copy in copies:
-        copy.wait()
+        out_ref[rank] = blocks_ref[s]
 
 
 def sort_blocks(block_ids, blocks):
@@ -121,19 +116,20 @@
         out_shape=jax.ShapeDtypeStruct(blocks.shape, blocks.dtype),
         in_specs=[
             pl.BlockSpec(memory_space=pltpu.SMEM),
-            pl.BlockSpec(memory_space=pl.ANY),
+            pl.BlockSpec(memory_space=pltpu.VMEM),
         ],
-        out_specs=pl.BlockSpec(memory_space=pl.ANY),
-        scratch_shapes=[pltpu.SemaphoreType.DMA((blocks.shape[0],))],
+        out_specs=pl.BlockSpec(memory_space=pltpu.VMEM),
         name="sort_blocks",
-    )(block_ids.reshape(-1), blocks)
+    )(block_ids.T, blocks)
 
 
 def chunk_kernel(chunk, reach, where_ref, codes_ref, table_ref, *refs):
     panels = refs[: 2 + 4 * reach]
-    keep0, send0, keep1, send1, hi_ref, lo_ref = refs[2 + 4 * reach :]
+    outs = refs[2 + 4 * reach : -2]
+    hi_ref, lo_ref = refs[-2:]
     core = where_ref[0]
     place = where_ref[1]
+    xhi = place // 8
 
     def put(panel, row, quarter):
         for rho in range(4):
@@ -156,6 +152,7 @@
         put(their_b, -ahead, core)
 
     lists = ((0, 3), (1, 2))[chunk]
+    held = [(c % 2 ^ core) + 2 * (c // 2 ^ xhi) for c in lists]
 
     def product(left, right):
         total = None
@@ -171,37 +168,46 @@
                 total = term if total is None else total + term
         return total
 
-    for half, (kept, sent) in enumerate(((keep0, send0), (keep1, send1))):
-        for side, out in enumerate((kept, sent)):
-
-            def body(index, carry, half=half, side=side, out=out):
-                spot = index // 2
-                dest = table_ref[(core * 16 + place) * 32 + half * 16 + side * 8 + spot]
-                far = dest // 8
-                layer = dest % 8
-                slot = layer * 8 + core * 4 + half * 2 + index % 2
-                code = codes_ref[jnp.where(far == 0, lists[0], lists[1]) * 64 + slot]
-                good = code >= 0
-                code = jnp.maximum(code, 0)
-                left_row = jnp.where(far == 0, LEFT[lists[0]], LEFT[lists[1]])
-                right_row = jnp.where(far == 0, RIGHT[lists[0]], RIGHT[lists[1]])
-                left = (left_row + 4) * 4 + code // 16
-                right = (right_row + 4) * 4 + code % 16
-                out[index] = jnp.where(good, product(left, right), jnp.float32(0.0))
+    def fill(out, index, dest, inner):
+        far = dest // 8
+        slot = dest % 8 * 8 + core * 4 + inner
+        code = codes_ref[jnp.where(far == 0, held[0], held[1]), slot]
+        good = code >= 0
+        code = jnp.maximum(code, 0)
+        left_row = jnp.where(far == 0, LEFT[lists[0]], LEFT[lists[1]])
+        right_row = jnp.where(far == 0, RIGHT[lists[0]], RIGHT[lists[1]])
+        left = (left_row + 4) * 4 + code // 16
+        right = (right_row + 4) * 4 + code % 16
+        out[index] = jnp.where(good, product(left, right), jnp.float32(0.0))
+
+    if chunk == 0:
+
+        def body(index, carry):
+            fill(outs[0], index, index // 4, index % 4)
+            return carry
+
+        lax.fori_loop(0, 64, body, 0, unroll=2)
+        return
+    for half in range(2):
+        for side in range(2):
+
+            def body(index, carry, half=half, side=side):
+                at = (core * 16 + place) * 32 + half * 16 + side * 8 + index // 2
+                fill(outs[half * 2 + side], index, table_ref[at], half * 2 + index % 2)
                 return carry
 
             lax.fori_loop(0, 16, body, 0, unroll=2)
 
 
 def chunk_products(chunk, reach, where, codes, table, panels):
-    piece = jax.ShapeDtypeStruct((16, 128, 128), jnp.float32)
+    sizes = ((64,), (16,) * 4)[chunk]
     vmem = pl.BlockSpec(memory_space=pltpu.VMEM)
     smem = pl.BlockSpec(memory_space=pltpu.SMEM)
     return pl.pallas_call(
         functools.partial(chunk_kernel, chunk, reach),
-        out_shape=[piece] * 4,
+        out_shape=[jax.ShapeDtypeStruct((n, 128, 128), jnp.float32) for n in sizes],
         in_specs=[smem] * 3 + [vmem] * len(panels),
-        out_specs=[vmem] * 4,
+        out_specs=[vmem] * len(sizes),
         scratch_shapes=[
             pltpu.VMEM((72, 128, 256), jnp.bfloat16),
             pltpu.VMEM((72, 128, 256), jnp.bfloat16),
@@ -237,9 +243,16 @@
         keeps = [keeps[h][:mid] + received[h][:mid] for h in range(2)]
 
 
-def bring_home(chunk, halves):
-    part = jnp.concatenate(halves, axis=0)
+def bring_home(chunk, part):
     return send(part, home(chunk, True)), send(part, home(chunk, False))
+
+
+def to_place(z, xhi, core, xlo, y):
+    return z - LEFT[xhi * 2 + core], xhi, core, xlo, y
+
+
+def other_xhi(z, xhi, core, xlo, y):
+    return z, 1 - xhi, core, xlo, y
 
 
 def shards(blocks, block_ids, out_ids):
@@ -259,12 +272,9 @@
         their_a.append(send(mine_a[k], other_core))
         their_b.append(send(mine_b[k], other_core))
 
-    codes = slot_codes(out_ids, z, xhi * 2 + core)
-
-    def to_place(z, xhi, core, xlo, y):
-        return z - LEFT[xhi * 2 + core], xhi, core, xlo, y
-
-    codes = lax.all_gather(send(codes, to_place), ("xhi", "core"), axis=0, tiled=True)
+    codes = send(slot_codes(out_ids, z, xhi * 2 + core)[None], to_place)
+    codes = jnp.concatenate([codes, send(codes, other_core)], axis=0)
+    codes = jnp.concatenate([codes, send(codes, other_xhi)], axis=0)
 
     def panels(reach):
         out = [mine_a[0], mine_b[0]]
@@ -272,16 +282,18 @@
             out += [mine_a[k], mine_b[k], their_a[k], their_b[k]]
         return out
 
-    results = []
-    for chunk, reach in ((0, 3), (1, 4)):
-        keep0, send0, keep1, send1 = chunk_products(chunk, reach, where, codes, table, panels(reach))
-        results.append(bring_home(chunk, halve([keep0, keep1], [send0, send1])))
-    same = jnp.where(core == xhi, results[0][0], results[1][0])
-    cross = jnp.where(core == xhi, results[0][1], results[1][1])
+    early, mine_a[4], mine_b[4] = lax.optimization_barrier((codes, mine_a[4], mine_b[4]))
+    [partial] = chunk_products(0, 3, where, early, table, panels(3))
+    near = lax.psum_scatter(partial, ("xhi", "xlo", "y"), scatter_dimension=0, tiled=True)
+    keep0, send0, keep1, send1 = chunk_products(1, 4, where, codes, table, panels(4))
+    wide = jnp.concatenate(halve([keep0, keep1], [send0, send1]), axis=0)
+
+    same, cross = [
+        jnp.where(core == xhi, a, b) for a, b in zip(bring_home(0, near), bring_home(1, wide))
+    ]
     first = jnp.where(core == 0, same, cross)
     second = jnp.where(core == 0, cross, same)
-    layers = jnp.concatenate([first, second], axis=0)
-    return layers
+    return jnp.concatenate([first, second], axis=0)
 
 
 def solution(mesh):

time: 241 us -> 241 us (level)
  the two profiles are of different devices: /device:TPU:12 before, /device:TPU:7 now
where the time goes in v2:
time: 241 us; the launch traced here: 239 us
  starting transfers between devices  101 us (42%)
  waiting for transfers between devices  80 us (33%)
  Pallas kernels  33.8 us (14%)
  between operations  13.9 us (6%)
  local copies, waits for them, and re-layouts  5.54 us (2%)
  other arithmetic  4.61 us (2%)
    ppermute x32, starting transfers between devices, send(): return lax.ppermute(value, AXES, pairs)  101 us
    ppermute x32, waiting for transfers between devices, send(): return lax.ppermute(value, AXES, pairs)  80 us
    pallas_call x2, Pallas kernels, chunk_products(): pl.pallas_call(functools.partial(chunk_kernel, chunk, reach), out_shape=[...  31.9 us
    unnamed x14, local copies, waits for them, and re-layouts  5.54 us
  transfers between devices with their start and end apart: 33, of which 18 were waited for; matrix products, arithmetic and copies ran while one was open for 2% of the time, Pallas kernels for 7%

profile of v2, /device:TPU:7, one launch (start us, length us, event | category | flops | bytes accessed | tf_op | source)
XLA Modules:
  0.0 239.4 jit_solution(17541856781628172605)
XLA Ops:
  8.5 2.6 %collective-permute-start.7 = (f32[8,128,128]{2,1,0:T(8,128)}, f32[8,128,128]{2,1,0:T(8,128)S(1)}, u32[]{:S(2)}, u32[]{:S(2)}) collective-permute-start(f32[8,128,128]{2,1,0:T(8,128)} %sort_blocks.1.refs_0_), channel_id=1, source_target_pairs={{0,8},{1,9},{2,10},{3,11},{4,12},{5,13},{6,14},{7,15},{8,0},{9,1},... | collective-permute-start | bytes 1572872 | tf_op jit(solution)/shard_map/ppermute | solution.py:45
  11.0 3.5 %collective-permute-start.3 = (f32[8,128,128]{2,1,0:T(8,128)}, f32[8,128,128]{2,1,0:T(8,128)S(1)}, u32[]{:S(2)}, u32[]{:S(2)}) collective-permute-start(f32[8,128,128]{2,1,0:T(8,128)} %sort_blocks.1.refs_0_), channel_id=1, source_target_pairs={{0,480},{1,481},{2,482},{3,483},{4,484},{5,485},{6,486},{7,487},{8... | collective-permute-start | bytes 1572872 | tf_op jit(solution)/shard_map/ppermute | solution.py:45
  14.6 3.5 %collective-permute-start.8 = (f32[8,128,128]{2,1,0:T(8,128)S(1)}, f32[8,128,128]{2,1,0:T(8,128)S(1)}, u32[]{:S(2)}, u32[]{:S(2)}) collective-permute-start(f32[8,128,128]{2,1,0:T(8,128)S(1)} %collective-permute-done.7.refs_1_), channel_id=1, source_target_pairs={{0,480},{1,481},{2,482},{3,483},{4,484},{5,485},{6,486},{7,487},{8... | collective-permute-start | bytes 1572872 | tf_op jit(solution)/shard_map/ppermute | solution.py:45
  18.2 10.8 %collective-permute-done.3.refs_2_ = f32[8,128,128]{2,1,0:T(8,128)S(1)} collective-permute-done((f32[8,128,128]{2,1,0:T(8,128)}, f32[8,128,128]{2,1,0:T(8,128)S(1)}, u32[]{:S(2)}, u32[]{:S(2)}) %collective-permute-start.3) | collective-permute-done | bytes 524320 | tf_op jit(solution)/shard_map/ppermute | solution.py:45
  30.9 3.7 %collective-permute-done.8.refs_3_ = f32[8,128,128]{2,1,0:T(8,128)S(1)} collective-permute-done((f32[8,128,128]{2,1,0:T(8,128)S(1)}, f32[8,128,128]{2,1,0:T(8,128)S(1)}, u32[]{:S(2)}, u32[]{:S(2)}) %collective-permute-start.8) | collective-permute-done | bytes 524320 | tf_op jit(solution)/shard_map/ppermute | solution.py:45
  36.5 3.7 %collective-permute-done.4.refs_6_ = f32[8,128,128]{2,1,0:T(8,128)S(1)} collective-permute-done((f32[8,128,128]{2,1,0:T(8,128)S(1)}, f32[8,128,128]{2,1,0:T(8,128)S(1)}, u32[]{:S(2)}, u32[]{:S(2)}) %collective-permute-start.4) | collective-permute-done | bytes 524320 | tf_op jit(solution)/shard_map/ppermute | solution.py:45
  42.1 3.7 %collective-permute-done.9.refs_7_ = f32[8,128,128]{2,1,0:T(8,128)S(1)} collective-permute-done((f32[8,128,128]{2,1,0:T(8,128)S(1)}, f32[8,128,128]{2,1,0:T(8,128)S(1)}, u32[]{:S(2)}, u32[]{:S(2)}) %collective-permute-start.9) | collective-permute-done | bytes 524320 | tf_op jit(solution)/shard_map/ppermute | solution.py:45
  49.2 7.0 %collective-permute-start.12 = (f32[8,128,128]{2,1,0:T(8,128)S(1)}, f32[8,128,128]{2,1,0:T(8,128)}, u32[]{:S(2)}, u32[]{:S(2)}) collective-permute-start(f32[8,128,128]{2,1,0:T(8,128)S(1)} %collective-permute-done.3.refs_2_), channel_id=1, source_target_pairs={{0,8},{1,9},{2,10},{3,11},{4,12},{5,13},{6,14},{7,15},{8,0},{9,1},... | collective-permute-start | bytes 1572872 | tf_op jit(solution)/shard_map/ppermute | solution.py:45
  61.8 4.6 %collective-permute-start = (s32[1,64]{1,0:T(1,128)S(1)}, s32[1,64]{1,0:T(1,128)S(1)}, u32[]{:S(2)}, u32[]{:S(2)}) collective-permute-start(s32[1,64]{1,0:T(1,128)S(1)} %fusion.2), channel_id=1, source_target_pairs={{0,0},{1,1},{2,2},{3,3},{4,4},{5,5},{6,6},{7,7},{8,136},{9,137},{1... | collective-permute-start | bytes 776 | tf_op jit(solution)/shard_map/ppermute | solution.py:45
  67.1 11.0 %collective-permute-start.1 = (s32[1,64]{1,0:T(1,128)S(1)}, s32[1,64]{1,0:T(1,128)S(1)}, u32[]{:S(2)}, u32[]{:S(2)}) collective-permute-start(s32[1,64]{1,0:T(1,128)S(1)} %collective-permute-done), channel_id=1, source_target_pairs={{0,8},{1,9},{2,10},{3,11},{4,12},{5,13},{6,14},{7,15},{8,0},{9,1},... | collective-permute-start | bytes 776 | tf_op jit(solution)/shard_map/ppermute | solution.py:45
  84.7 3.4 %collective-permute-start.13 = (f32[8,128,128]{2,1,0:T(8,128)S(1)}, f32[8,128,128]{2,1,0:T(8,128)}, u32[]{:S(2)}, u32[]{:S(2)}) collective-permute-start(f32[8,128,128]{2,1,0:T(8,128)S(1)} %collective-permute-done.8.refs_3_), channel_id=1, source_target_pairs={{0,8},{1,9},{2,10},{3,11},{4,12},{5,13},{6,14},{7,15},{8,0},{9,1},... | collective-permute-start | bytes 1572872 | tf_op jit(solution)/shard_map/ppermute | solution.py:45
  98.4 15.7 %products_0.1 = f32[64,128,128]{2,1,0:T(8,128)S(1)} custom-call(s32[2]{0:T(128)S(1)} %pad_add_fusion.2.where_ref, s32[4,64]{1,0:T(4,128)S(1)} %pad_add_fusion.codes_ref, s32[1024]{0:T(1024)S(1)} %copy-done.5, f32[8,128,128]{2,1,0:T(8,128)S(1)} %copy-done.1, f32[8,128,128]{2,1,0:T(8,128)S(1)} %collective-permute-done.7.refs_1_, ...), custom_call_target="tpu_custom_call" | custom-call | tf_op jit(solution)/shard_map/products_0/pallas_call | solution.py:206
  124.1 16.2 %products_1.1 = (f32[16,128,128]{2,1,0:T(8,128)S(1)}, f32[16,128,128]{2,1,0:T(8,128)S(1)}, f32[16,128,128]{2,1,0:T(8,128)S(1)}, f32[16,128,128]{2,1,0:T(8,128)S(1)}) custom-call(s32[2]{0:T(128)S(1)} %pad_add_fusion.2.where_ref, s32[4,64]{1,0:T(4,128)S(1)} %pad_add_fusion.codes_ref, s32[1024]{0:T(1024)S(1)} %copy-done.6, f32[8,128,128]{2,1,0:T(8,128)S(1)} %copy-done.2, ...), custom_call_target="tpu_custom_call" | custom-call | tf_op jit(solution)/shard_map/products_1/pallas_call | solution.py:206
  140.3 4.6 %collective-permute-start.21 = (f32[16,128,128]{2,1,0:T(8,128)S(1)}, f32[16,128,128]{2,1,0:T(8,128)S(1)}, u32[]{:S(2)}, u32[]{:S(2)}) collective-permute-start(f32[16,128,128]{2,1,0:T(8,128)S(1)} %get-tuple-element.16), channel_id=1, source_target_pairs={{0,1},{1,0},{2,3},{3,2},{4,5},{5,4},{6,7},{7,6},{8,11},{9,10},{10,... | collective-permute-start | bytes 3145736 | tf_op jit(solution)/shard_map/ppermute | solution.py:45
  147.4 16.5 %collective-permute-done.21 = f32[16,128,128]{2,1,0:T(8,128)S(1)} collective-permute-done((f32[16,128,128]{2,1,0:T(8,128)S(1)}, f32[16,128,128]{2,1,0:T(8,128)S(1)}, u32[]{:S(2)}, u32[]{:S(2)}) %collective-permute-start.21) | collective-permute-done | bytes 1048608 | tf_op jit(solution)/shard_map/ppermute | solution.py:45
  164.0 3.1 %collective-permute-start.22 = (f32[8,128,128]{2,1,0:T(8,128)S(1)}, f32[8,128,128]{2,1,0:T(8,128)S(1)}, u32[]{:S(2)}, u32[]{:S(2)}) collective-permute-start(f32[8,128,128]{2,1,0:T(8,128)S(1)} %get-tuple-element.22), channel_id=1, source_target_pairs={{0,4},{1,5},{2,6},{3,7},{4,0},{5,1},{6,2},{7,3},{8,28},{9,29},{10,... | collective-permute-start | bytes 1572872 | tf_op jit(solution)/shard_map/ppermute | solution.py:45
  167.2 2.5 %collective-permute-done.25 = f32[16,128,128]{2,1,0:T(8,128)S(1)} collective-permute-done((f32[16,128,128]{2,1,0:T(8,128)S(1)}, f32[16,128,128]{2,1,0:T(8,128)S(1)}, u32[]{:S(2)}, u32[]{:S(2)}) %collective-permute-start.25) | collective-permute-done | bytes 1048608 | tf_op jit(solution)/shard_map/ppermute | solution.py:45
  171.7 5.1 %collective-permute-done.22 = f32[8,128,128]{2,1,0:T(8,128)S(1)} collective-permute-done((f32[8,128,128]{2,1,0:T(8,128)S(1)}, f32[8,128,128]{2,1,0:T(8,128)S(1)}, u32[]{:S(2)}, u32[]{:S(2)}) %collective-permute-start.22) | collective-permute-done | bytes 524320 | tf_op jit(solution)/shard_map/ppermute | solution.py:45
  176.8 2.8 %collective-permute-start.23 = (f32[4,128,128]{2,1,0:T(8,128)S(1)}, f32[4,128,128]{2,1,0:T(8,128)S(1)}, u32[]{:S(2)}, u32[]{:S(2)}) collective-permute-start(f32[4,128,128]{2,1,0:T(8,128)S(1)} %get-tuple-element.28), channel_id=1, source_target_pairs={{0,3},{1,2},{2,1},{3,0},{4,7},{5,6},{6,5},{7,4},{8,9},{9,8},{10,11... | collective-permute-start | bytes 786440 | tf_op jit(solution)/shard_map/ppermute | solution.py:45
  187.5 3.5 %collective-permute-start.28 = (f32[2,128,128]{2,1,0:T(8,128)S(1)}, f32[2,128,128]{2,1,0:T(8,128)S(1)}, u32[]{:S(2)}, u32[]{:S(2)}) collective-permute-start(f32[2,128,128]{2,1,0:T(8,128)S(1)} %slice_add_fusion.8), channel_id=1, source_target_pairs={{0,1},{1,0},{2,3},{3,2},{4,5},{5,4},{6,7},{7,6},{8,11},{9,10},{10,... | collective-permute-start | bytes 393224 | tf_op jit(solution)/shard_map/ppermute | solution.py:45
  191.0 3.4 %collective-permute-done.28 = f32[2,128,128]{2,1,0:T(8,128)S(1)} collective-permute-done((f32[2,128,128]{2,1,0:T(8,128)S(1)}, f32[2,128,128]{2,1,0:T(8,128)S(1)}, u32[]{:S(2)}, u32[]{:S(2)}) %collective-permute-start.28) | collective-permute-done | bytes 131104 | tf_op jit(solution)/shard_map/ppermute | solution.py:45
  195.2 13.4 %collective-permute-start.31 = (f32[4,128,128]{2,1,0:T(8,128)S(1)}, f32[4,128,128]{2,1,0:T(8,128)S(1)}, u32[]{:S(2)}, u32[]{:S(2)}) collective-permute-start(f32[4,128,128]{2,1,0:T(8,128)S(1)} %pad_maximum_fusion.1), channel_id=1, source_target_pairs={{0,392},{1,393},{2,394},{3,395},{4,396},{5,397},{6,398},{7,399},{2... | collective-permute-start | bytes 786440 | tf_op jit(solution)/shard_map/ppermute | solution.py:45
  211.9 13.6 %collective-permute-done.31 = f32[4,128,128]{2,1,0:T(8,128)S(1)} collective-permute-done((f32[4,128,128]{2,1,0:T(8,128)S(1)}, f32[4,128,128]{2,1,0:T(8,128)S(1)}, u32[]{:S(2)}, u32[]{:S(2)}) %collective-permute-start.31) | collective-permute-done | bytes 262176 | tf_op jit(solution)/shard_map/ppermute | solution.py:45
  225.5 6.1 %collective-permute-done.18 = f32[4,128,128]{2,1,0:T(8,128)S(1)} collective-permute-done((f32[4,128,128]{2,1,0:T(8,128)}, f32[4,128,128]{2,1,0:T(8,128)S(1)}, u32[]{:S(2)}, u32[]{:S(2)}) %collective-permute-start.18) | collective-permute-done | bytes 262176 | tf_op jit(solution)/shard_map/ppermute | solution.py:45
  (79 shorter events, 61.4 us)
Async XLA Ops:
  6.5 202.1 %reduce-scatter.2.cloned.1.call-start = ((), (), s32[]{:S(2)}) async-start(), calls=%async_computation.1 | async-start | bytes 4456448 | tf_op jit(solution)/shard_map/reduce_scatter | solution.py:287
  11.0 17.9 %collective-permute-start.3 = (f32[8,128,128]{2,1,0:T(8,128)}, f32[8,128,128]{2,1,0:T(8,128)S(1)}, u32[]{:S(2)}, u32[]{:S(2)}) collective-permute-start(f32[8,128,128]{2,1,0:T(8,128)} %sort_blocks.1.refs_0_), channel_id=1, source_target_pairs={{0,480},{1,481},{2,482},{3,483},{4,484},{5,485},{6,486},{7,487},{8... | collective-permute-start | bytes 1572872 | tf_op jit(solution)/shard_map/ppermute | solution.py:45
  14.6 19.9 %collective-permute-start.8 = (f32[8,128,128]{2,1,0:T(8,128)S(1)}, f32[8,128,128]{2,1,0:T(8,128)S(1)}, u32[]{:S(2)}, u32[]{:S(2)}) collective-permute-start(f32[8,128,128]{2,1,0:T(8,128)S(1)} %collective-permute-done.7.refs_1_), channel_id=1, source_target_pairs={{0,480},{1,481},{2,482},{3,483},{4,484},{5,485},{6,486},{7,487},{8... | collective-permute-start | bytes 1572872 | tf_op jit(solution)/shard_map/ppermute | solution.py:45
  28.9 11.2 %collective-permute-start.4 = (f32[8,128,128]{2,1,0:T(8,128)S(1)}, f32[8,128,128]{2,1,0:T(8,128)S(1)}, u32[]{:S(2)}, u32[]{:S(2)}) collective-permute-start(f32[8,128,128]{2,1,0:T(8,128)S(1)} %collective-permute-done.3.refs_2_), channel_id=1, source_target_pairs={{0,480},{1,481},{2,482},{3,483},{4,484},{5,485},{6,486},{7,487},{8... | collective-permute-start | bytes 1572872 | tf_op jit(solution)/shard_map/ppermute | solution.py:45
  34.6 11.2 %collective-permute-start.9 = (f32[8,128,128]{2,1,0:T(8,128)S(1)}, f32[8,128,128]{2,1,0:T(8,128)S(1)}, u32[]{:S(2)}, u32[]{:S(2)}) collective-permute-start(f32[8,128,128]{2,1,0:T(8,128)S(1)} %collective-permute-done.8.refs_3_), channel_id=1, source_target_pairs={{0,480},{1,481},{2,482},{3,483},{4,484},{5,485},{6,486},{7,487},{8... | collective-permute-start | bytes 1572872 | tf_op jit(solution)/shard_map/ppermute | solution.py:45
  40.2 16.1 %collective-permute-start.5 = (f32[8,128,128]{2,1,0:T(8,128)S(1)}, f32[8,128,128]{2,1,0:T(8,128)S(1)}, u32[]{:S(2)}, u32[]{:S(2)}) collective-permute-start(f32[8,128,128]{2,1,0:T(8,128)S(1)} %collective-permute-done.4.refs_6_), channel_id=1, source_target_pairs={{0,480},{1,481},{2,482},{3,483},{4,484},{5,485},{6,486},{7,487},{8... | collective-permute-start | bytes 1572872 | tf_op jit(solution)/shard_map/ppermute | solution.py:45
  45.8 12.4 %collective-permute-start.10 = (f32[8,128,128]{2,1,0:T(8,128)S(1)}, f32[8,128,128]{2,1,0:T(8,128)}, u32[]{:S(2)}, u32[]{:S(2)}) collective-permute-start(f32[8,128,128]{2,1,0:T(8,128)S(1)} %collective-permute-done.9.refs_7_), channel_id=1, source_target_pairs={{0,480},{1,481},{2,482},{3,483},{4,484},{5,485},{6,486},{7,487},{8... | collective-permute-start | bytes 1572872 | tf_op jit(solution)/shard_map/ppermute | solution.py:45
  49.2 38.9 %collective-permute-start.12 = (f32[8,128,128]{2,1,0:T(8,128)S(1)}, f32[8,128,128]{2,1,0:T(8,128)}, u32[]{:S(2)}, u32[]{:S(2)}) collective-permute-start(f32[8,128,128]{2,1,0:T(8,128)S(1)} %collective-permute-done.3.refs_2_), channel_id=1, source_target_pairs={{0,8},{1,9},{2,10},{3,11},{4,12},{5,13},{6,14},{7,15},{8,0},{9,1},... | collective-permute-start | bytes 1572872 | tf_op jit(solution)/shard_map/ppermute | solution.py:45
  56.3 33.8 %collective-permute-start.6 = (f32[8,128,128]{2,1,0:T(8,128)S(1)}, f32[8,128,128]{2,1,0:T(8,128)}, u32[]{:S(2)}, u32[]{:S(2)}) collective-permute-start(f32[8,128,128]{2,1,0:T(8,128)S(1)} %collective-permute-done.5.refs_10_), channel_id=1, source_target_pairs={{0,480},{1,481},{2,482},{3,483},{4,484},{5,485},{6,486},{7,487},{8... | collective-permute-start | bytes 1572872 | tf_op jit(solution)/shard_map/ppermute | solution.py:45
  58.2 34.3 %collective-permute-start.11 = (f32[8,128,128]{2,1,0:T(8,128)}, f32[8,128,128]{2,1,0:T(8,128)}, u32[]{:S(2)}, u32[]{:S(2)}) collective-permute-start(f32[8,128,128]{2,1,0:T(8,128)} %collective-permute-done.10.refs_11_), channel_id=1, source_target_pairs={{0,480},{1,481},{2,482},{3,483},{4,484},{5,485},{6,486},{7,487},{8... | collective-permute-start | bytes 1572872 | tf_op jit(solution)/shard_map/ppermute | solution.py:45
  67.1 11.8 %collective-permute-start.1 = (s32[1,64]{1,0:T(1,128)S(1)}, s32[1,64]{1,0:T(1,128)S(1)}, u32[]{:S(2)}, u32[]{:S(2)}) collective-permute-start(s32[1,64]{1,0:T(1,128)S(1)} %collective-permute-done), channel_id=1, source_target_pairs={{0,8},{1,9},{2,10},{3,11},{4,12},{5,13},{6,14},{7,15},{8,0},{9,1},... | collective-permute-start | bytes 776 | tf_op jit(solution)/shard_map/ppermute | solution.py:45
  80.9 13.7 %collective-permute-start.14 = (f32[8,128,128]{2,1,0:T(8,128)S(1)}, f32[8,128,128]{2,1,0:T(8,128)}, u32[]{:S(2)}, u32[]{:S(2)}) collective-permute-start(f32[8,128,128]{2,1,0:T(8,128)S(1)} %collective-permute-done.4.refs_6_), channel_id=1, source_target_pairs={{0,8},{1,9},{2,10},{3,11},{4,12},{5,13},{6,14},{7,15},{8,0},{9,1},... | collective-permute-start | bytes 1572872 | tf_op jit(solution)/shard_map/ppermute | solution.py:45
  84.7 9.8 %collective-permute-start.13 = (f32[8,128,128]{2,1,0:T(8,128)S(1)}, f32[8,128,128]{2,1,0:T(8,128)}, u32[]{:S(2)}, u32[]{:S(2)}) collective-permute-start(f32[8,128,128]{2,1,0:T(8,128)S(1)} %collective-permute-done.8.refs_3_), channel_id=1, source_target_pairs={{0,8},{1,9},{2,10},{3,11},{4,12},{5,13},{6,14},{7,15},{8,0},{9,1},... | collective-permute-start | bytes 1572872 | tf_op jit(solution)/shard_map/ppermute | solution.py:45
  140.3 23.6 %collective-permute-start.21 = (f32[16,128,128]{2,1,0:T(8,128)S(1)}, f32[16,128,128]{2,1,0:T(8,128)S(1)}, u32[]{:S(2)}, u32[]{:S(2)}) collective-permute-start(f32[16,128,128]{2,1,0:T(8,128)S(1)} %get-tuple-element.16), channel_id=1, source_target_pairs={{0,1},{1,0},{2,3},{3,2},{4,5},{5,4},{6,7},{7,6},{8,11},{9,10},{10,... | collective-permute-start | bytes 3145736 | tf_op jit(solution)/shard_map/ppermute | solution.py:45
  145.0 24.6 %collective-permute-start.25 = (f32[16,128,128]{2,1,0:T(8,128)S(1)}, f32[16,128,128]{2,1,0:T(8,128)S(1)}, u32[]{:S(2)}, u32[]{:S(2)}) collective-permute-start(f32[16,128,128]{2,1,0:T(8,128)S(1)} %get-tuple-element.18), channel_id=1, source_target_pairs={{0,4},{1,5},{2,6},{3,7},{4,0},{5,1},{6,2},{7,3},{8,28},{9,29},{10,... | collective-permute-start | bytes 3145736 | tf_op jit(solution)/shard_map/ppermute | solution.py:45
  164.0 12.8 %collective-permute-start.22 = (f32[8,128,128]{2,1,0:T(8,128)S(1)}, f32[8,128,128]{2,1,0:T(8,128)S(1)}, u32[]{:S(2)}, u32[]{:S(2)}) collective-permute-start(f32[8,128,128]{2,1,0:T(8,128)S(1)} %get-tuple-element.22), channel_id=1, source_target_pairs={{0,4},{1,5},{2,6},{3,7},{4,0},{5,1},{6,2},{7,3},{8,28},{9,29},{10,... | collective-permute-start | bytes 1572872 | tf_op jit(solution)/shard_map/ppermute | solution.py:45
  169.7 10.6 %collective-permute-start.26 = (f32[8,128,128]{2,1,0:T(8,128)S(1)}, f32[8,128,128]{2,1,0:T(8,128)S(1)}, u32[]{:S(2)}, u32[]{:S(2)}) collective-permute-start(f32[8,128,128]{2,1,0:T(8,128)S(1)} %get-tuple-element.24), channel_id=1, source_target_pairs={{0,3},{1,2},{2,1},{3,0},{4,7},{5,6},{6,5},{7,4},{8,9},{9,8},{10,11... | collective-permute-start | bytes 1572872 | tf_op jit(solution)/shard_map/ppermute | solution.py:45
  176.8 7.4 %collective-permute-start.23 = (f32[4,128,128]{2,1,0:T(8,128)S(1)}, f32[4,128,128]{2,1,0:T(8,128)S(1)}, u32[]{:S(2)}, u32[]{:S(2)}) collective-permute-start(f32[4,128,128]{2,1,0:T(8,128)S(1)} %get-tuple-element.28), channel_id=1, source_target_pairs={{0,3},{1,2},{2,1},{3,0},{4,7},{5,6},{6,5},{7,4},{8,9},{9,8},{10,11... | collective-permute-start | bytes 786440 | tf_op jit(solution)/shard_map/ppermute | solution.py:45
  180.4 7.1 %collective-permute-start.27 = (f32[4,128,128]{2,1,0:T(8,128)S(1)}, f32[4,128,128]{2,1,0:T(8,128)S(1)}, u32[]{:S(2)}, u32[]{:S(2)}) collective-permute-start(f32[4,128,128]{2,1,0:T(8,128)S(1)} %get-tuple-element.30), channel_id=1, source_target_pairs={{0,20},{1,21},{2,22},{3,23},{4,16},{5,17},{6,18},{7,19},{8,12},{9,... | collective-permute-start | bytes 786440 | tf_op jit(solution)/shard_map/ppermute | solution.py:45
  187.5 6.9 %collective-permute-start.28 = (f32[2,128,128]{2,1,0:T(8,128)S(1)}, f32[2,128,128]{2,1,0:T(8,128)S(1)}, u32[]{:S(2)}, u32[]{:S(2)}) collective-permute-start(f32[2,128,128]{2,1,0:T(8,128)S(1)} %slice_add_fusion.8), channel_id=1, source_target_pairs={{0,1},{1,0},{2,3},{3,2},{4,5},{5,4},{6,7},{7,6},{8,11},{9,10},{10,... | collective-permute-start | bytes 393224 | tf_op jit(solution)/shard_map/ppermute | solution.py:45
  194.5 17.4 %collective-permute-start.29 = (f32[4,128,128]{2,1,0:T(8,128)S(1)}, f32[4,128,128]{2,1,0:T(8,128)S(1)}, u32[]{:S(2)}, u32[]{:S(2)}) collective-permute-start(f32[4,128,128]{2,1,0:T(8,128)S(1)} %pad_maximum_fusion.1), channel_id=1, source_target_pairs={{8,392},{9,393},{10,394},{11,395},{12,396},{13,397},{14,398},{15,3... | collective-permute-start | bytes 786440 | tf_op jit(solution)/shard_map/ppermute | solution.py:45
  195.2 30.3 %collective-permute-start.31 = (f32[4,128,128]{2,1,0:T(8,128)S(1)}, f32[4,128,128]{2,1,0:T(8,128)S(1)}, u32[]{:S(2)}, u32[]{:S(2)}) collective-permute-start(f32[4,128,128]{2,1,0:T(8,128)S(1)} %pad_maximum_fusion.1), channel_id=1, source_target_pairs={{0,392},{1,393},{2,394},{3,395},{4,396},{5,397},{6,398},{7,399},{2... | collective-permute-start | bytes 786440 | tf_op jit(solution)/shard_map/ppermute | solution.py:45
  208.6 23.0 %collective-permute-start.18 = (f32[4,128,128]{2,1,0:T(8,128)}, f32[4,128,128]{2,1,0:T(8,128)S(1)}, u32[]{:S(2)}, u32[]{:S(2)}) collective-permute-start(f32[4,128,128]{2,1,0:T(8,128)} %reduce-scatter.2.cloned.1.call-done), channel_id=1, source_target_pairs={{0,0},{1,1},{2,2},{3,3},{4,4},{5,5},{6,6},{7,7},{24,56},{25,57},{2... | collective-permute-start | bytes 786440 | tf_op jit(solution)/shard_map/ppermute | solution.py:45
  210.6 21.0 %collective-permute-start.30 = (f32[4,128,128]{2,1,0:T(8,128)}, f32[4,128,128]{2,1,0:T(8,128)S(1)}, u32[]{:S(2)}, u32[]{:S(2)}) collective-permute-start(f32[4,128,128]{2,1,0:T(8,128)} %reduce-scatter.2.cloned.1.call-done), channel_id=1, source_target_pairs={{8,0},{9,1},{10,2},{11,3},{12,4},{13,5},{14,6},{15,7},{16,56},{17,... | collective-permute-start | bytes 786440 | tf_op jit(solution)/shard_map/ppermute | solution.py:45
  (16 other events, 65.5 us)
Sparse Core Ops, SparseCore 0:
  117.0 87.9 reduce-scatter.1

commit v3 on v2

v3 whole, which is shorter than its diff:
```python
import functools

import jax
import jax.numpy as jnp
import numpy as np
from jax import lax
from jax.experimental import pallas as pl
from jax.experimental.pallas import tpu as pltpu
from jax.sharding import Mesh
from jax.sharding import PartitionSpec as P

NB = 1536
NZ = 16
AXES = ("z", "xhi", "core", "xlo", "y")
LEFT = (0, -4, 4, 1)
RIGHT = (0, 0, -4, -3)
YA, YB, XA, XB = range(4)
ORDERS = {
    (0, 0): (YA, XA, YB, XB),
    (0, 1): (XA, YB, XB, YA),
    (1, 0): (YB, XB, YA, XA),
    (1, 1): (XB, YA, XA, YB),
}


def flat(z, xhi, core, xlo, y):
    return (((z % NZ * 2 + xhi) * 2 + core) * 2 + xlo) * 4 + y


def coords():
    for z in range(NZ):
        for xhi in range(2):
            for core in range(2):
                for xlo in range(2):
                    for y in range(4):
                        yield z, xhi, core, xlo, y


def send(value, target):
    pairs = []
    for at in coords():
        to = target(*at)
        if to is not None:
            pairs.append((flat(*at), flat(*to)))
    return lax.ppermute(value, AXES, pairs)


def other_core(z, xhi, core, xlo, y):
    return z, xhi, 1 - core, xlo, y


def ring_z(z, xhi, core, xlo, y):
    return (z - 1 if core == 0 else z + 1), xhi, core, xlo, y


def across(dim, x, y):
    if dim == YA:
        return x, y ^ 1
    if dim == YB:
        return x, (3 - y)
    if dim == XA:
        return x ^ 1, y
    return 3 - x, y


def plane_step(half, step):
    def target(z, xhi, core, xlo, y):
        x, ny = across(ORDERS[core, half][step], xhi * 2 + xlo, y)
        return z, x // 2, core, x % 2, ny

    return target


def home(chunk, same):
    def target(z, xhi, core, xlo, y):
        c = ((0, 3), (1, 2))[chunk][xhi]
        if (core == c % 2) != same:
            return None
        return z + LEFT[c], xhi, c % 2, xlo, y

    return target


def dest_table():
    table = np.zeros((2, 16, 2, 16), np.int32)
    for core in range(2):
        for x in range(4):
            for y in range(4):
                for half in range(2):
                    for index in range(16):
                        nx, ny = x, y
                        for step in range(4):
                            if index >> (3 - step) & 1:
                                nx, ny = across(ORDERS[core, half][step], nx, ny)
                        table[core, x * 4 + y, half, index] = nx * 4 + ny
    return table.reshape(-1)


def sort_kernel(ids_ref, blocks_ref, out_ref):
    count = blocks_ref.shape[0]
    keys = []
    for s in range(count):
        row = ids_ref[0, s]
        keys.append(jnp.where(row >= 0, row * NB + ids_ref[1, s], 2**30 + s))
    for s in range(count):
        rank = jnp.int32(0)
        for o in range(count):
            if o != s:
                rank = rank + jnp.where(keys[o] < keys[s], 1, 0)
        out_ref[rank] = blocks_ref[s]


def sort_blocks(block_ids, blocks):
    return pl.pallas_call(
        sort_kernel,
        out_shape=jax.ShapeDtypeStruct(blocks.shape, blocks.dtype),
        in_specs=[
            pl.BlockSpec(memory_space=pltpu.SMEM),
            pl.BlockSpec(memory_space=pltpu.VMEM),
        ],
        out_specs=pl.BlockSpec(memory_space=pltpu.VMEM),
        name="sort_blocks",
    )(block_ids.T, blocks)


NEAR = 3


def split_into(panel, at, quarter, hi_ref, lo_ref):
    for rho in range(4):
        for col in range(2):
            x = panel[2 * rho + col]
            hi = x.astype(jnp.bfloat16)
            lo = (x - hi.astype(jnp.float32)).astype(jnp.bfloat16)
            lanes = pl.ds(pl.multiple_of(quarter * 256 + col * 128, 128), 128)
            hi_ref[at, rho * 128 : (rho + 1) * 128, lanes] = hi
            lo_ref[at, rho * 128 : (rho + 1) * 128, lanes] = lo


def split_pair(core, panels, hi_ref, lo_ref):
    ahead = 1 - core
    places = ((ahead, core), (ahead, 1 - core), (1 - ahead, 1 - core), (1 - ahead, core))
    for panel, (at, quarter) in zip(panels, places):
        split_into(panel, at, quarter, hi_ref, lo_ref)


def split_kernel(where_ref, *refs):
    core = where_ref[0]
    *panels, hi_ref, lo_ref = refs
    if len(panels) == 2:
        split_into(panels[0], 0, core, hi_ref, lo_ref)
        split_into(panels[1], 0, 1 - core, hi_ref, lo_ref)
    else:
        split_pair(core, panels, hi_ref, lo_ref)


def split_rows(where, *panels):
    vmem = pl.BlockSpec(memory_space=pltpu.VMEM)
    smem = pl.BlockSpec(memory_space=pltpu.SMEM)
    return pl.pallas_call(
        split_kernel,
        out_shape=[jax.ShapeDtypeStruct((len(panels) // 2, 512, 512), jnp.bfloat16)] * 2,
        in_specs=[smem] + [vmem] * len(panels),
        out_specs=[vmem] * 2,
        compiler_params=pltpu.CompilerParams(vmem_limit_bytes=8 << 20),
        name=f"split_{len(panels)}",
    )(where, *panels)


def chunk_kernel(chunk, where_ref, codes_ref, table_ref, *refs):
    core = where_ref[0]
    place = where_ref[1]
    xhi = place // 8
    rows_hi, rows_lo = list(refs[: 2 * NEAR + 2 : 2]), list(refs[1 : 2 * NEAR + 2 : 2])
    refs = refs[2 * NEAR + 2 :]
    if chunk == 1:
        panels, outs = refs[:4], refs[4:8]
        res_ref, far_hi, far_lo = refs[8:]
        split_pair(core, panels, far_hi, far_lo)
        rows_hi.append(far_hi)
        rows_lo.append(far_lo)
    else:
        outs = refs[:4]
        [res_ref] = refs[4:]

    def row(offset):
        at = int(offset > 0)
        return rows_hi[abs(offset)].at[at], rows_lo[abs(offset)].at[at]

    def times(a, b):
        return lax.dot_general(
            a[...], b[...], (((1,), (1,)), ((), ())), preferred_element_type=jnp.float32
        )

    lists = ((0, 3), (1, 2))[chunk]
    held = [(c % 2 ^ core) + 2 * (c // 2 ^ xhi) for c in lists]
    for far, c in enumerate(lists):
        left_hi, left_lo = row(LEFT[c])
        for step in range(4):
            right_hi, right_lo = row(RIGHT[c] + step)
            res_ref[far * 4 + step] = (
                times(left_hi, right_hi) + times(left_hi, right_lo) + times(left_lo, right_hi)
            )
    for half in range(2):
        for side in range(2):

            def pick(index, carry, half=half, side=side):
                at = (core * 16 + place) * 32 + half * 16 + side * 8 + index // 2
                dest = table_ref[at]
                far = dest // 8
                slot = dest % 8 * 8 + core * 4 + half * 2 + index % 2
                code = codes_ref[jnp.where(far == 0, held[0], held[1]), slot]
                good = code >= 0
                code = jnp.maximum(code, 0)
                rows = pl.ds(pl.multiple_of(code // 16 * 128, 128), 128)
                cols = pl.ds(pl.multiple_of(code % 4 * 128, 128), 128)
                block = res_ref[far * 4 + code // 4 % 4, rows, cols]
                outs[half * 2 + side][index] = jnp.where(good, block, jnp.float32(0.0))
                return carry

            lax.fori_loop(0, 16, pick, 0, unroll=4)


def chunk_products(chunk, where, codes, table, split, panels):
    vmem = pl.BlockSpec(memory_space=pltpu.VMEM)
    smem = pl.BlockSpec(memory_space=pltpu.SMEM)
    scratch = [pltpu.VMEM((8, 512, 512), jnp.float32)]
    if chunk == 1:
        scratch += [pltpu.VMEM((2, 512, 512), jnp.bfloat16)] * 2
    return pl.pallas_call(
        functools.partial(chunk_kernel, chunk),
        out_shape=[jax.ShapeDtypeStruct((16, 128, 128), jnp.float32)] * 4,
        in_specs=[smem] * 3 + [vmem] * (len(split) + len(panels)),
        out_specs=[vmem] * 4,
        scratch_shapes=scratch,
        compiler_params=pltpu.CompilerParams(vmem_limit_bytes=20 << 20),
        name=f"products_{chunk}",
    )(where, codes, table, *split, *panels)


def slot_codes(out_ids, row, col):
    i = out_ids[:, 0]
    j = out_ids[:, 1]
    good = (i >= 0) & (j >= 0)
    same_j = (j[None, :] == j[:, None]) & good[None, :]
    same_i = (i[None, :] == i[:, None]) & good[None, :]
    group = lax.rem(j, NZ)
    left = jnp.sum((same_j & (i[None, :] < i[:, None])).astype(jnp.int32), axis=1)
    right = jnp.sum(
        (same_i & (group[None, :] == group[:, None]) & (j[None, :] < j[:, None])).astype(jnp.int32),
        axis=1,
    )
    step = lax.rem(group - row - 4 * col + 8 * NZ, NZ)
    return jnp.where(good, left * 16 + step * 4 + right, -1)


def after(value, *others):
    return lax.optimization_barrier((value, *others))[0]


def halve(keeps, sends, others=((), (), (), ())):
    arrived = []
    for step in range(4):
        received = [
            send(after(sends[h], *others[step]) if others[step] else sends[h], plane_step(h, step))
            for h in range(2)
        ]
        arrived.append(received)
        if step == 3:
            return [keeps[h] + received[h] for h in range(2)], arrived
        mid = keeps[0].shape[0] // 2
        sends = [keeps[h][mid:] + received[h][mid:] for h in range(2)]
        keeps = [keeps[h][:mid] + received[h][:mid] for h in range(2)]


def bring_home(chunk, part):
    return send(part, home(chunk, True)), send(part, home(chunk, False))


def to_place(z, xhi, core, xlo, y):
    return z - LEFT[xhi * 2 + core], xhi, core, xlo, y


def other_xhi(z, xhi, core, xlo, y):
    return z, 1 - xhi, core, xlo, y


def shards(blocks, block_ids, out_ids):
    z = lax.axis_index("z")
    xhi = lax.axis_index("xhi")
    core = lax.axis_index("core")
    x = xhi * 2 + lax.axis_index("xlo")
    where = jnp.stack([core, x * 4 + lax.axis_index("y")]).astype(jnp.int32)
    table = jnp.asarray(dest_table())

    codes = send(slot_codes(out_ids, z, xhi * 2 + core)[None], to_place)
    codes = jnp.concatenate([codes, send(codes, other_core)], axis=0)
    codes = jnp.concatenate([codes, send(codes, other_xhi)], axis=0)

    mine_a = [sort_blocks(block_ids, blocks)]
    mine_b = [send(mine_a[0], other_core)]
    split = [split_rows(where, mine_a[0], mine_b[0])]
    their_a, their_b = [None], [None]
    for k in range(1, 5):
        next_a, next_b = mine_a[-1], mine_b[-1]
        if k == 2:
            next_a = after(next_a, codes)
        if k > 2:
            next_a = after(next_a, their_a[k - 2])
            next_b = after(next_b, split[k - 2][0])
        mine_a.append(send(next_a, ring_z))
        mine_b.append(send(next_b, ring_z))
        swap_a = mine_a[k] if k <= NEAR else after(mine_a[k], split[k - 1][0])
        their_a.append(send(swap_a, other_core))
        their_b.append(send(mine_b[k], other_core))
        if k <= NEAR:
            split.append(split_rows(where, mine_a[k], mine_b[k], their_a[k], their_b[k]))
    split = [part for pair in split for part in pair]

    keep0, send0, keep1, send1 = chunk_products(
        1, where, codes, table, split, [mine_a[4], mine_b[4], their_a[4], their_b[4]]
    )
    parts, arrived = halve([keep0, keep1], [send0, send1])
    far_home = bring_home(1, jnp.concatenate(parts, axis=0))
    first_codes = after(codes, keep0)
    keep0, send0, keep1, send1 = chunk_products(0, where, first_codes, table, split, [])
    parts, _ = halve([keep0, keep1], [send0, send1], ((), arrived[2], arrived[3], ()))
    near_home = bring_home(0, jnp.concatenate(parts, axis=0))

    same, cross = [jnp.where(core == xhi, a, b) for a, b in zip(near_home, far_home)]
    first = jnp.where(core == 0, same, cross)
    second = jnp.where(core == 0, cross, same)
    return jnp.concatenate([first, second], axis=0)


def solution(mesh):
    fine = Mesh(mesh.devices.reshape(16, 2, 2, 2, 4), AXES)
    return jax.shard_map(
        shards,
        mesh=fine,
        in_specs=(P(AXES, None, None), P(AXES, None), P(("z", "xhi", "core"), None)),
        out_specs=P(AXES, None, None),
        check_vma=False,
    )
```

time: 241 us -> 216 us (0.90)
  the two profiles are of different devices: /device:TPU:7 before, /device:TPU:5 now
where the time goes in v3:
time: 216 us; the launch traced here: 215 us
  starting transfers between devices  131 us (61%)
  waiting for transfers between devices  55.9 us (26%)
  Pallas kernels  24.4 us (11%)
  other arithmetic  2.21 us (1%)
    ppermute x40, starting transfers between devices, send(): return lax.ppermute(value, AXES, pairs)  131 us
    ppermute x40, waiting for transfers between devices, send(): return lax.ppermute(value, AXES, pairs)  55.9 us
    pallas_call x2, Pallas kernels, chunk_products(): pl.pallas_call(functools.partial(chunk_kernel, chunk), out_shape=[jax.Sha...  19.1 us
  transfers between devices with their start and end apart: 40, of which 17 were waited for; matrix products, arithmetic and copies ran while one was open for 1% of the time, Pallas kernels for 6%

profile of v3, /device:TPU:5, one launch (start us, length us, event | category | flops | bytes accessed | tf_op | source)
XLA Modules:
  0.0 215.3 jit_solution(5309208545169128997)
XLA Ops:
  1.9 3.5 %collective-permute-start.4 = (f32[8,128,128]{2,1,0:T(8,128)}, f32[8,128,128]{2,1,0:T(8,128)S(1)}, u32[]{:S(2)}, u32[]{:S(2)}) collective-permute-start(f32[8,128,128]{2,1,0:T(8,128)} %sort_blocks.1.refs_0_), channel_id=1, source_target_pairs={{0,480},{1,481},{2,482},{3,483},{4,484},{5,485},{6,486},{7,487},{8... | collective-permute-start | bytes 1572872 | tf_op jit(solution)/shard_map/ppermute | solution.py:45
  5.5 10.4 %collective-permute-start.3 = (f32[8,128,128]{2,1,0:T(8,128)}, f32[8,128,128]{2,1,0:T(8,128)S(1)}, u32[]{:S(2)}, u32[]{:S(2)}) collective-permute-start(f32[8,128,128]{2,1,0:T(8,128)} %sort_blocks.1.refs_0_), channel_id=1, source_target_pairs={{0,8},{1,9},{2,10},{3,11},{4,12},{5,13},{6,14},{7,15},{8,0},{9,1},... | collective-permute-start | bytes 1572872 | tf_op jit(solution)/shard_map/ppermute | solution.py:45
  20.6 4.6 %collective-permute-start = (s32[1,64]{1,0:T(1,128)S(1)}, s32[1,64]{1,0:T(1,128)S(1)}, u32[]{:S(2)}, u32[]{:S(2)}) collective-permute-start(s32[1,64]{1,0:T(1,128)S(1)} %fusion.4), channel_id=1, source_target_pairs={{0,0},{1,1},{2,2},{3,3},{4,4},{5,5},{6,6},{7,7},{8,136},{9,137},{1... | collective-permute-start | bytes 776 | tf_op jit(solution)/shard_map/ppermute | solution.py:45
  25.9 7.3 %collective-permute-start.1 = (s32[1,64]{1,0:T(1,128)S(1)}, s32[1,64]{1,0:T(1,128)S(1)}, u32[]{:S(2)}, u32[]{:S(2)}) collective-permute-start(s32[1,64]{1,0:T(1,128)S(1)} %collective-permute-done), channel_id=1, source_target_pairs={{0,8},{1,9},{2,10},{3,11},{4,12},{5,13},{6,14},{7,15},{8,0},{9,1},... | collective-permute-start | bytes 776 | tf_op jit(solution)/shard_map/ppermute | solution.py:45
  35.9 3.9 %collective-permute-done.2 = s32[2,64]{1,0:T(2,128)S(1)} collective-permute-done((s32[2,64]{1,0:T(2,128)S(1)}, s32[2,64]{1,0:T(2,128)S(1)}, u32[]{:S(2)}, u32[]{:S(2)}) %collective-permute-start.2) | collective-permute-done | bytes 544 | tf_op jit(solution)/shard_map/ppermute | solution.py:45
  42.5 3.6 %collective-permute-start.6 = (f32[8,128,128]{2,1,0:T(8,128)S(1)}, f32[8,128,128]{2,1,0:T(8,128)S(1)}, u32[]{:S(2)}, u32[]{:S(2)}) collective-permute-start(f32[8,128,128]{2,1,0:T(8,128)S(1)} %collective-permute-done.4.refs_0_), channel_id=1, source_target_pairs={{0,8},{1,9},{2,10},{3,11},{4,12},{5,13},{6,14},{7,15},{8,0},{9,1},... | collective-permute-start | bytes 1572872 | tf_op jit(solution)/shard_map/ppermute | solution.py:45
  53.5 4.9 %collective-permute-start.10 = (f32[8,128,128]{2,1,0:T(8,128)S(1)}, f32[8,128,128]{2,1,0:T(8,128)S(1)}, u32[]{:S(2)}, u32[]{:S(2)}) collective-permute-start(f32[8,128,128]{2,1,0:T(8,128)S(1)} %collective-permute-done.8.refs_0_), channel_id=1, source_target_pairs={{0,8},{1,9},{2,10},{3,11},{4,12},{5,13},{6,14},{7,15},{8,0},{9,1},... | collective-permute-start | bytes 1572872 | tf_op jit(solution)/shard_map/ppermute | solution.py:45
  61.3 4.4 %collective-permute-start.11 = (f32[8,128,128]{2,1,0:T(8,128)S(1)}, f32[8,128,128]{2,1,0:T(8,128)S(1)}, u32[]{:S(2)}, u32[]{:S(2)}) collective-permute-start(f32[8,128,128]{2,1,0:T(8,128)S(1)} %collective-permute-done.9.refs_1_), channel_id=1, source_target_pairs={{0,8},{1,9},{2,10},{3,11},{4,12},{5,13},{6,14},{7,15},{8,0},{9,1},... | collective-permute-start | bytes 1572872 | tf_op jit(solution)/shard_map/ppermute | solution.py:45
  80.1 4.2 %collective-permute-done.16.refs_8_ = f32[8,128,128]{2,1,0:T(8,128)S(1)} collective-permute-done((f32[8,128,128]{2,1,0:T(8,128)S(1)}, f32[8,128,128]{2,1,0:T(8,128)S(1)}, u32[]{:S(2)}, u32[]{:S(2)}) %collective-permute-start.16) | collective-permute-done | bytes 524320 | tf_op jit(solution)/shard_map/ppermute | solution.py:45
  86.6 3.3 %collective-permute-done.17.refs_9_ = f32[8,128,128]{2,1,0:T(8,128)S(1)} collective-permute-done((f32[8,128,128]{2,1,0:T(8,128)S(1)}, f32[8,128,128]{2,1,0:T(8,128)S(1)}, u32[]{:S(2)}, u32[]{:S(2)}) %collective-permute-start.17) | collective-permute-done | bytes 524320 | tf_op jit(solution)/shard_map/ppermute | solution.py:45
  94.4 9.7 %products_1.1 = (f32[16,128,128]{2,1,0:T(8,128)S(1)}, f32[16,128,128]{2,1,0:T(8,128)S(1)}, f32[16,128,128]{2,1,0:T(8,128)S(1)}, f32[16,128,128]{2,1,0:T(8,128)S(1)}) custom-call(s32[2]{0:T(128)S(1)} %pad_add_fusion.2.where_ref, s32[4,64]{1,0:T(4,128)S(1)} %pad_add_fusion.codes_ref, s32[1024]{0:T(1024)S(1)} %copy-done.3, ...), custom_call_target="tpu_custom_call" | custom-call | tf_op jit(solution)/shard_map/products_1/pallas_call | solution.py:230
  104.1 4.7 %collective-permute-start.21 = (f32[16,128,128]{2,1,0:T(8,128)S(1)}, f32[16,128,128]{2,1,0:T(8,128)S(1)}, u32[]{:S(2)}, u32[]{:S(2)}) collective-permute-start(f32[16,128,128]{2,1,0:T(8,128)S(1)} %get-tuple-element.50), channel_id=1, source_target_pairs={{0,1},{1,0},{2,3},{3,2},{4,5},{5,4},{6,7},{7,6},{8,11},{9,10},{10,... | collective-permute-start | bytes 3145736 | tf_op jit(solution)/shard_map/ppermute | solution.py:45
  110.9 9.4 %products_0.1 = (f32[16,128,128]{2,1,0:T(8,128)S(1)}, f32[16,128,128]{2,1,0:T(8,128)S(1)}, f32[16,128,128]{2,1,0:T(8,128)S(1)}, f32[16,128,128]{2,1,0:T(8,128)S(1)}) custom-call(s32[2]{0:T(128)S(1)} %pad_add_fusion.2.where_ref, s32[4,64]{1,0:T(4,128)S(1)} %pad_add_fusion.codes_ref, s32[1024]{0:T(1024)S(1)} %copy-done.3, ...), custom_call_target="tpu_custom_call" | custom-call | tf_op jit(solution)/shard_map/products_0/pallas_call | solution.py:230
  122.3 3.3 %collective-permute-start.32 = (f32[16,128,128]{2,1,0:T(8,128)S(1)}, f32[16,128,128]{2,1,0:T(8,128)S(1)}, u32[]{:S(2)}, u32[]{:S(2)}) collective-permute-start(f32[16,128,128]{2,1,0:T(8,128)S(1)} %get-tuple-element.56), channel_id=1, source_target_pairs={{0,4},{1,5},{2,6},{3,7},{4,0},{5,1},{6,2},{7,3},{8,28},{9,29},{10,... | collective-permute-start | bytes 3145736 | tf_op jit(solution)/shard_map/ppermute | solution.py:45
  129.9 9.4 %collective-permute-done.20 = f32[16,128,128]{2,1,0:T(8,128)S(1)} collective-permute-done((f32[16,128,128]{2,1,0:T(8,128)S(1)}, f32[16,128,128]{2,1,0:T(8,128)S(1)}, u32[]{:S(2)}, u32[]{:S(2)}) %collective-permute-start.20) | collective-permute-done | bytes 1048608 | tf_op jit(solution)/shard_map/ppermute | solution.py:45
  139.4 4.4 %collective-permute-done.22 = f32[8,128,128]{2,1,0:T(8,128)S(1)} collective-permute-done((f32[8,128,128]{2,1,0:T(8,128)S(1)}, f32[8,128,128]{2,1,0:T(8,128)S(1)}, u32[]{:S(2)}, u32[]{:S(2)}) %collective-permute-start.22) | collective-permute-done | bytes 524320 | tf_op jit(solution)/shard_map/ppermute | solution.py:45
  145.8 3.7 %collective-permute-start.26 = (f32[4,128,128]{2,1,0:T(8,128)S(1)}, f32[4,128,128]{2,1,0:T(8,128)S(1)}, u32[]{:S(2)}, u32[]{:S(2)}) collective-permute-start(f32[4,128,128]{2,1,0:T(8,128)S(1)} %get-tuple-element.76), channel_id=1, source_target_pairs={{0,20},{1,21},{2,22},{3,23},{4,16},{5,17},{6,18},{7,19},{8,12},{9,... | collective-permute-start | bytes 786440 | tf_op jit(solution)/shard_map/ppermute | solution.py:45
  150.9 4.0 %collective-permute-start.28 = (f32[2,128,128]{2,1,0:T(8,128)S(1)}, f32[2,128,128]{2,1,0:T(8,128)S(1)}, u32[]{:S(2)}, u32[]{:S(2)}) collective-permute-start(f32[2,128,128]{2,1,0:T(8,128)S(1)} %slice_add_fusion.23), channel_id=1, source_target_pairs={{0,20},{1,21},{2,22},{3,23},{4,16},{5,17},{6,18},{7,19},{8,12},{9,... | collective-permute-start | bytes 393224 | tf_op jit(solution)/shard_map/ppermute | solution.py:45
  154.9 3.8 %collective-permute-start.27 = (f32[8,128,128]{2,1,0:T(8,128)S(1)}, f32[8,128,128]{2,1,0:T(8,128)S(1)}, u32[]{:S(2)}, u32[]{:S(2)}) collective-permute-start(f32[8,128,128]{2,1,0:T(8,128)S(1)} %get-tuple-element.53), channel_id=1, source_target_pairs={{0,4},{1,5},{2,6},{3,7},{4,0},{5,1},{6,2},{7,3},{8,28},{9,29},{10,... | collective-permute-start | bytes 1572872 | tf_op jit(solution)/shard_map/ppermute | solution.py:45
  158.8 4.7 %collective-permute-start.29 = (f32[2,128,128]{2,1,0:T(8,128)S(1)}, f32[2,128,128]{2,1,0:T(8,128)S(1)}, u32[]{:S(2)}, u32[]{:S(2)}) collective-permute-start(f32[2,128,128]{2,1,0:T(8,128)S(1)} %slice_add_fusion.22), channel_id=1, source_target_pairs={{0,1},{1,0},{2,3},{3,2},{4,5},{5,4},{6,7},{7,6},{8,11},{9,10},{10,... | collective-permute-start | bytes 393224 | tf_op jit(solution)/shard_map/ppermute | solution.py:45
  169.1 5.7 %collective-permute-done.33 = f32[8,128,128]{2,1,0:T(8,128)S(1)} collective-permute-done((f32[8,128,128]{2,1,0:T(8,128)S(1)}, f32[8,128,128]{2,1,0:T(8,128)S(1)}, u32[]{:S(2)}, u32[]{:S(2)}) %collective-permute-start.33) | collective-permute-done | bytes 524320 | tf_op jit(solution)/shard_map/ppermute | solution.py:45
  177.4 11.2 %collective-permute-start.39 = (f32[4,128,128]{2,1,0:T(8,128)S(1)}, f32[4,128,128]{2,1,0:T(8,128)S(1)}, u32[]{:S(2)}, u32[]{:S(2)}) collective-permute-start(f32[4,128,128]{2,1,0:T(8,128)S(1)} %pad_maximum_fusion.2), channel_id=1, source_target_pairs={{0,392},{1,393},{2,394},{3,395},{4,396},{5,397},{6,398},{7,399},{2... | collective-permute-start | bytes 786440 | tf_op jit(solution)/shard_map/ppermute | solution.py:45
  191.4 4.3 %collective-permute-start.35 = (f32[2,128,128]{2,1,0:T(8,128)S(1)}, f32[2,128,128]{2,1,0:T(8,128)S(1)}, u32[]{:S(2)}, u32[]{:S(2)}) collective-permute-start(f32[2,128,128]{2,1,0:T(8,128)S(1)} %slice_add_fusion.18), channel_id=1, source_target_pairs={{0,1},{1,0},{2,3},{3,2},{4,5},{5,4},{6,7},{7,6},{8,11},{9,10},{10,... | collective-permute-start | bytes 393224 | tf_op jit(solution)/shard_map/ppermute | solution.py:45
  201.9 12.4 %collective-permute-done.36 = f32[4,128,128]{2,1,0:T(8,128)S(1)} collective-permute-done((f32[4,128,128]{2,1,0:T(8,128)S(1)}, f32[4,128,128]{2,1,0:T(8,128)S(1)}, u32[]{:S(2)}, u32[]{:S(2)}) %collective-permute-start.36) | collective-permute-done | bytes 262176 | tf_op jit(solution)/shard_map/ppermute | solution.py:45
  (101 shorter events, 73.7 us)
Async XLA Ops:
  1.9 37.9 %collective-permute-start.4 = (f32[8,128,128]{2,1,0:T(8,128)}, f32[8,128,128]{2,1,0:T(8,128)S(1)}, u32[]{:S(2)}, u32[]{:S(2)}) collective-permute-start(f32[8,128,128]{2,1,0:T(8,128)} %sort_blocks.1.refs_0_), channel_id=1, source_target_pairs={{0,480},{1,481},{2,482},{3,483},{4,484},{5,485},{6,486},{7,487},{8... | collective-permute-start | bytes 1572872 | tf_op jit(solution)/shard_map/ppermute | solution.py:45
  5.5 12.2 %collective-permute-start.3 = (f32[8,128,128]{2,1,0:T(8,128)}, f32[8,128,128]{2,1,0:T(8,128)S(1)}, u32[]{:S(2)}, u32[]{:S(2)}) collective-permute-start(f32[8,128,128]{2,1,0:T(8,128)} %sort_blocks.1.refs_0_), channel_id=1, source_target_pairs={{0,8},{1,9},{2,10},{3,11},{4,12},{5,13},{6,14},{7,15},{8,0},{9,1},... | collective-permute-start | bytes 1572872 | tf_op jit(solution)/shard_map/ppermute | solution.py:45
  17.7 28.5 %collective-permute-start.5 = (f32[8,128,128]{2,1,0:T(8,128)S(1)}, f32[8,128,128]{2,1,0:T(8,128)S(1)}, u32[]{:S(2)}, u32[]{:S(2)}) collective-permute-start(f32[8,128,128]{2,1,0:T(8,128)S(1)} %collective-permute-done.3.refs_1_), channel_id=1, source_target_pairs={{0,480},{1,481},{2,482},{3,483},{4,484},{5,485},{6,486},{7,487},{8... | collective-permute-start | bytes 1572872 | tf_op jit(solution)/shard_map/ppermute | solution.py:45
  46.2 12.3 %collective-permute-start.7 = (f32[8,128,128]{2,1,0:T(8,128)S(1)}, f32[8,128,128]{2,1,0:T(8,128)S(1)}, u32[]{:S(2)}, u32[]{:S(2)}) collective-permute-start(f32[8,128,128]{2,1,0:T(8,128)S(1)} %collective-permute-done.5.refs_1_), channel_id=1, source_target_pairs={{0,8},{1,9},{2,10},{3,11},{4,12},{5,13},{6,14},{7,15},{8,0},{9,1},... | collective-permute-start | bytes 1572872 | tf_op jit(solution)/shard_map/ppermute | solution.py:45
  51.0 14.7 %collective-permute-start.12 = (f32[8,128,128]{2,1,0:T(8,128)S(1)}, f32[8,128,128]{2,1,0:T(8,128)S(1)}, u32[]{:S(2)}, u32[]{:S(2)}) collective-permute-start(f32[8,128,128]{2,1,0:T(8,128)S(1)} %collective-permute-done.8.refs_0_), channel_id=1, source_target_pairs={{0,480},{1,481},{2,482},{3,483},{4,484},{5,485},{6,486},{7,487},{8... | collective-permute-start | bytes 1572872 | tf_op jit(solution)/shard_map/ppermute | solution.py:45
  53.5 12.2 %collective-permute-start.10 = (f32[8,128,128]{2,1,0:T(8,128)S(1)}, f32[8,128,128]{2,1,0:T(8,128)S(1)}, u32[]{:S(2)}, u32[]{:S(2)}) collective-permute-start(f32[8,128,128]{2,1,0:T(8,128)S(1)} %collective-permute-done.8.refs_0_), channel_id=1, source_target_pairs={{0,8},{1,9},{2,10},{3,11},{4,12},{5,13},{6,14},{7,15},{8,0},{9,1},... | collective-permute-start | bytes 1572872 | tf_op jit(solution)/shard_map/ppermute | solution.py:45
  61.3 14.2 %collective-permute-start.11 = (f32[8,128,128]{2,1,0:T(8,128)S(1)}, f32[8,128,128]{2,1,0:T(8,128)S(1)}, u32[]{:S(2)}, u32[]{:S(2)}) collective-permute-start(f32[8,128,128]{2,1,0:T(8,128)S(1)} %collective-permute-done.9.refs_1_), channel_id=1, source_target_pairs={{0,8},{1,9},{2,10},{3,11},{4,12},{5,13},{6,14},{7,15},{8,0},{9,1},... | collective-permute-start | bytes 1572872 | tf_op jit(solution)/shard_map/ppermute | solution.py:45
  65.7 13.4 %collective-permute-start.14 = (f32[8,128,128]{2,1,0:T(8,128)S(1)}, f32[8,128,128]{2,1,0:T(8,128)S(1)}, u32[]{:S(2)}, u32[]{:S(2)}) collective-permute-start(f32[8,128,128]{2,1,0:T(8,128)S(1)} %collective-permute-done.12.refs_0_), channel_id=1, source_target_pairs={{0,8},{1,9},{2,10},{3,11},{4,12},{5,13},{6,14},{7,15},{8,0},{9,1},... | collective-permute-start | bytes 1572872 | tf_op jit(solution)/shard_map/ppermute | solution.py:45
  72.8 11.4 %collective-permute-start.16 = (f32[8,128,128]{2,1,0:T(8,128)S(1)}, f32[8,128,128]{2,1,0:T(8,128)S(1)}, u32[]{:S(2)}, u32[]{:S(2)}) collective-permute-start(f32[8,128,128]{2,1,0:T(8,128)S(1)} %collective-permute-done.12.refs_0_), channel_id=1, source_target_pairs={{0,480},{1,481},{2,482},{3,483},{4,484},{5,485},{6,486},{7,487},{8... | collective-permute-start | bytes 1572872 | tf_op jit(solution)/shard_map/ppermute | solution.py:45
  76.4 13.5 %collective-permute-start.17 = (f32[8,128,128]{2,1,0:T(8,128)S(1)}, f32[8,128,128]{2,1,0:T(8,128)S(1)}, u32[]{:S(2)}, u32[]{:S(2)}) collective-permute-start(f32[8,128,128]{2,1,0:T(8,128)S(1)} %collective-permute-done.13.refs_1_), channel_id=1, source_target_pairs={{0,480},{1,481},{2,482},{3,483},{4,484},{5,485},{6,486},{7,487},{8... | collective-permute-start | bytes 1572872 | tf_op jit(solution)/shard_map/ppermute | solution.py:45
  104.1 21.5 %collective-permute-start.21 = (f32[16,128,128]{2,1,0:T(8,128)S(1)}, f32[16,128,128]{2,1,0:T(8,128)S(1)}, u32[]{:S(2)}, u32[]{:S(2)}) collective-permute-start(f32[16,128,128]{2,1,0:T(8,128)S(1)} %get-tuple-element.50), channel_id=1, source_target_pairs={{0,1},{1,0},{2,3},{3,2},{4,5},{5,4},{6,7},{7,6},{8,11},{9,10},{10,... | collective-permute-start | bytes 3145736 | tf_op jit(solution)/shard_map/ppermute | solution.py:45
  108.7 19.0 %collective-permute-start.24 = (f32[16,128,128]{2,1,0:T(8,128)S(1)}, f32[16,128,128]{2,1,0:T(8,128)S(1)}, u32[]{:S(2)}, u32[]{:S(2)}) collective-permute-start(f32[16,128,128]{2,1,0:T(8,128)S(1)} %get-tuple-element.52), channel_id=1, source_target_pairs={{0,4},{1,5},{2,6},{3,7},{4,0},{5,1},{6,2},{7,3},{8,28},{9,29},{10,... | collective-permute-start | bytes 3145736 | tf_op jit(solution)/shard_map/ppermute | solution.py:45
  120.4 18.9 %collective-permute-start.20 = (f32[16,128,128]{2,1,0:T(8,128)S(1)}, f32[16,128,128]{2,1,0:T(8,128)S(1)}, u32[]{:S(2)}, u32[]{:S(2)}) collective-permute-start(f32[16,128,128]{2,1,0:T(8,128)S(1)} %get-tuple-element.49), channel_id=1, source_target_pairs={{0,1},{1,0},{2,3},{3,2},{4,5},{5,4},{6,7},{7,6},{8,11},{9,10},{10,... | collective-permute-start | bytes 3145736 | tf_op jit(solution)/shard_map/ppermute | solution.py:45
  122.3 27.2 %collective-permute-start.32 = (f32[16,128,128]{2,1,0:T(8,128)S(1)}, f32[16,128,128]{2,1,0:T(8,128)S(1)}, u32[]{:S(2)}, u32[]{:S(2)}) collective-permute-start(f32[16,128,128]{2,1,0:T(8,128)S(1)} %get-tuple-element.56), channel_id=1, source_target_pairs={{0,4},{1,5},{2,6},{3,7},{4,0},{5,1},{6,2},{7,3},{8,28},{9,29},{10,... | collective-permute-start | bytes 3145736 | tf_op jit(solution)/shard_map/ppermute | solution.py:45
  125.7 18.0 %collective-permute-start.22 = (f32[8,128,128]{2,1,0:T(8,128)S(1)}, f32[8,128,128]{2,1,0:T(8,128)S(1)}, u32[]{:S(2)}, u32[]{:S(2)}) collective-permute-start(f32[8,128,128]{2,1,0:T(8,128)S(1)} %get-tuple-element.68), channel_id=1, source_target_pairs={{0,4},{1,5},{2,6},{3,7},{4,0},{5,1},{6,2},{7,3},{8,28},{9,29},{10,... | collective-permute-start | bytes 1572872 | tf_op jit(solution)/shard_map/ppermute | solution.py:45
  127.9 17.8 %collective-permute-start.25 = (f32[8,128,128]{2,1,0:T(8,128)S(1)}, f32[8,128,128]{2,1,0:T(8,128)S(1)}, u32[]{:S(2)}, u32[]{:S(2)}) collective-permute-start(f32[8,128,128]{2,1,0:T(8,128)S(1)} %get-tuple-element.66), channel_id=1, source_target_pairs={{0,3},{1,2},{2,1},{3,0},{4,7},{5,6},{6,5},{7,4},{8,9},{9,8},{10,11... | collective-permute-start | bytes 1572872 | tf_op jit(solution)/shard_map/ppermute | solution.py:45
  150.9 14.5 %collective-permute-start.28 = (f32[2,128,128]{2,1,0:T(8,128)S(1)}, f32[2,128,128]{2,1,0:T(8,128)S(1)}, u32[]{:S(2)}, u32[]{:S(2)}) collective-permute-start(f32[2,128,128]{2,1,0:T(8,128)S(1)} %slice_add_fusion.23), channel_id=1, source_target_pairs={{0,20},{1,21},{2,22},{3,23},{4,16},{5,17},{6,18},{7,19},{8,12},{9,... | collective-permute-start | bytes 393224 | tf_op jit(solution)/shard_map/ppermute | solution.py:45
  154.9 12.1 %collective-permute-start.27 = (f32[8,128,128]{2,1,0:T(8,128)S(1)}, f32[8,128,128]{2,1,0:T(8,128)S(1)}, u32[]{:S(2)}, u32[]{:S(2)}) collective-permute-start(f32[8,128,128]{2,1,0:T(8,128)S(1)} %get-tuple-element.53), channel_id=1, source_target_pairs={{0,4},{1,5},{2,6},{3,7},{4,0},{5,1},{6,2},{7,3},{8,28},{9,29},{10,... | collective-permute-start | bytes 1572872 | tf_op jit(solution)/shard_map/ppermute | solution.py:45
  167.1 21.6 %collective-permute-start.30 = (f32[4,128,128]{2,1,0:T(8,128)S(1)}, f32[4,128,128]{2,1,0:T(8,128)S(1)}, u32[]{:S(2)}, u32[]{:S(2)}) collective-permute-start(f32[4,128,128]{2,1,0:T(8,128)S(1)} %get-tuple-element.54), channel_id=1, source_target_pairs={{0,3},{1,2},{2,1},{3,0},{4,7},{5,6},{6,5},{7,4},{8,9},{9,8},{10,11... | collective-permute-start | bytes 786440 | tf_op jit(solution)/shard_map/ppermute | solution.py:45
  174.8 16.6 %collective-permute-start.34 = (f32[4,128,128]{2,1,0:T(8,128)S(1)}, f32[4,128,128]{2,1,0:T(8,128)S(1)}, u32[]{:S(2)}, u32[]{:S(2)}) collective-permute-start(f32[4,128,128]{2,1,0:T(8,128)S(1)} %get-tuple-element.58), channel_id=1, source_target_pairs={{0,20},{1,21},{2,22},{3,23},{4,16},{5,17},{6,18},{7,19},{8,12},{9,... | collective-permute-start | bytes 786440 | tf_op jit(solution)/shard_map/ppermute | solution.py:45
  176.7 25.2 %collective-permute-start.37 = (f32[4,128,128]{2,1,0:T(8,128)S(1)}, f32[4,128,128]{2,1,0:T(8,128)S(1)}, u32[]{:S(2)}, u32[]{:S(2)}) collective-permute-start(f32[4,128,128]{2,1,0:T(8,128)S(1)} %pad_maximum_fusion.2), channel_id=1, source_target_pairs={{8,392},{9,393},{10,394},{11,395},{12,396},{13,397},{14,398},{15,3... | collective-permute-start | bytes 786440 | tf_op jit(solution)/shard_map/ppermute | solution.py:45
  177.4 24.5 %collective-permute-start.39 = (f32[4,128,128]{2,1,0:T(8,128)S(1)}, f32[4,128,128]{2,1,0:T(8,128)S(1)}, u32[]{:S(2)}, u32[]{:S(2)}) collective-permute-start(f32[4,128,128]{2,1,0:T(8,128)S(1)} %pad_maximum_fusion.2), channel_id=1, source_target_pairs={{0,392},{1,393},{2,394},{3,395},{4,396},{5,397},{6,398},{7,399},{2... | collective-permute-start | bytes 786440 | tf_op jit(solution)/shard_map/ppermute | solution.py:45
  198.7 15.7 %collective-permute-start.36 = (f32[4,128,128]{2,1,0:T(8,128)S(1)}, f32[4,128,128]{2,1,0:T(8,128)S(1)}, u32[]{:S(2)}, u32[]{:S(2)}) collective-permute-start(f32[4,128,128]{2,1,0:T(8,128)S(1)} %pad_maximum_fusion.1), channel_id=1, source_target_pairs={{0,0},{1,1},{2,2},{3,3},{4,4},{5,5},{6,6},{7,7},{24,56},{25,57},{2... | collective-permute-start | bytes 786440 | tf_op jit(solution)/shard_map/ppermute | solution.py:45
  200.6 13.8 %collective-permute-start.38 = (f32[4,128,128]{2,1,0:T(8,128)S(1)}, f32[4,128,128]{2,1,0:T(8,128)S(1)}, u32[]{:S(2)}, u32[]{:S(2)}) collective-permute-start(f32[4,128,128]{2,1,0:T(8,128)S(1)} %pad_maximum_fusion.1), channel_id=1, source_target_pairs={{8,0},{9,1},{10,2},{11,3},{12,4},{13,5},{14,6},{15,7},{16,56},{17,... | collective-permute-start | bytes 786440 | tf_op jit(solution)/shard_map/ppermute | solution.py:45
  (21 other events, 180.2 us)

commit v4 on v3

--- a/solution.py
+++ b/solution.py
@@ -2,7 +2,6 @@
 
 import jax
 import jax.numpy as jnp
-import numpy as np
 from jax import lax
 from jax.experimental import pallas as pl
 from jax.experimental.pallas import tpu as pltpu
@@ -14,13 +13,6 @@
 AXES = ("z", "xhi", "core", "xlo", "y")
 LEFT = (0, -4, 4, 1)
 RIGHT = (0, 0, -4, -3)
-YA, YB, XA, XB = range(4)
-ORDERS = {
-    (0, 0): (YA, XA, YB, XB),
-    (0, 1): (XA, YB, XB, YA),
-    (1, 0): (YB, XB, YA, XA),
-    (1, 1): (XB, YA, XA, YB),
-}
 
 
 def flat(z, xhi, core, xlo, y):
@@ -53,20 +45,12 @@
     return (z - 1 if core == 0 else z + 1), xhi, core, xlo, y
 
 
-def across(dim, x, y):
-    if dim == YA:
-        return x, y ^ 1
-    if dim == YB:
-        return x, (3 - y)
-    if dim == XA:
-        return x ^ 1, y
-    return 3 - x, y
-
-
-def plane_step(half, step):
+def plane_step(phase, offset):
     def target(z, xhi, core, xlo, y):
-        x, ny = across(ORDERS[core, half][step], xhi * 2 + xlo, y)
-        return z, x // 2, core, x % 2, ny
+        if phase == core:
+            return z, xhi, core, xlo, (y + offset) % 4
+        x = (xhi * 2 + xlo + offset) % 4
+        return z, x // 2, core, x % 2, y
 
     return target
 
@@ -79,21 +63,6 @@
         return z + LEFT[c], xhi, c % 2, xlo, y
 
     return target
-
-
-def dest_table():
-    table = np.zeros((2, 16, 2, 16), np.int32)
-    for core in range(2):
-        for x in range(4):
-            for y in range(4):
-                for half in range(2):
-                    for index in range(16):
-                        nx, ny = x, y
-                        for step in range(4):
-                            if index >> (3 - step) & 1:
-                                nx, ny = across(ORDERS[core, half][step], nx, ny)
-                        table[core, x * 4 + y, half, index] = nx * 4 + ny
-    return table.reshape(-1)
 
 
 def sort_kernel(ids_ref, blocks_ref, out_ref):
@@ -167,7 +136,7 @@
     )(where, *panels)
 
 
-def chunk_kernel(chunk, where_ref, codes_ref, table_ref, *refs):
+def chunk_kernel(chunk, where_ref, codes_ref, *refs):
     core = where_ref[0]
     place = where_ref[1]
     xhi = place // 8
@@ -201,27 +170,28 @@
             res_ref[far * 4 + step] = (
                 times(left_hi, right_hi) + times(left_hi, right_lo) + times(left_lo, right_hi)
             )
-    for half in range(2):
-        for side in range(2):
-
-            def pick(index, carry, half=half, side=side):
-                at = (core * 16 + place) * 32 + half * 16 + side * 8 + index // 2
-                dest = table_ref[at]
-                far = dest // 8
-                slot = dest % 8 * 8 + core * 4 + half * 2 + index % 2
-                code = codes_ref[jnp.where(far == 0, held[0], held[1]), slot]
-                good = code >= 0
-                code = jnp.maximum(code, 0)
-                rows = pl.ds(pl.multiple_of(code // 16 * 128, 128), 128)
-                cols = pl.ds(pl.multiple_of(code % 4 * 128, 128), 128)
-                block = res_ref[far * 4 + code // 4 % 4, rows, cols]
-                outs[half * 2 + side][index] = jnp.where(good, block, jnp.float32(0.0))
-                return carry
-
-            lax.fori_loop(0, 16, pick, 0, unroll=4)
-
-
-def chunk_products(chunk, where, codes, table, split, panels):
+    x, y = place // 4, place % 4
+    for offset in range(4):
+
+        def pick(index, carry, offset=offset):
+            after_that = index // 4
+            to_x = (x + jnp.where(core == 0, after_that, offset)) % 4
+            to_y = (y + jnp.where(core == 0, offset, after_that)) % 4
+            far = to_x // 2
+            slot = (to_x % 2 * 4 + to_y) * 8 + core * 4 + index % 4
+            code = codes_ref[jnp.where(far == 0, held[0], held[1]), slot]
+            good = code >= 0
+            code = jnp.maximum(code, 0)
+            rows = pl.ds(pl.multiple_of(code // 16 * 128, 128), 128)
+            cols = pl.ds(pl.multiple_of(code % 4 * 128, 128), 128)
+            block = res_ref[far * 4 + code // 4 % 4, rows, cols]
+            outs[offset][index] = jnp.where(good, block, jnp.float32(0.0))
+            return carry
+
+        lax.fori_loop(0, 16, pick, 0, unroll=4)
+
+
+def chunk_products(chunk, where, codes, split, panels):
     vmem = pl.BlockSpec(memory_space=pltpu.VMEM)
     smem = pl.BlockSpec(memory_space=pltpu.SMEM)
     scratch = [pltpu.VMEM((8, 512, 512), jnp.float32)]
@@ -230,12 +200,12 @@
     return pl.pallas_call(
         functools.partial(chunk_kernel, chunk),
         out_shape=[jax.ShapeDtypeStruct((16, 128, 128), jnp.float32)] * 4,
-        in_specs=[smem] * 3 + [vmem] * (len(split) + len(panels)),
+        in_specs=[smem] * 2 + [vmem] * (len(split) + len(panels)),
         out_specs=[vmem] * 4,
         scratch_shapes=scratch,
         compiler_params=pltpu.CompilerParams(vmem_limit_bytes=20 << 20),
         name=f"products_{chunk}",
-    )(where, codes, table, *split, *panels)
+    )(where, codes, *split, *panels)
 
 
 def slot_codes(out_ids, row, col):
@@ -258,19 +228,19 @@
     return lax.optimization_barrier((value, *others))[0]
 
 
-def halve(keeps, sends, others=((), (), (), ())):
-    arrived = []
-    for step in range(4):
-        received = [
-            send(after(sends[h], *others[step]) if others[step] else sends[h], plane_step(h, step))
-            for h in range(2)
-        ]
-        arrived.append(received)
-        if step == 3:
-            return [keeps[h] + received[h] for h in range(2)], arrived
-        mid = keeps[0].shape[0] // 2
-        sends = [keeps[h][mid:] + received[h][mid:] for h in range(2)]
-        keeps = [keeps[h][:mid] + received[h][:mid] for h in range(2)]
+def reduce_plane(pieces, others=()):
+    received = [None] * 4
+    for offset in (2, 1, 3):
+        received[offset] = send(pieces[offset], plane_step(0, offset))
+    if others:
+        received[1:] = lax.optimization_barrier((*received[1:], *others))[:3]
+    count = pieces[0].shape[0] // 4
+    total = [
+        sum((received[o][n * count : (n + 1) * count] for o in (1, 2, 3)), pieces[0][n * count : (n + 1) * count])
+        for n in range(4)
+    ]
+    arrived = [send(total[offset], plane_step(1, offset)) for offset in (2, 1, 3)]
+    return total[0] + arrived[0] + arrived[1] + arrived[2], arrived
 
 
 def bring_home(chunk, part):
@@ -291,7 +261,6 @@
     core = lax.axis_index("core")
     x = xhi * 2 + lax.axis_index("xlo")
     where = jnp.stack([core, x * 4 + lax.axis_index("y")]).astype(jnp.int32)
-    table = jnp.asarray(dest_table())
 
     codes = send(slot_codes(out_ids, z, xhi * 2 + core)[None], to_place)
     codes = jnp.concatenate([codes, send(codes, other_core)], axis=0)
@@ -303,11 +272,11 @@
     their_a, their_b = [None], [None]
     for k in range(1, 5):
         next_a, next_b = mine_a[-1], mine_b[-1]
-        if k == 2:
-            next_a = after(next_a, codes)
         if k > 2:
             next_a = after(next_a, their_a[k - 2])
             next_b = after(next_b, split[k - 2][0])
+        if k == 4:
+            next_a = after(next_a, codes)
         mine_a.append(send(next_a, ring_z))
         mine_b.append(send(next_b, ring_z))
         swap_a = mine_a[k] if k <= NEAR else after(mine_a[k], split[k - 1][0])
@@ -317,15 +286,14 @@
             split.append(split_rows(where, mine_a[k], mine_b[k], their_a[k], their_b[k]))
     split = [part for pair in split for part in pair]
 
-    keep0, send0, keep1, send1 = chunk_products(
-        1, where, codes, table, split, [mine_a[4], mine_b[4], their_a[4], their_b[4]]
+    pieces = chunk_products(
+        1, where, codes, split, [mine_a[4], mine_b[4], their_a[4], their_b[4]]
     )
-    parts, arrived = halve([keep0, keep1], [send0, send1])
-    far_home = bring_home(1, jnp.concatenate(parts, axis=0))
-    first_codes = after(codes, keep0)
-    keep0, send0, keep1, send1 = chunk_products(0, where, first_codes, table, split, [])
-    parts, _ = halve([keep0, keep1], [send0, send1], ((), arrived[2], arrived[3], ()))
-    near_home = bring_home(0, jnp.concatenate(parts, axis=0))
+    wide, arrived = reduce_plane(pieces)
+    far_home = bring_home(1, wide)
+    pieces = chunk_products(0, where, after(codes, pieces[0]), split, [])
+    near, _ = reduce_plane(pieces, arrived)
+    near_home = bring_home(0, near)
 
     same, cross = [jnp.where(core == xhi, a, b) for a, b in zip(near_home, far_home)]
     first = jnp.where(core == 0, same, cross)

time: 216 us -> 212 us (0.981)
  the two profiles are of different devices: /device:TPU:5 before, /device:TPU:15 now
where the time goes in v4:
time: 212 us; the launch traced here: 211 us
  starting transfers between devices  114 us (54%)
  waiting for transfers between devices  68.6 us (32%)
  Pallas kernels  24.8 us (12%)
    ppermute x36, starting transfers between devices, send(): return lax.ppermute(value, AXES, pairs)  114 us
    ppermute x36, waiting for transfers between devices, send(): return lax.ppermute(value, AXES, pairs)  68.6 us
    pallas_call x2, Pallas kernels, chunk_products(): pl.pallas_call(functools.partial(chunk_kernel, chunk), out_shape=[jax.Sha...  19.5 us
  transfers between devices with their start and end apart: 36, of which 15 were waited for; matrix products, arithmetic and copies ran while one was open for 0% of the time, Pallas kernels for 6%

profile of v4, /device:TPU:15, one launch (start us, length us, event | category | flops | bytes accessed | tf_op | source)
XLA Modules:
  0.0 210.6 jit_solution(4226667124987277537)
XLA Ops:
  4.5 3.5 %collective-permute-start.4 = (f32[8,128,128]{2,1,0:T(8,128)}, f32[8,128,128]{2,1,0:T(8,128)S(1)}, u32[]{:S(2)}, u32[]{:S(2)}) collective-permute-start(f32[8,128,128]{2,1,0:T(8,128)} %sort_blocks.1.refs_0_), channel_id=1, source_target_pairs={{0,480},{1,481},{2,482},{3,483},{4,484},{5,485},{6,486},{7,487},{8... | collective-permute-start | bytes 1572872 | tf_op jit(solution)/shard_map/ppermute | solution.py:37
  8.1 3.5 %collective-permute-start.5 = (f32[8,128,128]{2,1,0:T(8,128)S(1)}, f32[8,128,128]{2,1,0:T(8,128)S(1)}, u32[]{:S(2)}, u32[]{:S(2)}) collective-permute-start(f32[8,128,128]{2,1,0:T(8,128)S(1)} %collective-permute-done.3.refs_1_), channel_id=1, source_target_pairs={{0,480},{1,481},{2,482},{3,483},{4,484},{5,485},{6,486},{7,487},{8... | collective-permute-start | bytes 1572872 | tf_op jit(solution)/shard_map/ppermute | solution.py:37
  12.3 10.1 %collective-permute-done.4.refs_0_ = f32[8,128,128]{2,1,0:T(8,128)S(1)} collective-permute-done((f32[8,128,128]{2,1,0:T(8,128)}, f32[8,128,128]{2,1,0:T(8,128)S(1)}, u32[]{:S(2)}, u32[]{:S(2)}) %collective-permute-start.4) | collective-permute-done | bytes 524320 | tf_op jit(solution)/shard_map/ppermute | solution.py:37
  28.0 4.2 %collective-permute-start.7 = (f32[8,128,128]{2,1,0:T(8,128)S(1)}, f32[8,128,128]{2,1,0:T(8,128)S(1)}, u32[]{:S(2)}, u32[]{:S(2)}) collective-permute-start(f32[8,128,128]{2,1,0:T(8,128)S(1)} %collective-permute-done.5.refs_1_), channel_id=1, source_target_pairs={{0,8},{1,9},{2,10},{3,11},{4,12},{5,13},{6,14},{7,15},{8,0},{9,1},... | collective-permute-start | bytes 1572872 | tf_op jit(solution)/shard_map/ppermute | solution.py:37
  38.5 6.0 %collective-permute-start.10 = (f32[8,128,128]{2,1,0:T(8,128)S(1)}, f32[8,128,128]{2,1,0:T(8,128)S(1)}, u32[]{:S(2)}, u32[]{:S(2)}) collective-permute-start(f32[8,128,128]{2,1,0:T(8,128)S(1)} %collective-permute-done.8.refs_0_), channel_id=1, source_target_pairs={{0,8},{1,9},{2,10},{3,11},{4,12},{5,13},{6,14},{7,15},{8,0},{9,1},... | collective-permute-start | bytes 1572872 | tf_op jit(solution)/shard_map/ppermute | solution.py:37
  50.4 3.7 %collective-permute-start = (s32[1,64]{1,0:T(1,128)S(1)}, s32[1,64]{1,0:T(1,128)S(1)}, u32[]{:S(2)}, u32[]{:S(2)}) collective-permute-start(s32[1,64]{1,0:T(1,128)S(1)} %fusion.3), channel_id=1, source_target_pairs={{0,0},{1,1},{2,2},{3,3},{4,4},{5,5},{6,6},{7,7},{8,136},{9,137},{1... | collective-permute-start | bytes 776 | tf_op jit(solution)/shard_map/ppermute | solution.py:37
  55.0 6.6 %collective-permute-start.1 = (s32[1,64]{1,0:T(1,128)S(1)}, s32[1,64]{1,0:T(1,128)S(1)}, u32[]{:S(2)}, u32[]{:S(2)}) collective-permute-start(s32[1,64]{1,0:T(1,128)S(1)} %collective-permute-done), channel_id=1, source_target_pairs={{0,8},{1,9},{2,10},{3,11},{4,12},{5,13},{6,14},{7,15},{8,0},{9,1},... | collective-permute-start | bytes 776 | tf_op jit(solution)/shard_map/ppermute | solution.py:37
  64.6 3.6 %collective-permute-done.2 = s32[2,64]{1,0:T(2,128)S(1)} collective-permute-done((s32[2,64]{1,0:T(2,128)S(1)}, s32[2,64]{1,0:T(2,128)S(1)}, u32[]{:S(2)}, u32[]{:S(2)}) %collective-permute-start.2) | collective-permute-done | bytes 544 | tf_op jit(solution)/shard_map/ppermute | solution.py:37
  68.3 3.4 %collective-permute-start.14 = (f32[8,128,128]{2,1,0:T(8,128)S(1)}, f32[8,128,128]{2,1,0:T(8,128)S(1)}, u32[]{:S(2)}, u32[]{:S(2)}) collective-permute-start(f32[8,128,128]{2,1,0:T(8,128)S(1)} %collective-permute-done.12.refs_0_), channel_id=1, source_target_pairs={{0,8},{1,9},{2,10},{3,11},{4,12},{5,13},{6,14},{7,15},{8,0},{9,1},... | collective-permute-start | bytes 1572872 | tf_op jit(solution)/shard_map/ppermute | solution.py:37
  73.6 2.8 %collective-permute-start.16 = (f32[8,128,128]{2,1,0:T(8,128)S(1)}, f32[8,128,128]{2,1,0:T(8,128)S(1)}, u32[]{:S(2)}, u32[]{:S(2)}) collective-permute-start(f32[8,128,128]{2,1,0:T(8,128)S(1)} %collective-permute-done.12.refs_0_), channel_id=1, source_target_pairs={{0,480},{1,481},{2,482},{3,483},{4,484},{5,485},{6,486},{7,487},{8... | collective-permute-start | bytes 1572872 | tf_op jit(solution)/shard_map/ppermute | solution.py:37
  80.3 4.5 %collective-permute-done.16.refs_8_ = f32[8,128,128]{2,1,0:T(8,128)S(1)} collective-permute-done((f32[8,128,128]{2,1,0:T(8,128)S(1)}, f32[8,128,128]{2,1,0:T(8,128)S(1)}, u32[]{:S(2)}, u32[]{:S(2)}) %collective-permute-start.16) | collective-permute-done | bytes 524320 | tf_op jit(solution)/shard_map/ppermute | solution.py:37
  87.2 3.2 %collective-permute-done.17.refs_9_ = f32[8,128,128]{2,1,0:T(8,128)S(1)} collective-permute-done((f32[8,128,128]{2,1,0:T(8,128)S(1)}, f32[8,128,128]{2,1,0:T(8,128)S(1)}, u32[]{:S(2)}, u32[]{:S(2)}) %collective-permute-start.17) | collective-permute-done | bytes 524320 | tf_op jit(solution)/shard_map/ppermute | solution.py:37
  94.3 9.8 %products_1.1 = (f32[16,128,128]{2,1,0:T(8,128)S(1)}, f32[16,128,128]{2,1,0:T(8,128)S(1)}, f32[16,128,128]{2,1,0:T(8,128)S(1)}, f32[16,128,128]{2,1,0:T(8,128)S(1)}) custom-call(s32[2]{0:T(128)S(1)} %pad_add_fusion.2.where_ref, s32[4,64]{1,0:T(4,128)S(1)} %pad_add_fusion.codes_ref, bf16[1,512,512]{2,1,0:T(8,128)(2,1)S(1)} %get-tuple-element.31.refs_0_, ...), custom_call_target="tpu_custom_call" | custom-call | tf_op jit(solution)/shard_map/products_1/pallas_call | solution.py:200
  106.0 4.2 %collective-permute-start.24 = (f32[16,128,128]{2,1,0:T(8,128)S(1)}, f32[16,128,128]{2,1,0:T(8,128)S(1)}, u32[]{:S(2)}, u32[]{:S(2)}) collective-permute-start(f32[16,128,128]{2,1,0:T(8,128)S(1)} %get-tuple-element.52), channel_id=1, source_target_pairs={{0,2},{1,3},{2,0},{3,1},{4,6},{5,7},{6,4},{7,5},{8,24},{9,25},{10,... | collective-permute-start | bytes 3145736 | tf_op jit(solution)/shard_map/ppermute | solution.py:37
  112.4 9.7 %products_0.1 = (f32[16,128,128]{2,1,0:T(8,128)S(1)}, f32[16,128,128]{2,1,0:T(8,128)S(1)}, f32[16,128,128]{2,1,0:T(8,128)S(1)}, f32[16,128,128]{2,1,0:T(8,128)S(1)}) custom-call(s32[2]{0:T(128)S(1)} %pad_add_fusion.2.where_ref, s32[4,64]{1,0:T(4,128)S(1)} %pad_add_fusion.codes_ref, bf16[1,512,512]{2,1,0:T(8,128)(2,1)S(1)} %get-tuple-element.31.refs_0_, ...), custom_call_target="tpu_custom_call" | custom-call | tf_op jit(solution)/shard_map/products_0/pallas_call | solution.py:200
  122.0 4.6 %collective-permute-start.20 = (f32[16,128,128]{2,1,0:T(8,128)S(1)}, f32[16,128,128]{2,1,0:T(8,128)S(1)}, u32[]{:S(2)}, u32[]{:S(2)}) collective-permute-start(f32[16,128,128]{2,1,0:T(8,128)S(1)} %get-tuple-element.48), channel_id=1, source_target_pairs={{0,1},{1,2},{2,3},{3,0},{4,5},{5,6},{6,7},{7,4},{8,12},{9,13},{10,... | collective-permute-start | bytes 3145736 | tf_op jit(solution)/shard_map/ppermute | solution.py:37
  128.6 5.0 %collective-permute-start.22 = (f32[16,128,128]{2,1,0:T(8,128)S(1)}, f32[16,128,128]{2,1,0:T(8,128)S(1)}, u32[]{:S(2)}, u32[]{:S(2)}) collective-permute-start(f32[16,128,128]{2,1,0:T(8,128)S(1)} %get-tuple-element.50), channel_id=1, source_target_pairs={{0,3},{1,0},{2,1},{3,2},{4,7},{5,4},{6,5},{7,6},{8,28},{9,29},{10,... | collective-permute-start | bytes 3145736 | tf_op jit(solution)/shard_map/ppermute | solution.py:37
  134.5 4.2 %collective-permute-start.26 = (f32[4,128,128]{2,1,0:T(8,128)S(1)}, f32[4,128,128]{2,1,0:T(8,128)S(1)}, u32[]{:S(2)}, u32[]{:S(2)}) collective-permute-start(f32[4,128,128]{2,1,0:T(8,128)S(1)} %get-tuple-element.64), channel_id=1, source_target_pairs={{0,16},{1,17},{2,18},{3,19},{4,20},{5,21},{6,22},{7,23},{8,10},{9,... | collective-permute-start | bytes 786440 | tf_op jit(solution)/shard_map/ppermute | solution.py:37
  143.4 3.0 %collective-permute-start.28 = (f32[4,128,128]{2,1,0:T(8,128)S(1)}, f32[4,128,128]{2,1,0:T(8,128)S(1)}, u32[]{:S(2)}, u32[]{:S(2)}) collective-permute-start(f32[4,128,128]{2,1,0:T(8,128)S(1)} %get-tuple-element.62), channel_id=1, source_target_pairs={{0,20},{1,21},{2,22},{3,23},{4,0},{5,1},{6,2},{7,3},{8,11},{9,8},{... | collective-permute-start | bytes 786440 | tf_op jit(solution)/shard_map/ppermute | solution.py:37
  147.6 14.8 %collective-permute-done.22 = f32[16,128,128]{2,1,0:T(8,128)S(1)} collective-permute-done((f32[16,128,128]{2,1,0:T(8,128)S(1)}, f32[16,128,128]{2,1,0:T(8,128)S(1)}, u32[]{:S(2)}, u32[]{:S(2)}) %collective-permute-start.22) | collective-permute-done | bytes 1048608 | tf_op jit(solution)/shard_map/ppermute | solution.py:37
  162.6 4.2 %collective-permute-start.29 = (f32[4,128,128]{2,1,0:T(8,128)S(1)}, f32[4,128,128]{2,1,0:T(8,128)S(1)}, u32[]{:S(2)}, u32[]{:S(2)}) collective-permute-start(f32[4,128,128]{2,1,0:T(8,128)S(1)} %get-tuple-element.59), channel_id=1, source_target_pairs={{0,16},{1,17},{2,18},{3,19},{4,20},{5,21},{6,22},{7,23},{8,10},{9,... | collective-permute-start | bytes 786440 | tf_op jit(solution)/shard_map/ppermute | solution.py:37
  168.8 3.4 %collective-permute-start.31 = (f32[4,128,128]{2,1,0:T(8,128)S(1)}, f32[4,128,128]{2,1,0:T(8,128)S(1)}, u32[]{:S(2)}, u32[]{:S(2)}) collective-permute-start(f32[4,128,128]{2,1,0:T(8,128)S(1)} %get-tuple-element.60), channel_id=1, source_target_pairs={{0,20},{1,21},{2,22},{3,23},{4,0},{5,1},{6,2},{7,3},{8,11},{9,8},{... | collective-permute-start | bytes 786440 | tf_op jit(solution)/shard_map/ppermute | solution.py:37
  173.0 10.9 %collective-permute-start.35 = (f32[4,128,128]{2,1,0:T(8,128)S(1)}, f32[4,128,128]{2,1,0:T(8,128)S(1)}, u32[]{:S(2)}, u32[]{:S(2)}) collective-permute-start(f32[4,128,128]{2,1,0:T(8,128)S(1)} %fusion.2), channel_id=1, source_target_pairs={{0,392},{1,393},{2,394},{3,395},{4,396},{5,397},{6,398},{7,399},{2... | collective-permute-start | bytes 786440 | tf_op jit(solution)/shard_map/ppermute | solution.py:37
  190.6 19.1 %collective-permute-done.32 = f32[4,128,128]{2,1,0:T(8,128)S(1)} collective-permute-done((f32[4,128,128]{2,1,0:T(8,128)S(1)}, f32[4,128,128]{2,1,0:T(8,128)S(1)}, u32[]{:S(2)}, u32[]{:S(2)}) %collective-permute-start.32) | collective-permute-done | bytes 262176 | tf_op jit(solution)/shard_map/ppermute | solution.py:37
  (73 shorter events, 62.0 us)
Async XLA Ops:
  4.5 17.9 %collective-permute-start.4 = (f32[8,128,128]{2,1,0:T(8,128)}, f32[8,128,128]{2,1,0:T(8,128)S(1)}, u32[]{:S(2)}, u32[]{:S(2)}) collective-permute-start(f32[8,128,128]{2,1,0:T(8,128)} %sort_blocks.1.refs_0_), channel_id=1, source_target_pairs={{0,480},{1,481},{2,482},{3,483},{4,484},{5,485},{6,486},{7,487},{8... | collective-permute-start | bytes 1572872 | tf_op jit(solution)/shard_map/ppermute | solution.py:37
  8.1 19.9 %collective-permute-start.5 = (f32[8,128,128]{2,1,0:T(8,128)S(1)}, f32[8,128,128]{2,1,0:T(8,128)S(1)}, u32[]{:S(2)}, u32[]{:S(2)}) collective-permute-start(f32[8,128,128]{2,1,0:T(8,128)S(1)} %collective-permute-done.3.refs_1_), channel_id=1, source_target_pairs={{0,480},{1,481},{2,482},{3,483},{4,484},{5,485},{6,486},{7,487},{8... | collective-permute-start | bytes 1572872 | tf_op jit(solution)/shard_map/ppermute | solution.py:37
  28.0 16.5 %collective-permute-start.7 = (f32[8,128,128]{2,1,0:T(8,128)S(1)}, f32[8,128,128]{2,1,0:T(8,128)S(1)}, u32[]{:S(2)}, u32[]{:S(2)}) collective-permute-start(f32[8,128,128]{2,1,0:T(8,128)S(1)} %collective-permute-done.5.refs_1_), channel_id=1, source_target_pairs={{0,8},{1,9},{2,10},{3,11},{4,12},{5,13},{6,14},{7,15},{8,0},{9,1},... | collective-permute-start | bytes 1572872 | tf_op jit(solution)/shard_map/ppermute | solution.py:37
  32.3 13.2 %collective-permute-start.9 = (f32[8,128,128]{2,1,0:T(8,128)S(1)}, f32[8,128,128]{2,1,0:T(8,128)S(1)}, u32[]{:S(2)}, u32[]{:S(2)}) collective-permute-start(f32[8,128,128]{2,1,0:T(8,128)S(1)} %collective-permute-done.5.refs_1_), channel_id=1, source_target_pairs={{0,480},{1,481},{2,482},{3,483},{4,484},{5,485},{6,486},{7,487},{8... | collective-permute-start | bytes 1572872 | tf_op jit(solution)/shard_map/ppermute | solution.py:37
  36.6 31.7 %collective-permute-start.12 = (f32[8,128,128]{2,1,0:T(8,128)S(1)}, f32[8,128,128]{2,1,0:T(8,128)S(1)}, u32[]{:S(2)}, u32[]{:S(2)}) collective-permute-start(f32[8,128,128]{2,1,0:T(8,128)S(1)} %collective-permute-done.8.refs_0_), channel_id=1, source_target_pairs={{0,480},{1,481},{2,482},{3,483},{4,484},{5,485},{6,486},{7,487},{8... | collective-permute-start | bytes 1572872 | tf_op jit(solution)/shard_map/ppermute | solution.py:37
  38.5 29.7 %collective-permute-start.10 = (f32[8,128,128]{2,1,0:T(8,128)S(1)}, f32[8,128,128]{2,1,0:T(8,128)S(1)}, u32[]{:S(2)}, u32[]{:S(2)}) collective-permute-start(f32[8,128,128]{2,1,0:T(8,128)S(1)} %collective-permute-done.8.refs_0_), channel_id=1, source_target_pairs={{0,8},{1,9},{2,10},{3,11},{4,12},{5,13},{6,14},{7,15},{8,0},{9,1},... | collective-permute-start | bytes 1572872 | tf_op jit(solution)/shard_map/ppermute | solution.py:37
  45.4 26.2 %collective-permute-start.13 = (f32[8,128,128]{2,1,0:T(8,128)S(1)}, f32[8,128,128]{2,1,0:T(8,128)S(1)}, u32[]{:S(2)}, u32[]{:S(2)}) collective-permute-start(f32[8,128,128]{2,1,0:T(8,128)S(1)} %collective-permute-done.9.refs_1_), channel_id=1, source_target_pairs={{0,480},{1,481},{2,482},{3,483},{4,484},{5,485},{6,486},{7,487},{8... | collective-permute-start | bytes 1572872 | tf_op jit(solution)/shard_map/ppermute | solution.py:37
  47.4 29.0 %collective-permute-start.11 = (f32[8,128,128]{2,1,0:T(8,128)S(1)}, f32[8,128,128]{2,1,0:T(8,128)S(1)}, u32[]{:S(2)}, u32[]{:S(2)}) collective-permute-start(f32[8,128,128]{2,1,0:T(8,128)S(1)} %collective-permute-done.9.refs_1_), channel_id=1, source_target_pairs={{0,8},{1,9},{2,10},{3,11},{4,12},{5,13},{6,14},{7,15},{8,0},{9,1},... | collective-permute-start | bytes 1572872 | tf_op jit(solution)/shard_map/ppermute | solution.py:37
  104.1 24.5 %collective-permute-start.23 = (f32[16,128,128]{2,1,0:T(8,128)S(1)}, f32[16,128,128]{2,1,0:T(8,128)S(1)}, u32[]{:S(2)}, u32[]{:S(2)}) collective-permute-start(f32[16,128,128]{2,1,0:T(8,128)S(1)} %get-tuple-element.51), channel_id=1, source_target_pairs={{0,1},{1,2},{2,3},{3,0},{4,5},{5,6},{6,7},{7,4},{8,12},{9,13},{10,... | collective-permute-start | bytes 3145736 | tf_op jit(solution)/shard_map/ppermute | solution.py:37
  106.0 27.6 %collective-permute-start.24 = (f32[16,128,128]{2,1,0:T(8,128)S(1)}, f32[16,128,128]{2,1,0:T(8,128)S(1)}, u32[]{:S(2)}, u32[]{:S(2)}) collective-permute-start(f32[16,128,128]{2,1,0:T(8,128)S(1)} %get-tuple-element.52), channel_id=1, source_target_pairs={{0,2},{1,3},{2,0},{3,1},{4,6},{5,7},{6,4},{7,5},{8,24},{9,25},{10,... | collective-permute-start | bytes 3145736 | tf_op jit(solution)/shard_map/ppermute | solution.py:37
  110.3 24.1 %collective-permute-start.25 = (f32[16,128,128]{2,1,0:T(8,128)S(1)}, f32[16,128,128]{2,1,0:T(8,128)S(1)}, u32[]{:S(2)}, u32[]{:S(2)}) collective-permute-start(f32[16,128,128]{2,1,0:T(8,128)S(1)} %get-tuple-element.53), channel_id=1, source_target_pairs={{0,3},{1,0},{2,1},{3,2},{4,7},{5,4},{6,5},{7,6},{8,28},{9,29},{10,... | collective-permute-start | bytes 3145736 | tf_op jit(solution)/shard_map/ppermute | solution.py:37
  122.0 21.3 %collective-permute-start.20 = (f32[16,128,128]{2,1,0:T(8,128)S(1)}, f32[16,128,128]{2,1,0:T(8,128)S(1)}, u32[]{:S(2)}, u32[]{:S(2)}) collective-permute-start(f32[16,128,128]{2,1,0:T(8,128)S(1)} %get-tuple-element.48), channel_id=1, source_target_pairs={{0,1},{1,2},{2,3},{3,0},{4,5},{5,6},{6,7},{7,4},{8,12},{9,13},{10,... | collective-permute-start | bytes 3145736 | tf_op jit(solution)/shard_map/ppermute | solution.py:37
  126.6 21.0 %collective-permute-start.21 = (f32[16,128,128]{2,1,0:T(8,128)S(1)}, f32[16,128,128]{2,1,0:T(8,128)S(1)}, u32[]{:S(2)}, u32[]{:S(2)}) collective-permute-start(f32[16,128,128]{2,1,0:T(8,128)S(1)} %get-tuple-element.49), channel_id=1, source_target_pairs={{0,2},{1,3},{2,0},{3,1},{4,6},{5,7},{6,4},{7,5},{8,24},{9,25},{10,... | collective-permute-start | bytes 3145736 | tf_op jit(solution)/shard_map/ppermute | solution.py:37
  128.6 33.8 %collective-permute-start.22 = (f32[16,128,128]{2,1,0:T(8,128)S(1)}, f32[16,128,128]{2,1,0:T(8,128)S(1)}, u32[]{:S(2)}, u32[]{:S(2)}) collective-permute-start(f32[16,128,128]{2,1,0:T(8,128)S(1)} %get-tuple-element.50), channel_id=1, source_target_pairs={{0,3},{1,0},{2,1},{3,2},{4,7},{5,4},{6,5},{7,6},{8,28},{9,29},{10,... | collective-permute-start | bytes 3145736 | tf_op jit(solution)/shard_map/ppermute | solution.py:37
  134.5 27.9 %collective-permute-start.26 = (f32[4,128,128]{2,1,0:T(8,128)S(1)}, f32[4,128,128]{2,1,0:T(8,128)S(1)}, u32[]{:S(2)}, u32[]{:S(2)}) collective-permute-start(f32[4,128,128]{2,1,0:T(8,128)S(1)} %get-tuple-element.64), channel_id=1, source_target_pairs={{0,16},{1,17},{2,18},{3,19},{4,20},{5,21},{6,22},{7,23},{8,10},{9,... | collective-permute-start | bytes 786440 | tf_op jit(solution)/shard_map/ppermute | solution.py:37
  138.7 23.7 %collective-permute-start.27 = (f32[4,128,128]{2,1,0:T(8,128)S(1)}, f32[4,128,128]{2,1,0:T(8,128)S(1)}, u32[]{:S(2)}, u32[]{:S(2)}) collective-permute-start(f32[4,128,128]{2,1,0:T(8,128)S(1)} %get-tuple-element.63), channel_id=1, source_target_pairs={{0,4},{1,5},{2,6},{3,7},{4,16},{5,17},{6,18},{7,19},{8,9},{9,10},{... | collective-permute-start | bytes 786440 | tf_op jit(solution)/shard_map/ppermute | solution.py:37
  143.4 19.0 %collective-permute-start.28 = (f32[4,128,128]{2,1,0:T(8,128)S(1)}, f32[4,128,128]{2,1,0:T(8,128)S(1)}, u32[]{:S(2)}, u32[]{:S(2)}) collective-permute-start(f32[4,128,128]{2,1,0:T(8,128)S(1)} %get-tuple-element.62), channel_id=1, source_target_pairs={{0,20},{1,21},{2,22},{3,23},{4,0},{5,1},{6,2},{7,3},{8,11},{9,8},{... | collective-permute-start | bytes 786440 | tf_op jit(solution)/shard_map/ppermute | solution.py:37
  162.6 21.3 %collective-permute-start.29 = (f32[4,128,128]{2,1,0:T(8,128)S(1)}, f32[4,128,128]{2,1,0:T(8,128)S(1)}, u32[]{:S(2)}, u32[]{:S(2)}) collective-permute-start(f32[4,128,128]{2,1,0:T(8,128)S(1)} %get-tuple-element.59), channel_id=1, source_target_pairs={{0,16},{1,17},{2,18},{3,19},{4,20},{5,21},{6,22},{7,23},{8,10},{9,... | collective-permute-start | bytes 786440 | tf_op jit(solution)/shard_map/ppermute | solution.py:37
  166.9 17.1 %collective-permute-start.30 = (f32[4,128,128]{2,1,0:T(8,128)S(1)}, f32[4,128,128]{2,1,0:T(8,128)S(1)}, u32[]{:S(2)}, u32[]{:S(2)}) collective-permute-start(f32[4,128,128]{2,1,0:T(8,128)S(1)} %get-tuple-element.61), channel_id=1, source_target_pairs={{0,4},{1,5},{2,6},{3,7},{4,16},{5,17},{6,18},{7,19},{8,9},{9,10},{... | collective-permute-start | bytes 786440 | tf_op jit(solution)/shard_map/ppermute | solution.py:37
  168.8 15.2 %collective-permute-start.31 = (f32[4,128,128]{2,1,0:T(8,128)S(1)}, f32[4,128,128]{2,1,0:T(8,128)S(1)}, u32[]{:S(2)}, u32[]{:S(2)}) collective-permute-start(f32[4,128,128]{2,1,0:T(8,128)S(1)} %get-tuple-element.60), channel_id=1, source_target_pairs={{0,20},{1,21},{2,22},{3,23},{4,0},{5,1},{6,2},{7,3},{8,11},{9,8},{... | collective-permute-start | bytes 786440 | tf_op jit(solution)/shard_map/ppermute | solution.py:37
  172.3 15.6 %collective-permute-start.33 = (f32[4,128,128]{2,1,0:T(8,128)S(1)}, f32[4,128,128]{2,1,0:T(8,128)S(1)}, u32[]{:S(2)}, u32[]{:S(2)}) collective-permute-start(f32[4,128,128]{2,1,0:T(8,128)S(1)} %fusion.2), channel_id=1, source_target_pairs={{8,392},{9,393},{10,394},{11,395},{12,396},{13,397},{14,398},{15,3... | collective-permute-start | bytes 786440 | tf_op jit(solution)/shard_map/ppermute | solution.py:37
  173.0 17.6 %collective-permute-start.35 = (f32[4,128,128]{2,1,0:T(8,128)S(1)}, f32[4,128,128]{2,1,0:T(8,128)S(1)}, u32[]{:S(2)}, u32[]{:S(2)}) collective-permute-start(f32[4,128,128]{2,1,0:T(8,128)S(1)} %fusion.2), channel_id=1, source_target_pairs={{0,392},{1,393},{2,394},{3,395},{4,396},{5,397},{6,398},{7,399},{2... | collective-permute-start | bytes 786440 | tf_op jit(solution)/shard_map/ppermute | solution.py:37
  184.1 25.6 %collective-permute-start.32 = (f32[4,128,128]{2,1,0:T(8,128)S(1)}, f32[4,128,128]{2,1,0:T(8,128)S(1)}, u32[]{:S(2)}, u32[]{:S(2)}) collective-permute-start(f32[4,128,128]{2,1,0:T(8,128)S(1)} %add_add_fusion), channel_id=1, source_target_pairs={{0,0},{1,1},{2,2},{3,3},{4,4},{5,5},{6,6},{7,7},{24,56},{25,57},{2... | collective-permute-start | bytes 786440 | tf_op jit(solution)/shard_map/ppermute | solution.py:37
  186.6 23.1 %collective-permute-start.34 = (f32[4,128,128]{2,1,0:T(8,128)S(1)}, f32[4,128,128]{2,1,0:T(8,128)S(1)}, u32[]{:S(2)}, u32[]{:S(2)}) collective-permute-start(f32[4,128,128]{2,1,0:T(8,128)S(1)} %add_add_fusion), channel_id=1, source_target_pairs={{8,0},{9,1},{10,2},{11,3},{12,4},{13,5},{14,6},{15,7},{16,56},{17,... | collective-permute-start | bytes 786440 | tf_op jit(solution)/shard_map/ppermute | solution.py:37
  (14 other events, 119.6 us)

commit v5 on v4

--- a/solution.py
+++ b/solution.py
@@ -11,8 +11,8 @@
 NB = 1536
 NZ = 16
 AXES = ("z", "xhi", "core", "xlo", "y")
-LEFT = (0, -4, 4, 1)
-RIGHT = (0, 0, -4, -3)
+LEFT = (0, -4, 4, 0)
+RIGHT = (0, 0, -4, -4)
 
 
 def flat(z, xhi, core, xlo, y):
@@ -92,7 +92,7 @@
     )(block_ids.T, blocks)
 
 
-NEAR = 3
+REACH = 4
 
 
 def split_into(panel, at, quarter, hi_ref, lo_ref):
@@ -140,17 +140,10 @@
     core = where_ref[0]
     place = where_ref[1]
     xhi = place // 8
-    rows_hi, rows_lo = list(refs[: 2 * NEAR + 2 : 2]), list(refs[1 : 2 * NEAR + 2 : 2])
-    refs = refs[2 * NEAR + 2 :]
-    if chunk == 1:
-        panels, outs = refs[:4], refs[4:8]
-        res_ref, far_hi, far_lo = refs[8:]
-        split_pair(core, panels, far_hi, far_lo)
-        rows_hi.append(far_hi)
-        rows_lo.append(far_lo)
-    else:
-        outs = refs[:4]
-        [res_ref] = refs[4:]
+    count = 2 * REACH + 2
+    rows_hi, rows_lo = refs[:count:2], refs[1:count:2]
+    outs = refs[count : count + 4]
+    [res_ref] = refs[count + 4 :]
 
     def row(offset):
         at = int(offset > 0)
@@ -191,21 +184,18 @@
         lax.fori_loop(0, 16, pick, 0, unroll=4)
 
 
-def chunk_products(chunk, where, codes, split, panels):
+def chunk_products(chunk, where, codes, split):
     vmem = pl.BlockSpec(memory_space=pltpu.VMEM)
     smem = pl.BlockSpec(memory_space=pltpu.SMEM)
-    scratch = [pltpu.VMEM((8, 512, 512), jnp.float32)]
-    if chunk == 1:
-        scratch += [pltpu.VMEM((2, 512, 512), jnp.bfloat16)] * 2
     return pl.pallas_call(
         functools.partial(chunk_kernel, chunk),
         out_shape=[jax.ShapeDtypeStruct((16, 128, 128), jnp.float32)] * 4,
-        in_specs=[smem] * 2 + [vmem] * (len(split) + len(panels)),
+        in_specs=[smem] * 2 + [vmem] * len(split),
         out_specs=[vmem] * 4,
-        scratch_shapes=scratch,
+        scratch_shapes=[pltpu.VMEM((8, 512, 512), jnp.float32)],
         compiler_params=pltpu.CompilerParams(vmem_limit_bytes=20 << 20),
         name=f"products_{chunk}",
-    )(where, codes, *split, *panels)
+    )(where, codes, *split)
 
 
 def slot_codes(out_ids, row, col):
@@ -228,23 +218,25 @@
     return lax.optimization_barrier((value, *others))[0]
 
 
-def reduce_plane(pieces, others=()):
+def reduce_plane(pieces, others=(), late=()):
     received = [None] * 4
     for offset in (2, 1, 3):
         received[offset] = send(pieces[offset], plane_step(0, offset))
     if others:
-        received[1:] = lax.optimization_barrier((*received[1:], *others))[:3]
+        received[1:] = lax.optimization_barrier((*others, *received[1:]))[-3:]
     count = pieces[0].shape[0] // 4
     total = [
         sum((received[o][n * count : (n + 1) * count] for o in (1, 2, 3)), pieces[0][n * count : (n + 1) * count])
         for n in range(4)
     ]
     arrived = [send(total[offset], plane_step(1, offset)) for offset in (2, 1, 3)]
+    if late:
+        arrived = lax.optimization_barrier((*late, *arrived))[-3:]
     return total[0] + arrived[0] + arrived[1] + arrived[2], arrived
 
 
-def bring_home(chunk, part):
-    return send(part, home(chunk, True)), send(part, home(chunk, False))
+def bring_home(part):
+    return send(part, home(1, True)), send(part, home(1, False))
 
 
 def to_place(z, xhi, core, xlo, y):
@@ -262,7 +254,10 @@
     x = xhi * 2 + lax.axis_index("xlo")
     where = jnp.stack([core, x * 4 + lax.axis_index("y")]).astype(jnp.int32)
 
-    codes = send(slot_codes(out_ids, z, xhi * 2 + core)[None], to_place)
+    placed = send(out_ids, to_place)
+    col = xhi * 2 + core
+    left = jnp.where(col == 1, LEFT[1], jnp.where(col == 2, LEFT[2], LEFT[0]))
+    codes = slot_codes(placed, z + left, col)[None]
     codes = jnp.concatenate([codes, send(codes, other_core)], axis=0)
     codes = jnp.concatenate([codes, send(codes, other_xhi)], axis=0)
 
@@ -270,32 +265,30 @@
     mine_b = [send(mine_a[0], other_core)]
     split = [split_rows(where, mine_a[0], mine_b[0])]
     their_a, their_b = [None], [None]
-    for k in range(1, 5):
+    for k in range(1, REACH + 1):
         next_a, next_b = mine_a[-1], mine_b[-1]
+        if k == 1:
+            next_a = after(next_a, placed)
         if k > 2:
             next_a = after(next_a, their_a[k - 2])
             next_b = after(next_b, split[k - 2][0])
-        if k == 4:
-            next_a = after(next_a, codes)
         mine_a.append(send(next_a, ring_z))
         mine_b.append(send(next_b, ring_z))
-        swap_a = mine_a[k] if k <= NEAR else after(mine_a[k], split[k - 1][0])
+        swap_a = mine_a[k] if k < REACH else after(mine_a[k], split[k - 1][0], codes)
         their_a.append(send(swap_a, other_core))
         their_b.append(send(mine_b[k], other_core))
-        if k <= NEAR:
-            split.append(split_rows(where, mine_a[k], mine_b[k], their_a[k], their_b[k]))
+        split.append(split_rows(where, mine_a[k], mine_b[k], their_a[k], their_b[k]))
     split = [part for pair in split for part in pair]
 
-    pieces = chunk_products(
-        1, where, codes, split, [mine_a[4], mine_b[4], their_a[4], their_b[4]]
-    )
+    pieces = chunk_products(1, where, codes, split)
     wide, arrived = reduce_plane(pieces)
-    far_home = bring_home(1, wide)
-    pieces = chunk_products(0, where, after(codes, pieces[0]), split, [])
-    near, _ = reduce_plane(pieces, arrived)
-    near_home = bring_home(0, near)
-
-    same, cross = [jnp.where(core == xhi, a, b) for a, b in zip(near_home, far_home)]
+    far_same, far_cross = bring_home(wide)
+    pieces = chunk_products(0, where, after(codes, pieces[0]), split)
+    near, _ = reduce_plane(pieces, [wide], (far_same, far_cross))
+    near_cross = send(near, home(0, False))
+
+    same = jnp.where(core == xhi, near, far_same)
+    cross = jnp.where(core == xhi, near_cross, far_cross)
     first = jnp.where(core == 0, same, cross)
     second = jnp.where(core == 0, cross, same)
     return jnp.concatenate([first, second], axis=0)

time: 212 us -> 198 us (0.934)
  the two profiles are of different devices: /device:TPU:15 before, /device:TPU:1 now
where the time goes in v5:
time: 198 us; the launch traced here: 197 us
  starting transfers between devices  112 us (57%)
  waiting for transfers between devices  56.3 us (28%)
  Pallas kernels  25.4 us (13%)
    ppermute x35, starting transfers between devices, send(): return lax.ppermute(value, AXES, pairs)  112 us
    ppermute x35, waiting for transfers between devices, send(): return lax.ppermute(value, AXES, pairs)  56.3 us
    pallas_call x2, Pallas kernels, chunk_products(): pl.pallas_call(functools.partial(chunk_kernel, chunk), out_shape=[jax.Sha...  19.3 us
    pallas_call x5, Pallas kernels, split_rows(): pl.pallas_call(split_kernel, out_shape=[jax.ShapeDtypeStruct((len(panels)...  4.24 us
  transfers between devices with their start and end apart: 35, of which 14 were waited for; matrix products, arithmetic and copies ran while one was open for 0% of the time, Pallas kernels for 7%

profile of v5, /device:TPU:1, one launch (start us, length us, event | category | flops | bytes accessed | tf_op | source)
XLA Modules:
  0.0 197.4 jit_solution(1028589783455486191)
XLA Ops:
  1.9 8.8 %collective-permute-start.3 = (f32[8,128,128]{2,1,0:T(8,128)}, f32[8,128,128]{2,1,0:T(8,128)S(1)}, u32[]{:S(2)}, u32[]{:S(2)}) collective-permute-start(f32[8,128,128]{2,1,0:T(8,128)} %sort_blocks.1.refs_0_), channel_id=1, source_target_pairs={{0,8},{1,9},{2,10},{3,11},{4,12},{5,13},{6,14},{7,15},{8,0},{9,1},... | collective-permute-start | bytes 1572872 | tf_op jit(solution)/shard_map/ppermute | solution.py:37
  10.7 3.4 %collective-permute-start = (s32[64,2]{0,1:T(2,128)S(1)}, s32[64,2]{0,1:T(2,128)S(1)}, u32[]{:S(2)}, u32[]{:S(2)}) collective-permute-start(s32[64,2]{0,1:T(2,128)S(1)} %copy-done.3), channel_id=1, source_target_pairs={{0,0},{1,1},{2,2},{3,3},{4,4},{5,5},{6,6},{7,7},{8,136},{9,137},{1... | collective-permute-start | bytes 1544 | tf_op jit(solution)/shard_map/ppermute | solution.py:37
  14.2 4.8 %collective-permute-done = s32[64,2]{0,1:T(2,128)S(1)} collective-permute-done((s32[64,2]{0,1:T(2,128)S(1)}, s32[64,2]{0,1:T(2,128)S(1)}, u32[]{:S(2)}, u32[]{:S(2)}) %collective-permute-start) | collective-permute-done | bytes 544 | tf_op jit(solution)/shard_map/ppermute | solution.py:37
  24.9 6.6 %collective-permute-done.4.refs_0_ = f32[8,128,128]{2,1,0:T(8,128)S(1)} collective-permute-done((f32[8,128,128]{2,1,0:T(8,128)}, f32[8,128,128]{2,1,0:T(8,128)S(1)}, u32[]{:S(2)}, u32[]{:S(2)}) %collective-permute-start.4) | collective-permute-done | bytes 524320 | tf_op jit(solution)/shard_map/ppermute | solution.py:37
  46.4 5.3 %collective-permute-start.10 = (f32[8,128,128]{2,1,0:T(8,128)S(1)}, f32[8,128,128]{2,1,0:T(8,128)S(1)}, u32[]{:S(2)}, u32[]{:S(2)}) collective-permute-start(f32[8,128,128]{2,1,0:T(8,128)S(1)} %collective-permute-done.8.refs_0_), channel_id=1, source_target_pairs={{0,8},{1,9},{2,10},{3,11},{4,12},{5,13},{6,14},{7,15},{8,0},{9,1},... | collective-permute-start | bytes 1572872 | tf_op jit(solution)/shard_map/ppermute | solution.py:37
  60.3 3.8 %collective-permute-start.14 = (f32[8,128,128]{2,1,0:T(8,128)S(1)}, f32[8,128,128]{2,1,0:T(8,128)S(1)}, u32[]{:S(2)}, u32[]{:S(2)}) collective-permute-start(f32[8,128,128]{2,1,0:T(8,128)S(1)} %collective-permute-done.12.refs_0_), channel_id=1, source_target_pairs={{0,8},{1,9},{2,10},{3,11},{4,12},{5,13},{6,14},{7,15},{8,0},{9,1},... | collective-permute-start | bytes 1572872 | tf_op jit(solution)/shard_map/ppermute | solution.py:37
  72.9 7.6 %collective-permute-start.2 = (s32[2,64]{1,0:T(2,128)S(1)}, s32[2,64]{1,0:T(2,128)S(1)}, u32[]{:S(2)}, u32[]{:S(2)}) collective-permute-start(s32[2,64]{1,0:T(2,128)S(1)} %pad_add_fusion.1), channel_id=1, source_target_pairs={{0,16},{1,17},{2,18},{3,19},{4,20},{5,21},{6,22},{7,23},{8,24},{9,... | collective-permute-start | bytes 1544 | tf_op jit(solution)/shard_map/ppermute | solution.py:37
  90.1 9.6 %products_1.1 = (f32[16,128,128]{2,1,0:T(8,128)S(1)}, f32[16,128,128]{2,1,0:T(8,128)S(1)}, f32[16,128,128]{2,1,0:T(8,128)S(1)}, f32[16,128,128]{2,1,0:T(8,128)S(1)}) custom-call(s32[2]{0:T(128)S(1)} %pad_add_fusion.2.where_ref, s32[4,64]{1,0:T(4,128)S(1)} %pad_add_fusion.codes_ref, bf16[1,512,512]{2,1,0:T(8,128)(2,1)S(1)} %get-tuple-element.36.refs_0_, ...), custom_call_target="tpu_custom_call" | custom-call | tf_op jit(solution)/shard_map/products_1/pallas_call | solution.py:190
  99.8 4.9 %collective-permute-start.22 = (f32[16,128,128]{2,1,0:T(8,128)S(1)}, f32[16,128,128]{2,1,0:T(8,128)S(1)}, u32[]{:S(2)}, u32[]{:S(2)}) collective-permute-start(f32[16,128,128]{2,1,0:T(8,128)S(1)} %get-tuple-element.57), channel_id=1, source_target_pairs={{0,3},{1,0},{2,1},{3,2},{4,7},{5,4},{6,5},{7,6},{8,28},{9,29},{10,... | collective-permute-start | bytes 3145736 | tf_op jit(solution)/shard_map/ppermute | solution.py:37
  109.8 9.6 %products_0.1 = (f32[16,128,128]{2,1,0:T(8,128)S(1)}, f32[16,128,128]{2,1,0:T(8,128)S(1)}, f32[16,128,128]{2,1,0:T(8,128)S(1)}, f32[16,128,128]{2,1,0:T(8,128)S(1)}) custom-call(s32[2]{0:T(128)S(1)} %pad_add_fusion.2.where_ref, s32[4,64]{1,0:T(4,128)S(1)} %pad_add_fusion.codes_ref, bf16[1,512,512]{2,1,0:T(8,128)(2,1)S(1)} %get-tuple-element.36.refs_0_, ...), custom_call_target="tpu_custom_call" | custom-call | tf_op jit(solution)/shard_map/products_0/pallas_call | solution.py:190
  119.4 3.4 %collective-permute-start.26 = (f32[16,128,128]{2,1,0:T(8,128)S(1)}, f32[16,128,128]{2,1,0:T(8,128)S(1)}, u32[]{:S(2)}, u32[]{:S(2)}) collective-permute-start(f32[16,128,128]{2,1,0:T(8,128)S(1)} %get-tuple-element.58), channel_id=1, source_target_pairs={{0,1},{1,2},{2,3},{3,0},{4,5},{5,6},{6,7},{7,4},{8,12},{9,13},{10,... | collective-permute-start | bytes 3145736 | tf_op jit(solution)/shard_map/ppermute | solution.py:37
  122.9 3.4 %collective-permute-start.27 = (f32[16,128,128]{2,1,0:T(8,128)S(1)}, f32[16,128,128]{2,1,0:T(8,128)S(1)}, u32[]{:S(2)}, u32[]{:S(2)}) collective-permute-start(f32[16,128,128]{2,1,0:T(8,128)S(1)} %get-tuple-element.59), channel_id=1, source_target_pairs={{0,2},{1,3},{2,0},{3,1},{4,6},{5,7},{6,4},{7,5},{8,24},{9,25},{10,... | collective-permute-start | bytes 3145736 | tf_op jit(solution)/shard_map/ppermute | solution.py:37
  126.3 12.6 %collective-permute-done.22 = f32[16,128,128]{2,1,0:T(8,128)S(1)} collective-permute-done((f32[16,128,128]{2,1,0:T(8,128)S(1)}, f32[16,128,128]{2,1,0:T(8,128)S(1)}, u32[]{:S(2)}, u32[]{:S(2)}) %collective-permute-start.22) | collective-permute-done | bytes 1048608 | tf_op jit(solution)/shard_map/ppermute | solution.py:37
  138.8 5.3 %collective-permute-start.28 = (f32[16,128,128]{2,1,0:T(8,128)S(1)}, f32[16,128,128]{2,1,0:T(8,128)S(1)}, u32[]{:S(2)}, u32[]{:S(2)}) collective-permute-start(f32[16,128,128]{2,1,0:T(8,128)S(1)} %get-tuple-element.60), channel_id=1, source_target_pairs={{0,3},{1,0},{2,1},{3,2},{4,7},{5,4},{6,5},{7,6},{8,28},{9,29},{10,... | collective-permute-start | bytes 3145736 | tf_op jit(solution)/shard_map/ppermute | solution.py:37
  144.4 3.7 %collective-permute-start.25 = (f32[4,128,128]{2,1,0:T(8,128)S(1)}, f32[4,128,128]{2,1,0:T(8,128)S(1)}, u32[]{:S(2)}, u32[]{:S(2)}) collective-permute-start(f32[4,128,128]{2,1,0:T(8,128)S(1)} %get-tuple-element.73), channel_id=1, source_target_pairs={{0,20},{1,21},{2,22},{3,23},{4,0},{5,1},{6,2},{7,3},{8,11},{9,8},{... | collective-permute-start | bytes 786440 | tf_op jit(solution)/shard_map/ppermute | solution.py:37
  150.1 4.4 %collective-permute-done.25 = f32[4,128,128]{2,1,0:T(8,128)S(1)} collective-permute-done((f32[4,128,128]{2,1,0:T(8,128)S(1)}, f32[4,128,128]{2,1,0:T(8,128)S(1)}, u32[]{:S(2)}, u32[]{:S(2)}) %collective-permute-start.25) | collective-permute-done | bytes 262176 | tf_op jit(solution)/shard_map/ppermute | solution.py:37
  154.5 3.6 %collective-permute-start.23 = (f32[4,128,128]{2,1,0:T(8,128)S(1)}, f32[4,128,128]{2,1,0:T(8,128)S(1)}, u32[]{:S(2)}, u32[]{:S(2)}) collective-permute-start(f32[4,128,128]{2,1,0:T(8,128)S(1)} %get-tuple-element.72), channel_id=1, source_target_pairs={{0,16},{1,17},{2,18},{3,19},{4,20},{5,21},{6,22},{7,23},{8,10},{9,... | collective-permute-start | bytes 786440 | tf_op jit(solution)/shard_map/ppermute | solution.py:37
  159.9 3.2 %collective-permute-done.23 = f32[4,128,128]{2,1,0:T(8,128)S(1)} collective-permute-done((f32[4,128,128]{2,1,0:T(8,128)S(1)}, f32[4,128,128]{2,1,0:T(8,128)S(1)}, u32[]{:S(2)}, u32[]{:S(2)}) %collective-permute-start.23) | collective-permute-done | bytes 262176 | tf_op jit(solution)/shard_map/ppermute | solution.py:37
  163.2 5.2 %collective-permute-start.29 = (f32[4,128,128]{2,1,0:T(8,128)S(1)}, f32[4,128,128]{2,1,0:T(8,128)S(1)}, u32[]{:S(2)}, u32[]{:S(2)}) collective-permute-start(f32[4,128,128]{2,1,0:T(8,128)S(1)} %fusion.2), channel_id=1, source_target_pairs={{8,392},{9,393},{10,394},{11,395},{12,396},{13,397},{14,398},{15,3... | collective-permute-start | bytes 786440 | tf_op jit(solution)/shard_map/ppermute | solution.py:37
  169.9 3.6 %collective-permute-start.31 = (f32[4,128,128]{2,1,0:T(8,128)S(1)}, f32[4,128,128]{2,1,0:T(8,128)S(1)}, u32[]{:S(2)}, u32[]{:S(2)}) collective-permute-start(f32[4,128,128]{2,1,0:T(8,128)S(1)} %get-tuple-element.71), channel_id=1, source_target_pairs={{0,16},{1,17},{2,18},{3,19},{4,20},{5,21},{6,22},{7,23},{8,10},{9,... | collective-permute-start | bytes 786440 | tf_op jit(solution)/shard_map/ppermute | solution.py:37
  173.5 3.2 %collective-permute-start.32 = (f32[4,128,128]{2,1,0:T(8,128)S(1)}, f32[4,128,128]{2,1,0:T(8,128)S(1)}, u32[]{:S(2)}, u32[]{:S(2)}) collective-permute-start(f32[4,128,128]{2,1,0:T(8,128)S(1)} %get-tuple-element.70), channel_id=1, source_target_pairs={{0,4},{1,5},{2,6},{3,7},{4,16},{5,17},{6,18},{7,19},{8,9},{9,10},{... | collective-permute-start | bytes 786440 | tf_op jit(solution)/shard_map/ppermute | solution.py:37
  176.7 3.3 %collective-permute-start.33 = (f32[4,128,128]{2,1,0:T(8,128)S(1)}, f32[4,128,128]{2,1,0:T(8,128)S(1)}, u32[]{:S(2)}, u32[]{:S(2)}) collective-permute-start(f32[4,128,128]{2,1,0:T(8,128)S(1)} %get-tuple-element.69), channel_id=1, source_target_pairs={{0,20},{1,21},{2,22},{3,23},{4,0},{5,1},{6,2},{7,3},{8,11},{9,8},{... | collective-permute-start | bytes 786440 | tf_op jit(solution)/shard_map/ppermute | solution.py:37
  180.0 9.0 %collective-permute-done.29 = f32[4,128,128]{2,1,0:T(8,128)S(1)} collective-permute-done((f32[4,128,128]{2,1,0:T(8,128)S(1)}, f32[4,128,128]{2,1,0:T(8,128)S(1)}, u32[]{:S(2)}, u32[]{:S(2)}) %collective-permute-start.29) | collective-permute-done | bytes 262176 | tf_op jit(solution)/shard_map/ppermute | solution.py:37
  189.0 4.9 %collective-permute-done.30 = f32[4,128,128]{2,1,0:T(8,128)S(1)} collective-permute-done((f32[4,128,128]{2,1,0:T(8,128)S(1)}, f32[4,128,128]{2,1,0:T(8,128)S(1)}, u32[]{:S(2)}, u32[]{:S(2)}) %collective-permute-start.30) | collective-permute-done | bytes 262176 | tf_op jit(solution)/shard_map/ppermute | solution.py:37
  (76 shorter events, 63.6 us)
Async XLA Ops:
  1.9 19.5 %collective-permute-start.3 = (f32[8,128,128]{2,1,0:T(8,128)}, f32[8,128,128]{2,1,0:T(8,128)S(1)}, u32[]{:S(2)}, u32[]{:S(2)}) collective-permute-start(f32[8,128,128]{2,1,0:T(8,128)} %sort_blocks.1.refs_0_), channel_id=1, source_target_pairs={{0,8},{1,9},{2,10},{3,11},{4,12},{5,13},{6,14},{7,15},{8,0},{9,1},... | collective-permute-start | bytes 1572872 | tf_op jit(solution)/shard_map/ppermute | solution.py:37
  19.0 12.5 %collective-permute-start.4 = (f32[8,128,128]{2,1,0:T(8,128)}, f32[8,128,128]{2,1,0:T(8,128)S(1)}, u32[]{:S(2)}, u32[]{:S(2)}) collective-permute-start(f32[8,128,128]{2,1,0:T(8,128)} %sort_blocks.1.refs_0_), channel_id=1, source_target_pairs={{0,480},{1,481},{2,482},{3,483},{4,484},{5,485},{6,486},{7,487},{8... | collective-permute-start | bytes 1572872 | tf_op jit(solution)/shard_map/ppermute | solution.py:37
  21.4 15.7 %collective-permute-start.5 = (f32[8,128,128]{2,1,0:T(8,128)S(1)}, f32[8,128,128]{2,1,0:T(8,128)S(1)}, u32[]{:S(2)}, u32[]{:S(2)}) collective-permute-start(f32[8,128,128]{2,1,0:T(8,128)S(1)} %collective-permute-done.3.refs_1_), channel_id=1, source_target_pairs={{0,480},{1,481},{2,482},{3,483},{4,484},{5,485},{6,486},{7,487},{8... | collective-permute-start | bytes 1572872 | tf_op jit(solution)/shard_map/ppermute | solution.py:37
  33.4 11.1 %collective-permute-start.8 = (f32[8,128,128]{2,1,0:T(8,128)S(1)}, f32[8,128,128]{2,1,0:T(8,128)S(1)}, u32[]{:S(2)}, u32[]{:S(2)}) collective-permute-start(f32[8,128,128]{2,1,0:T(8,128)S(1)} %collective-permute-done.4.refs_0_), channel_id=1, source_target_pairs={{0,480},{1,481},{2,482},{3,483},{4,484},{5,485},{6,486},{7,487},{8... | collective-permute-start | bytes 1572872 | tf_op jit(solution)/shard_map/ppermute | solution.py:37
  37.1 14.7 %collective-permute-start.7 = (f32[8,128,128]{2,1,0:T(8,128)S(1)}, f32[8,128,128]{2,1,0:T(8,128)S(1)}, u32[]{:S(2)}, u32[]{:S(2)}) collective-permute-start(f32[8,128,128]{2,1,0:T(8,128)S(1)} %collective-permute-done.5.refs_1_), channel_id=1, source_target_pairs={{0,8},{1,9},{2,10},{3,11},{4,12},{5,13},{6,14},{7,15},{8,0},{9,1},... | collective-permute-start | bytes 1572872 | tf_op jit(solution)/shard_map/ppermute | solution.py:37
  39.5 13.2 %collective-permute-start.9 = (f32[8,128,128]{2,1,0:T(8,128)S(1)}, f32[8,128,128]{2,1,0:T(8,128)S(1)}, u32[]{:S(2)}, u32[]{:S(2)}) collective-permute-start(f32[8,128,128]{2,1,0:T(8,128)S(1)} %collective-permute-done.5.refs_1_), channel_id=1, source_target_pairs={{0,480},{1,481},{2,482},{3,483},{4,484},{5,485},{6,486},{7,487},{8... | collective-permute-start | bytes 1572872 | tf_op jit(solution)/shard_map/ppermute | solution.py:37
  44.5 12.9 %collective-permute-start.12 = (f32[8,128,128]{2,1,0:T(8,128)S(1)}, f32[8,128,128]{2,1,0:T(8,128)S(1)}, u32[]{:S(2)}, u32[]{:S(2)}) collective-permute-start(f32[8,128,128]{2,1,0:T(8,128)S(1)} %collective-permute-done.8.refs_0_), channel_id=1, source_target_pairs={{0,480},{1,481},{2,482},{3,483},{4,484},{5,485},{6,486},{7,487},{8... | collective-permute-start | bytes 1572872 | tf_op jit(solution)/shard_map/ppermute | solution.py:37
  52.7 12.3 %collective-permute-start.13 = (f32[8,128,128]{2,1,0:T(8,128)S(1)}, f32[8,128,128]{2,1,0:T(8,128)S(1)}, u32[]{:S(2)}, u32[]{:S(2)}) collective-permute-start(f32[8,128,128]{2,1,0:T(8,128)S(1)} %collective-permute-done.9.refs_1_), channel_id=1, source_target_pairs={{0,480},{1,481},{2,482},{3,483},{4,484},{5,485},{6,486},{7,487},{8... | collective-permute-start | bytes 1572872 | tf_op jit(solution)/shard_map/ppermute | solution.py:37
  57.5 25.0 %collective-permute-start.16 = (f32[8,128,128]{2,1,0:T(8,128)S(1)}, f32[8,128,128]{2,1,0:T(8,128)S(1)}, u32[]{:S(2)}, u32[]{:S(2)}) collective-permute-start(f32[8,128,128]{2,1,0:T(8,128)S(1)} %collective-permute-done.12.refs_0_), channel_id=1, source_target_pairs={{0,480},{1,481},{2,482},{3,483},{4,484},{5,485},{6,486},{7,487},{8... | collective-permute-start | bytes 1572872 | tf_op jit(solution)/shard_map/ppermute | solution.py:37
  60.3 21.2 %collective-permute-start.14 = (f32[8,128,128]{2,1,0:T(8,128)S(1)}, f32[8,128,128]{2,1,0:T(8,128)S(1)}, u32[]{:S(2)}, u32[]{:S(2)}) collective-permute-start(f32[8,128,128]{2,1,0:T(8,128)S(1)} %collective-permute-done.12.refs_0_), channel_id=1, source_target_pairs={{0,8},{1,9},{2,10},{3,11},{4,12},{5,13},{6,14},{7,15},{8,0},{9,1},... | collective-permute-start | bytes 1572872 | tf_op jit(solution)/shard_map/ppermute | solution.py:37
  65.0 20.5 %collective-permute-start.17 = (f32[8,128,128]{2,1,0:T(8,128)S(1)}, f32[8,128,128]{2,1,0:T(8,128)S(1)}, u32[]{:S(2)}, u32[]{:S(2)}) collective-permute-start(f32[8,128,128]{2,1,0:T(8,128)S(1)} %collective-permute-done.13.refs_1_), channel_id=1, source_target_pairs={{0,480},{1,481},{2,482},{3,483},{4,484},{5,485},{6,486},{7,487},{8... | collective-permute-start | bytes 1572872 | tf_op jit(solution)/shard_map/ppermute | solution.py:37
  66.9 14.6 %collective-permute-start.15 = (f32[8,128,128]{2,1,0:T(8,128)S(1)}, f32[8,128,128]{2,1,0:T(8,128)S(1)}, u32[]{:S(2)}, u32[]{:S(2)}) collective-permute-start(f32[8,128,128]{2,1,0:T(8,128)S(1)} %collective-permute-done.13.refs_1_), channel_id=1, source_target_pairs={{0,8},{1,9},{2,10},{3,11},{4,12},{5,13},{6,14},{7,15},{8,0},{9,1},... | collective-permute-start | bytes 1572872 | tf_op jit(solution)/shard_map/ppermute | solution.py:37
  99.8 39.1 %collective-permute-start.22 = (f32[16,128,128]{2,1,0:T(8,128)S(1)}, f32[16,128,128]{2,1,0:T(8,128)S(1)}, u32[]{:S(2)}, u32[]{:S(2)}) collective-permute-start(f32[16,128,128]{2,1,0:T(8,128)S(1)} %get-tuple-element.57), channel_id=1, source_target_pairs={{0,3},{1,0},{2,1},{3,2},{4,7},{5,4},{6,5},{7,6},{8,28},{9,29},{10,... | collective-permute-start | bytes 3145736 | tf_op jit(solution)/shard_map/ppermute | solution.py:37
  104.7 39.5 %collective-permute-start.21 = (f32[16,128,128]{2,1,0:T(8,128)S(1)}, f32[16,128,128]{2,1,0:T(8,128)S(1)}, u32[]{:S(2)}, u32[]{:S(2)}) collective-permute-start(f32[16,128,128]{2,1,0:T(8,128)S(1)} %get-tuple-element.56), channel_id=1, source_target_pairs={{0,2},{1,3},{2,0},{3,1},{4,6},{5,7},{6,4},{7,5},{8,24},{9,25},{10,... | collective-permute-start | bytes 3145736 | tf_op jit(solution)/shard_map/ppermute | solution.py:37
  106.8 37.3 %collective-permute-start.20 = (f32[16,128,128]{2,1,0:T(8,128)S(1)}, f32[16,128,128]{2,1,0:T(8,128)S(1)}, u32[]{:S(2)}, u32[]{:S(2)}) collective-permute-start(f32[16,128,128]{2,1,0:T(8,128)S(1)} %get-tuple-element.55), channel_id=1, source_target_pairs={{0,1},{1,2},{2,3},{3,0},{4,5},{5,6},{6,7},{7,4},{8,12},{9,13},{10,... | collective-permute-start | bytes 3145736 | tf_op jit(solution)/shard_map/ppermute | solution.py:37
  119.4 50.2 %collective-permute-start.26 = (f32[16,128,128]{2,1,0:T(8,128)S(1)}, f32[16,128,128]{2,1,0:T(8,128)S(1)}, u32[]{:S(2)}, u32[]{:S(2)}) collective-permute-start(f32[16,128,128]{2,1,0:T(8,128)S(1)} %get-tuple-element.58), channel_id=1, source_target_pairs={{0,1},{1,2},{2,3},{3,0},{4,5},{5,6},{6,7},{7,4},{8,12},{9,13},{10,... | collective-permute-start | bytes 3145736 | tf_op jit(solution)/shard_map/ppermute | solution.py:37
  122.9 46.8 %collective-permute-start.27 = (f32[16,128,128]{2,1,0:T(8,128)S(1)}, f32[16,128,128]{2,1,0:T(8,128)S(1)}, u32[]{:S(2)}, u32[]{:S(2)}) collective-permute-start(f32[16,128,128]{2,1,0:T(8,128)S(1)} %get-tuple-element.59), channel_id=1, source_target_pairs={{0,2},{1,3},{2,0},{3,1},{4,6},{5,7},{6,4},{7,5},{8,24},{9,25},{10,... | collective-permute-start | bytes 3145736 | tf_op jit(solution)/shard_map/ppermute | solution.py:37
  138.8 30.9 %collective-permute-start.28 = (f32[16,128,128]{2,1,0:T(8,128)S(1)}, f32[16,128,128]{2,1,0:T(8,128)S(1)}, u32[]{:S(2)}, u32[]{:S(2)}) collective-permute-start(f32[16,128,128]{2,1,0:T(8,128)S(1)} %get-tuple-element.60), channel_id=1, source_target_pairs={{0,3},{1,0},{2,1},{3,2},{4,7},{5,4},{6,5},{7,6},{8,28},{9,29},{10,... | collective-permute-start | bytes 3145736 | tf_op jit(solution)/shard_map/ppermute | solution.py:37
  148.2 11.7 %collective-permute-start.24 = (f32[4,128,128]{2,1,0:T(8,128)S(1)}, f32[4,128,128]{2,1,0:T(8,128)S(1)}, u32[]{:S(2)}, u32[]{:S(2)}) collective-permute-start(f32[4,128,128]{2,1,0:T(8,128)S(1)} %get-tuple-element.74), channel_id=1, source_target_pairs={{0,4},{1,5},{2,6},{3,7},{4,16},{5,17},{6,18},{7,19},{8,9},{9,10},{... | collective-permute-start | bytes 786440 | tf_op jit(solution)/shard_map/ppermute | solution.py:37
  163.2 25.8 %collective-permute-start.29 = (f32[4,128,128]{2,1,0:T(8,128)S(1)}, f32[4,128,128]{2,1,0:T(8,128)S(1)}, u32[]{:S(2)}, u32[]{:S(2)}) collective-permute-start(f32[4,128,128]{2,1,0:T(8,128)S(1)} %fusion.2), channel_id=1, source_target_pairs={{8,392},{9,393},{10,394},{11,395},{12,396},{13,397},{14,398},{15,3... | collective-permute-start | bytes 786440 | tf_op jit(solution)/shard_map/ppermute | solution.py:37
  168.4 25.5 %collective-permute-start.30 = (f32[4,128,128]{2,1,0:T(8,128)S(1)}, f32[4,128,128]{2,1,0:T(8,128)S(1)}, u32[]{:S(2)}, u32[]{:S(2)}) collective-permute-start(f32[4,128,128]{2,1,0:T(8,128)S(1)} %fusion.2), channel_id=1, source_target_pairs={{0,392},{1,393},{2,394},{3,395},{4,396},{5,397},{6,398},{7,399},{2... | collective-permute-start | bytes 786440 | tf_op jit(solution)/shard_map/ppermute | solution.py:37
  169.9 24.0 %collective-permute-start.31 = (f32[4,128,128]{2,1,0:T(8,128)S(1)}, f32[4,128,128]{2,1,0:T(8,128)S(1)}, u32[]{:S(2)}, u32[]{:S(2)}) collective-permute-start(f32[4,128,128]{2,1,0:T(8,128)S(1)} %get-tuple-element.71), channel_id=1, source_target_pairs={{0,16},{1,17},{2,18},{3,19},{4,20},{5,21},{6,22},{7,23},{8,10},{9,... | collective-permute-start | bytes 786440 | tf_op jit(solution)/shard_map/ppermute | solution.py:37
  173.5 20.4 %collective-permute-start.32 = (f32[4,128,128]{2,1,0:T(8,128)S(1)}, f32[4,128,128]{2,1,0:T(8,128)S(1)}, u32[]{:S(2)}, u32[]{:S(2)}) collective-permute-start(f32[4,128,128]{2,1,0:T(8,128)S(1)} %get-tuple-element.70), channel_id=1, source_target_pairs={{0,4},{1,5},{2,6},{3,7},{4,16},{5,17},{6,18},{7,19},{8,9},{9,10},{... | collective-permute-start | bytes 786440 | tf_op jit(solution)/shard_map/ppermute | solution.py:37
  176.7 17.2 %collective-permute-start.33 = (f32[4,128,128]{2,1,0:T(8,128)S(1)}, f32[4,128,128]{2,1,0:T(8,128)S(1)}, u32[]{:S(2)}, u32[]{:S(2)}) collective-permute-start(f32[4,128,128]{2,1,0:T(8,128)S(1)} %get-tuple-element.69), channel_id=1, source_target_pairs={{0,20},{1,21},{2,22},{3,23},{4,0},{5,1},{6,2},{7,3},{8,11},{9,8},{... | collective-permute-start | bytes 786440 | tf_op jit(solution)/shard_map/ppermute | solution.py:37
  (15 other events, 104.2 us)

commit v6 on v5

--- a/solution.py
+++ b/solution.py
@@ -218,10 +218,13 @@
     return lax.optimization_barrier((value, *others))[0]
 
 
-def reduce_plane(pieces, others=(), late=()):
+def reduce_plane(pieces, others=(), late=(), third=()):
     received = [None] * 4
     for offset in (2, 1, 3):
-        received[offset] = send(pieces[offset], plane_step(0, offset))
+        piece = pieces[offset]
+        if third and offset == 3:
+            piece = after(piece, *third)
+        received[offset] = send(piece, plane_step(0, offset))
     if others:
         received[1:] = lax.optimization_barrier((*others, *received[1:]))[-3:]
     count = pieces[0].shape[0] // 4
@@ -256,10 +259,10 @@
 
     placed = send(out_ids, to_place)
     col = xhi * 2 + core
-    left = jnp.where(col == 1, LEFT[1], jnp.where(col == 2, LEFT[2], LEFT[0]))
+    left = jnp.where(col == 1, LEFT[1], jnp.where(col == 2, LEFT[2], 0))
     codes = slot_codes(placed, z + left, col)[None]
-    codes = jnp.concatenate([codes, send(codes, other_core)], axis=0)
-    codes = jnp.concatenate([codes, send(codes, other_xhi)], axis=0)
+    chip_codes = jnp.concatenate([codes, send(codes, other_core)], axis=0)
+    codes = jnp.concatenate([chip_codes, send(chip_codes, other_xhi)], axis=0)
 
     mine_a = [sort_blocks(block_ids, blocks)]
     mine_b = [send(mine_a[0], other_core)]
@@ -268,13 +271,17 @@
     for k in range(1, REACH + 1):
         next_a, next_b = mine_a[-1], mine_b[-1]
         if k == 1:
-            next_a = after(next_a, placed)
+            next_b = after(next_b, placed)
+        if k == 2:
+            next_b = after(next_b, chip_codes)
+        if k == 3:
+            next_b = after(next_b, codes)
         if k > 2:
             next_a = after(next_a, their_a[k - 2])
             next_b = after(next_b, split[k - 2][0])
         mine_a.append(send(next_a, ring_z))
         mine_b.append(send(next_b, ring_z))
-        swap_a = mine_a[k] if k < REACH else after(mine_a[k], split[k - 1][0], codes)
+        swap_a = mine_a[k] if k < REACH else after(mine_a[k], split[k - 1][0])
         their_a.append(send(swap_a, other_core))
         their_b.append(send(mine_b[k], other_core))
         split.append(split_rows(where, mine_a[k], mine_b[k], their_a[k], their_b[k]))
@@ -284,7 +291,7 @@
     wide, arrived = reduce_plane(pieces)
     far_same, far_cross = bring_home(wide)
     pieces = chunk_products(0, where, after(codes, pieces[0]), split)
-    near, _ = reduce_plane(pieces, [wide], (far_same, far_cross))
+    near, _ = reduce_plane(pieces, [wide], (far_same, far_cross), ())
     near_cross = send(near, home(0, False))
 
     same = jnp.where(core == xhi, near, far_same)

time: 198 us -> 195 us (0.985); the launches traced: 197 us -> 192 us
  waiting for transfers between devices: 56.3 us -> 52.7 us
    ppermute x35, waiting for transfers between devices: 56.3 us -> 52.7 us  [send(): return lax.ppermute(value, AXES, pairs)]
where the time goes in v6:
time: 195 us; the launch traced here: 192 us
  starting transfers between devices  111 us (57%)
  waiting for transfers between devices  52.7 us (27%)
  Pallas kernels  25.4 us (13%)
    ppermute x35, starting transfers between devices, send(): return lax.ppermute(value, AXES, pairs)  111 us
    ppermute x35, waiting for transfers between devices, send(): return lax.ppermute(value, AXES, pairs)  52.7 us
    pallas_call x2, Pallas kernels, chunk_products(): pl.pallas_call(functools.partial(chunk_kernel, chunk), out_shape=[jax.Sha...  19.3 us
    pallas_call x5, Pallas kernels, split_rows(): pl.pallas_call(split_kernel, out_shape=[jax.ShapeDtypeStruct((len(panels)...  4.24 us
  transfers between devices with their start and end apart: 35, of which 14 were waited for; matrix products, arithmetic and copies ran while one was open for 0% of the time, Pallas kernels for 7%

profile of v6, /device:TPU:1, one launch (start us, length us, event | category | flops | bytes accessed | tf_op | source)
XLA Modules:
  0.0 192.2 jit_solution(1772301711704239897)
XLA Ops:
  1.9 8.8 %collective-permute-start.3 = (f32[8,128,128]{2,1,0:T(8,128)}, f32[8,128,128]{2,1,0:T(8,128)S(1)}, u32[]{:S(2)}, u32[]{:S(2)}) collective-permute-start(f32[8,128,128]{2,1,0:T(8,128)} %sort_blocks.1.refs_0_), channel_id=1, source_target_pairs={{0,8},{1,9},{2,10},{3,11},{4,12},{5,13},{6,14},{7,15},{8,0},{9,1},... | collective-permute-start | bytes 1572872 | tf_op jit(solution)/shard_map/ppermute | solution.py:37
  12.7 5.1 %collective-permute-start = (s32[64,2]{0,1:T(2,128)S(1)}, s32[64,2]{0,1:T(2,128)S(1)}, u32[]{:S(2)}, u32[]{:S(2)}) collective-permute-start(s32[64,2]{0,1:T(2,128)S(1)} %copy-done.3), channel_id=1, source_target_pairs={{0,0},{1,1},{2,2},{3,3},{4,4},{5,5},{6,6},{7,7},{8,136},{9,137},{1... | collective-permute-start | bytes 1544 | tf_op jit(solution)/shard_map/ppermute | solution.py:37
  17.8 7.6 %collective-permute-done = s32[64,2]{0,1:T(2,128)S(1)} collective-permute-done((s32[64,2]{0,1:T(2,128)S(1)}, s32[64,2]{0,1:T(2,128)S(1)}, u32[]{:S(2)}, u32[]{:S(2)}) %collective-permute-start) | collective-permute-done | bytes 544 | tf_op jit(solution)/shard_map/ppermute | solution.py:37
  38.4 4.0 %collective-permute-start.7 = (f32[8,128,128]{2,1,0:T(8,128)S(1)}, f32[8,128,128]{2,1,0:T(8,128)S(1)}, u32[]{:S(2)}, u32[]{:S(2)}) collective-permute-start(f32[8,128,128]{2,1,0:T(8,128)S(1)} %collective-permute-done.5.refs_1_), channel_id=1, source_target_pairs={{0,8},{1,9},{2,10},{3,11},{4,12},{5,13},{6,14},{7,15},{8,0},{9,1},... | collective-permute-start | bytes 1572872 | tf_op jit(solution)/shard_map/ppermute | solution.py:37
  42.4 5.6 %collective-permute-start.2 = (s32[2,64]{1,0:T(2,128)S(1)}, s32[2,64]{1,0:T(2,128)S(1)}, u32[]{:S(2)}, u32[]{:S(2)}) collective-permute-start(s32[2,64]{1,0:T(2,128)S(1)} %pad_add_fusion.1), channel_id=1, source_target_pairs={{0,16},{1,17},{2,18},{3,19},{4,20},{5,21},{6,22},{7,23},{8,24},{9,... | collective-permute-start | bytes 1544 | tf_op jit(solution)/shard_map/ppermute | solution.py:37
  50.9 4.3 %collective-permute-start.10 = (f32[8,128,128]{2,1,0:T(8,128)S(1)}, f32[8,128,128]{2,1,0:T(8,128)S(1)}, u32[]{:S(2)}, u32[]{:S(2)}) collective-permute-start(f32[8,128,128]{2,1,0:T(8,128)S(1)} %collective-permute-done.8.refs_0_), channel_id=1, source_target_pairs={{0,8},{1,9},{2,10},{3,11},{4,12},{5,13},{6,14},{7,15},{8,0},{9,1},... | collective-permute-start | bytes 1572872 | tf_op jit(solution)/shard_map/ppermute | solution.py:37
  62.9 4.4 %collective-permute-done.13.refs_1_ = f32[8,128,128]{2,1,0:T(8,128)S(1)} collective-permute-done((f32[8,128,128]{2,1,0:T(8,128)S(1)}, f32[8,128,128]{2,1,0:T(8,128)S(1)}, u32[]{:S(2)}, u32[]{:S(2)}) %collective-permute-start.13) | collective-permute-done | bytes 524320 | tf_op jit(solution)/shard_map/ppermute | solution.py:37
  75.4 4.9 %collective-permute-done.16.refs_0_ = f32[8,128,128]{2,1,0:T(8,128)S(1)} collective-permute-done((f32[8,128,128]{2,1,0:T(8,128)S(1)}, f32[8,128,128]{2,1,0:T(8,128)S(1)}, u32[]{:S(2)}, u32[]{:S(2)}) %collective-permute-start.16) | collective-permute-done | bytes 524320 | tf_op jit(solution)/shard_map/ppermute | solution.py:37
  82.7 3.3 %collective-permute-done.17.refs_1_ = f32[8,128,128]{2,1,0:T(8,128)S(1)} collective-permute-done((f32[8,128,128]{2,1,0:T(8,128)S(1)}, f32[8,128,128]{2,1,0:T(8,128)S(1)}, u32[]{:S(2)}, u32[]{:S(2)}) %collective-permute-start.17) | collective-permute-done | bytes 524320 | tf_op jit(solution)/shard_map/ppermute | solution.py:37
  90.7 9.6 %products_1.1 = (f32[16,128,128]{2,1,0:T(8,128)S(1)}, f32[16,128,128]{2,1,0:T(8,128)S(1)}, f32[16,128,128]{2,1,0:T(8,128)S(1)}, f32[16,128,128]{2,1,0:T(8,128)S(1)}) custom-call(s32[2]{0:T(128)S(1)} %pad_add_fusion.2.where_ref, s32[4,64]{1,0:T(4,128)S(1)} %pad_add_fusion.codes_ref, bf16[1,512,512]{2,1,0:T(8,128)(2,1)S(1)} %get-tuple-element.38.refs_0_, ...), custom_call_target="tpu_custom_call" | custom-call | tf_op jit(solution)/shard_map/products_1/pallas_call | solution.py:190
  100.3 4.9 %collective-permute-start.22 = (f32[16,128,128]{2,1,0:T(8,128)S(1)}, f32[16,128,128]{2,1,0:T(8,128)S(1)}, u32[]{:S(2)}, u32[]{:S(2)}) collective-permute-start(f32[16,128,128]{2,1,0:T(8,128)S(1)} %get-tuple-element.61), channel_id=1, source_target_pairs={{0,3},{1,0},{2,1},{3,2},{4,7},{5,4},{6,5},{7,6},{8,28},{9,29},{10,... | collective-permute-start | bytes 3145736 | tf_op jit(solution)/shard_map/ppermute | solution.py:37
  110.4 9.6 %products_0.1 = (f32[16,128,128]{2,1,0:T(8,128)S(1)}, f32[16,128,128]{2,1,0:T(8,128)S(1)}, f32[16,128,128]{2,1,0:T(8,128)S(1)}, f32[16,128,128]{2,1,0:T(8,128)S(1)}) custom-call(s32[2]{0:T(128)S(1)} %pad_add_fusion.2.where_ref, s32[4,64]{1,0:T(4,128)S(1)} %pad_add_fusion.codes_ref, bf16[1,512,512]{2,1,0:T(8,128)(2,1)S(1)} %get-tuple-element.38.refs_0_, ...), custom_call_target="tpu_custom_call" | custom-call | tf_op jit(solution)/shard_map/products_0/pallas_call | solution.py:190
  120.0 3.4 %collective-permute-start.26 = (f32[16,128,128]{2,1,0:T(8,128)S(1)}, f32[16,128,128]{2,1,0:T(8,128)S(1)}, u32[]{:S(2)}, u32[]{:S(2)}) collective-permute-start(f32[16,128,128]{2,1,0:T(8,128)S(1)} %get-tuple-element.62), channel_id=1, source_target_pairs={{0,1},{1,2},{2,3},{3,0},{4,5},{5,6},{6,7},{7,4},{8,12},{9,13},{10,... | collective-permute-start | bytes 3145736 | tf_op jit(solution)/shard_map/ppermute | solution.py:37
  123.5 3.4 %collective-permute-start.27 = (f32[16,128,128]{2,1,0:T(8,128)S(1)}, f32[16,128,128]{2,1,0:T(8,128)S(1)}, u32[]{:S(2)}, u32[]{:S(2)}) collective-permute-start(f32[16,128,128]{2,1,0:T(8,128)S(1)} %get-tuple-element.63), channel_id=1, source_target_pairs={{0,2},{1,3},{2,0},{3,1},{4,6},{5,7},{6,4},{7,5},{8,24},{9,25},{10,... | collective-permute-start | bytes 3145736 | tf_op jit(solution)/shard_map/ppermute | solution.py:37
  126.9 12.6 %collective-permute-done.22 = f32[16,128,128]{2,1,0:T(8,128)S(1)} collective-permute-done((f32[16,128,128]{2,1,0:T(8,128)S(1)}, f32[16,128,128]{2,1,0:T(8,128)S(1)}, u32[]{:S(2)}, u32[]{:S(2)}) %collective-permute-start.22) | collective-permute-done | bytes 1048608 | tf_op jit(solution)/shard_map/ppermute | solution.py:37
  139.4 5.3 %collective-permute-start.28 = (f32[16,128,128]{2,1,0:T(8,128)S(1)}, f32[16,128,128]{2,1,0:T(8,128)S(1)}, u32[]{:S(2)}, u32[]{:S(2)}) collective-permute-start(f32[16,128,128]{2,1,0:T(8,128)S(1)} %get-tuple-element.64), channel_id=1, source_target_pairs={{0,3},{1,0},{2,1},{3,2},{4,7},{5,4},{6,5},{7,6},{8,28},{9,29},{10,... | collective-permute-start | bytes 3145736 | tf_op jit(solution)/shard_map/ppermute | solution.py:37
  145.0 4.0 %collective-permute-start.25 = (f32[4,128,128]{2,1,0:T(8,128)S(1)}, f32[4,128,128]{2,1,0:T(8,128)S(1)}, u32[]{:S(2)}, u32[]{:S(2)}) collective-permute-start(f32[4,128,128]{2,1,0:T(8,128)S(1)} %get-tuple-element.77), channel_id=1, source_target_pairs={{0,20},{1,21},{2,22},{3,23},{4,0},{5,1},{6,2},{7,3},{8,11},{9,8},{... | collective-permute-start | bytes 786440 | tf_op jit(solution)/shard_map/ppermute | solution.py:37
  150.9 4.4 %collective-permute-done.25 = f32[4,128,128]{2,1,0:T(8,128)S(1)} collective-permute-done((f32[4,128,128]{2,1,0:T(8,128)S(1)}, f32[4,128,128]{2,1,0:T(8,128)S(1)}, u32[]{:S(2)}, u32[]{:S(2)}) %collective-permute-start.25) | collective-permute-done | bytes 262176 | tf_op jit(solution)/shard_map/ppermute | solution.py:37
  155.3 3.6 %collective-permute-start.23 = (f32[4,128,128]{2,1,0:T(8,128)S(1)}, f32[4,128,128]{2,1,0:T(8,128)S(1)}, u32[]{:S(2)}, u32[]{:S(2)}) collective-permute-start(f32[4,128,128]{2,1,0:T(8,128)S(1)} %get-tuple-element.76), channel_id=1, source_target_pairs={{0,16},{1,17},{2,18},{3,19},{4,20},{5,21},{6,22},{7,23},{8,10},{9,... | collective-permute-start | bytes 786440 | tf_op jit(solution)/shard_map/ppermute | solution.py:37
  164.0 5.2 %collective-permute-start.29 = (f32[4,128,128]{2,1,0:T(8,128)S(1)}, f32[4,128,128]{2,1,0:T(8,128)S(1)}, u32[]{:S(2)}, u32[]{:S(2)}) collective-permute-start(f32[4,128,128]{2,1,0:T(8,128)S(1)} %fusion.2), channel_id=1, source_target_pairs={{8,392},{9,393},{10,394},{11,395},{12,396},{13,397},{14,398},{15,3... | collective-permute-start | bytes 786440 | tf_op jit(solution)/shard_map/ppermute | solution.py:37
  170.7 3.6 %collective-permute-start.31 = (f32[4,128,128]{2,1,0:T(8,128)S(1)}, f32[4,128,128]{2,1,0:T(8,128)S(1)}, u32[]{:S(2)}, u32[]{:S(2)}) collective-permute-start(f32[4,128,128]{2,1,0:T(8,128)S(1)} %get-tuple-element.75), channel_id=1, source_target_pairs={{0,16},{1,17},{2,18},{3,19},{4,20},{5,21},{6,22},{7,23},{8,10},{9,... | collective-permute-start | bytes 786440 | tf_op jit(solution)/shard_map/ppermute | solution.py:37
  174.3 3.2 %collective-permute-start.32 = (f32[4,128,128]{2,1,0:T(8,128)S(1)}, f32[4,128,128]{2,1,0:T(8,128)S(1)}, u32[]{:S(2)}, u32[]{:S(2)}) collective-permute-start(f32[4,128,128]{2,1,0:T(8,128)S(1)} %get-tuple-element.74), channel_id=1, source_target_pairs={{0,4},{1,5},{2,6},{3,7},{4,16},{5,17},{6,18},{7,19},{8,9},{9,10},{... | collective-permute-start | bytes 786440 | tf_op jit(solution)/shard_map/ppermute | solution.py:37
  177.5 3.3 %collective-permute-start.33 = (f32[4,128,128]{2,1,0:T(8,128)S(1)}, f32[4,128,128]{2,1,0:T(8,128)S(1)}, u32[]{:S(2)}, u32[]{:S(2)}) collective-permute-start(f32[4,128,128]{2,1,0:T(8,128)S(1)} %get-tuple-element.73), channel_id=1, source_target_pairs={{0,20},{1,21},{2,22},{3,23},{4,0},{5,1},{6,2},{7,3},{8,11},{9,8},{... | collective-permute-start | bytes 786440 | tf_op jit(solution)/shard_map/ppermute | solution.py:37
  180.8 6.9 %collective-permute-done.29 = f32[4,128,128]{2,1,0:T(8,128)S(1)} collective-permute-done((f32[4,128,128]{2,1,0:T(8,128)S(1)}, f32[4,128,128]{2,1,0:T(8,128)S(1)}, u32[]{:S(2)}, u32[]{:S(2)}) %collective-permute-start.29) | collective-permute-done | bytes 262176 | tf_op jit(solution)/shard_map/ppermute | solution.py:37
  (76 shorter events, 60.8 us)
Async XLA Ops:
  1.9 23.4 %collective-permute-start.3 = (f32[8,128,128]{2,1,0:T(8,128)}, f32[8,128,128]{2,1,0:T(8,128)S(1)}, u32[]{:S(2)}, u32[]{:S(2)}) collective-permute-start(f32[8,128,128]{2,1,0:T(8,128)} %sort_blocks.1.refs_0_), channel_id=1, source_target_pairs={{0,8},{1,9},{2,10},{3,11},{4,12},{5,13},{6,14},{7,15},{8,0},{9,1},... | collective-permute-start | bytes 1572872 | tf_op jit(solution)/shard_map/ppermute | solution.py:37
  10.7 20.2 %collective-permute-start.4 = (f32[8,128,128]{2,1,0:T(8,128)}, f32[8,128,128]{2,1,0:T(8,128)S(1)}, u32[]{:S(2)}, u32[]{:S(2)}) collective-permute-start(f32[8,128,128]{2,1,0:T(8,128)} %sort_blocks.1.refs_0_), channel_id=1, source_target_pairs={{0,480},{1,481},{2,482},{3,483},{4,484},{5,485},{6,486},{7,487},{8... | collective-permute-start | bytes 1572872 | tf_op jit(solution)/shard_map/ppermute | solution.py:37
  12.7 12.6 %collective-permute-start = (s32[64,2]{0,1:T(2,128)S(1)}, s32[64,2]{0,1:T(2,128)S(1)}, u32[]{:S(2)}, u32[]{:S(2)}) collective-permute-start(s32[64,2]{0,1:T(2,128)S(1)} %copy-done.3), channel_id=1, source_target_pairs={{0,0},{1,1},{2,2},{3,3},{4,4},{5,5},{6,6},{7,7},{8,136},{9,137},{1... | collective-permute-start | bytes 1544 | tf_op jit(solution)/shard_map/ppermute | solution.py:37
  25.3 11.1 %collective-permute-start.5 = (f32[8,128,128]{2,1,0:T(8,128)S(1)}, f32[8,128,128]{2,1,0:T(8,128)S(1)}, u32[]{:S(2)}, u32[]{:S(2)}) collective-permute-start(f32[8,128,128]{2,1,0:T(8,128)S(1)} %collective-permute-done.3.refs_1_), channel_id=1, source_target_pairs={{0,480},{1,481},{2,482},{3,483},{4,484},{5,485},{6,486},{7,487},{8... | collective-permute-start | bytes 1572872 | tf_op jit(solution)/shard_map/ppermute | solution.py:37
  30.9 18.0 %collective-permute-start.6 = (f32[8,128,128]{2,1,0:T(8,128)S(1)}, f32[8,128,128]{2,1,0:T(8,128)S(1)}, u32[]{:S(2)}, u32[]{:S(2)}) collective-permute-start(f32[8,128,128]{2,1,0:T(8,128)S(1)} %collective-permute-done.4.refs_0_), channel_id=1, source_target_pairs={{0,8},{1,9},{2,10},{3,11},{4,12},{5,13},{6,14},{7,15},{8,0},{9,1},... | collective-permute-start | bytes 1572872 | tf_op jit(solution)/shard_map/ppermute | solution.py:37
  33.4 15.6 %collective-permute-start.8 = (f32[8,128,128]{2,1,0:T(8,128)S(1)}, f32[8,128,128]{2,1,0:T(8,128)S(1)}, u32[]{:S(2)}, u32[]{:S(2)}) collective-permute-start(f32[8,128,128]{2,1,0:T(8,128)S(1)} %collective-permute-done.4.refs_0_), channel_id=1, source_target_pairs={{0,480},{1,481},{2,482},{3,483},{4,484},{5,485},{6,486},{7,487},{8... | collective-permute-start | bytes 1572872 | tf_op jit(solution)/shard_map/ppermute | solution.py:37
  36.5 18.8 %collective-permute-start.9 = (f32[8,128,128]{2,1,0:T(8,128)S(1)}, f32[8,128,128]{2,1,0:T(8,128)S(1)}, u32[]{:S(2)}, u32[]{:S(2)}) collective-permute-start(f32[8,128,128]{2,1,0:T(8,128)S(1)} %collective-permute-done.5.refs_1_), channel_id=1, source_target_pairs={{0,480},{1,481},{2,482},{3,483},{4,484},{5,485},{6,486},{7,487},{8... | collective-permute-start | bytes 1572872 | tf_op jit(solution)/shard_map/ppermute | solution.py:37
  38.4 16.9 %collective-permute-start.7 = (f32[8,128,128]{2,1,0:T(8,128)S(1)}, f32[8,128,128]{2,1,0:T(8,128)S(1)}, u32[]{:S(2)}, u32[]{:S(2)}) collective-permute-start(f32[8,128,128]{2,1,0:T(8,128)S(1)} %collective-permute-done.5.refs_1_), channel_id=1, source_target_pairs={{0,8},{1,9},{2,10},{3,11},{4,12},{5,13},{6,14},{7,15},{8,0},{9,1},... | collective-permute-start | bytes 1572872 | tf_op jit(solution)/shard_map/ppermute | solution.py:37
  48.9 12.1 %collective-permute-start.12 = (f32[8,128,128]{2,1,0:T(8,128)S(1)}, f32[8,128,128]{2,1,0:T(8,128)S(1)}, u32[]{:S(2)}, u32[]{:S(2)}) collective-permute-start(f32[8,128,128]{2,1,0:T(8,128)S(1)} %collective-permute-done.8.refs_0_), channel_id=1, source_target_pairs={{0,480},{1,481},{2,482},{3,483},{4,484},{5,485},{6,486},{7,487},{8... | collective-permute-start | bytes 1572872 | tf_op jit(solution)/shard_map/ppermute | solution.py:37
  56.1 11.1 %collective-permute-start.13 = (f32[8,128,128]{2,1,0:T(8,128)S(1)}, f32[8,128,128]{2,1,0:T(8,128)S(1)}, u32[]{:S(2)}, u32[]{:S(2)}) collective-permute-start(f32[8,128,128]{2,1,0:T(8,128)S(1)} %collective-permute-done.9.refs_1_), channel_id=1, source_target_pairs={{0,480},{1,481},{2,482},{3,483},{4,484},{5,485},{6,486},{7,487},{8... | collective-permute-start | bytes 1572872 | tf_op jit(solution)/shard_map/ppermute | solution.py:37
  58.2 13.0 %collective-permute-start.11 = (f32[8,128,128]{2,1,0:T(8,128)S(1)}, f32[8,128,128]{2,1,0:T(8,128)S(1)}, u32[]{:S(2)}, u32[]{:S(2)}) collective-permute-start(f32[8,128,128]{2,1,0:T(8,128)S(1)} %collective-permute-done.9.refs_1_), channel_id=1, source_target_pairs={{0,8},{1,9},{2,10},{3,11},{4,12},{5,13},{6,14},{7,15},{8,0},{9,1},... | collective-permute-start | bytes 1572872 | tf_op jit(solution)/shard_map/ppermute | solution.py:37
  61.0 13.5 %collective-permute-start.14 = (f32[8,128,128]{2,1,0:T(8,128)S(1)}, f32[8,128,128]{2,1,0:T(8,128)S(1)}, u32[]{:S(2)}, u32[]{:S(2)}) collective-permute-start(f32[8,128,128]{2,1,0:T(8,128)S(1)} %collective-permute-done.12.refs_0_), channel_id=1, source_target_pairs={{0,8},{1,9},{2,10},{3,11},{4,12},{5,13},{6,14},{7,15},{8,0},{9,1},... | collective-permute-start | bytes 1572872 | tf_op jit(solution)/shard_map/ppermute | solution.py:37
  72.1 13.8 %collective-permute-start.17 = (f32[8,128,128]{2,1,0:T(8,128)S(1)}, f32[8,128,128]{2,1,0:T(8,128)S(1)}, u32[]{:S(2)}, u32[]{:S(2)}) collective-permute-start(f32[8,128,128]{2,1,0:T(8,128)S(1)} %collective-permute-done.13.refs_1_), channel_id=1, source_target_pairs={{0,480},{1,481},{2,482},{3,483},{4,484},{5,485},{6,486},{7,487},{8... | collective-permute-start | bytes 1572872 | tf_op jit(solution)/shard_map/ppermute | solution.py:37
  100.3 39.1 %collective-permute-start.22 = (f32[16,128,128]{2,1,0:T(8,128)S(1)}, f32[16,128,128]{2,1,0:T(8,128)S(1)}, u32[]{:S(2)}, u32[]{:S(2)}) collective-permute-start(f32[16,128,128]{2,1,0:T(8,128)S(1)} %get-tuple-element.61), channel_id=1, source_target_pairs={{0,3},{1,0},{2,1},{3,2},{4,7},{5,4},{6,5},{7,6},{8,28},{9,29},{10,... | collective-permute-start | bytes 3145736 | tf_op jit(solution)/shard_map/ppermute | solution.py:37
  105.2 39.5 %collective-permute-start.21 = (f32[16,128,128]{2,1,0:T(8,128)S(1)}, f32[16,128,128]{2,1,0:T(8,128)S(1)}, u32[]{:S(2)}, u32[]{:S(2)}) collective-permute-start(f32[16,128,128]{2,1,0:T(8,128)S(1)} %get-tuple-element.60), channel_id=1, source_target_pairs={{0,2},{1,3},{2,0},{3,1},{4,6},{5,7},{6,4},{7,5},{8,24},{9,25},{10,... | collective-permute-start | bytes 3145736 | tf_op jit(solution)/shard_map/ppermute | solution.py:37
  107.4 37.3 %collective-permute-start.20 = (f32[16,128,128]{2,1,0:T(8,128)S(1)}, f32[16,128,128]{2,1,0:T(8,128)S(1)}, u32[]{:S(2)}, u32[]{:S(2)}) collective-permute-start(f32[16,128,128]{2,1,0:T(8,128)S(1)} %get-tuple-element.59), channel_id=1, source_target_pairs={{0,1},{1,2},{2,3},{3,0},{4,5},{5,6},{6,7},{7,4},{8,12},{9,13},{10,... | collective-permute-start | bytes 3145736 | tf_op jit(solution)/shard_map/ppermute | solution.py:37
  120.0 50.5 %collective-permute-start.26 = (f32[16,128,128]{2,1,0:T(8,128)S(1)}, f32[16,128,128]{2,1,0:T(8,128)S(1)}, u32[]{:S(2)}, u32[]{:S(2)}) collective-permute-start(f32[16,128,128]{2,1,0:T(8,128)S(1)} %get-tuple-element.62), channel_id=1, source_target_pairs={{0,1},{1,2},{2,3},{3,0},{4,5},{5,6},{6,7},{7,4},{8,12},{9,13},{10,... | collective-permute-start | bytes 3145736 | tf_op jit(solution)/shard_map/ppermute | solution.py:37
  123.5 47.0 %collective-permute-start.27 = (f32[16,128,128]{2,1,0:T(8,128)S(1)}, f32[16,128,128]{2,1,0:T(8,128)S(1)}, u32[]{:S(2)}, u32[]{:S(2)}) collective-permute-start(f32[16,128,128]{2,1,0:T(8,128)S(1)} %get-tuple-element.63), channel_id=1, source_target_pairs={{0,2},{1,3},{2,0},{3,1},{4,6},{5,7},{6,4},{7,5},{8,24},{9,25},{10,... | collective-permute-start | bytes 3145736 | tf_op jit(solution)/shard_map/ppermute | solution.py:37
  139.4 31.1 %collective-permute-start.28 = (f32[16,128,128]{2,1,0:T(8,128)S(1)}, f32[16,128,128]{2,1,0:T(8,128)S(1)}, u32[]{:S(2)}, u32[]{:S(2)}) collective-permute-start(f32[16,128,128]{2,1,0:T(8,128)S(1)} %get-tuple-element.64), channel_id=1, source_target_pairs={{0,3},{1,0},{2,1},{3,2},{4,7},{5,4},{6,5},{7,6},{8,28},{9,29},{10,... | collective-permute-start | bytes 3145736 | tf_op jit(solution)/shard_map/ppermute | solution.py:37
  149.0 11.7 %collective-permute-start.24 = (f32[4,128,128]{2,1,0:T(8,128)S(1)}, f32[4,128,128]{2,1,0:T(8,128)S(1)}, u32[]{:S(2)}, u32[]{:S(2)}) collective-permute-start(f32[4,128,128]{2,1,0:T(8,128)S(1)} %get-tuple-element.78), channel_id=1, source_target_pairs={{0,4},{1,5},{2,6},{3,7},{4,16},{5,17},{6,18},{7,19},{8,9},{9,10},{... | collective-permute-start | bytes 786440 | tf_op jit(solution)/shard_map/ppermute | solution.py:37
  164.0 23.8 %collective-permute-start.29 = (f32[4,128,128]{2,1,0:T(8,128)S(1)}, f32[4,128,128]{2,1,0:T(8,128)S(1)}, u32[]{:S(2)}, u32[]{:S(2)}) collective-permute-start(f32[4,128,128]{2,1,0:T(8,128)S(1)} %fusion.2), channel_id=1, source_target_pairs={{8,392},{9,393},{10,394},{11,395},{12,396},{13,397},{14,398},{15,3... | collective-permute-start | bytes 786440 | tf_op jit(solution)/shard_map/ppermute | solution.py:37
  169.2 19.0 %collective-permute-start.30 = (f32[4,128,128]{2,1,0:T(8,128)S(1)}, f32[4,128,128]{2,1,0:T(8,128)S(1)}, u32[]{:S(2)}, u32[]{:S(2)}) collective-permute-start(f32[4,128,128]{2,1,0:T(8,128)S(1)} %fusion.2), channel_id=1, source_target_pairs={{0,392},{1,393},{2,394},{3,395},{4,396},{5,397},{6,398},{7,399},{2... | collective-permute-start | bytes 786440 | tf_op jit(solution)/shard_map/ppermute | solution.py:37
  170.7 17.5 %collective-permute-start.31 = (f32[4,128,128]{2,1,0:T(8,128)S(1)}, f32[4,128,128]{2,1,0:T(8,128)S(1)}, u32[]{:S(2)}, u32[]{:S(2)}) collective-permute-start(f32[4,128,128]{2,1,0:T(8,128)S(1)} %get-tuple-element.75), channel_id=1, source_target_pairs={{0,16},{1,17},{2,18},{3,19},{4,20},{5,21},{6,22},{7,23},{8,10},{9,... | collective-permute-start | bytes 786440 | tf_op jit(solution)/shard_map/ppermute | solution.py:37
  174.3 13.9 %collective-permute-start.32 = (f32[4,128,128]{2,1,0:T(8,128)S(1)}, f32[4,128,128]{2,1,0:T(8,128)S(1)}, u32[]{:S(2)}, u32[]{:S(2)}) collective-permute-start(f32[4,128,128]{2,1,0:T(8,128)S(1)} %get-tuple-element.74), channel_id=1, source_target_pairs={{0,4},{1,5},{2,6},{3,7},{4,16},{5,17},{6,18},{7,19},{8,9},{9,10},{... | collective-permute-start | bytes 786440 | tf_op jit(solution)/shard_map/ppermute | solution.py:37
  (15 other events, 132.9 us)

commit v7 on v6

--- a/solution.py
+++ b/solution.py
@@ -281,7 +281,7 @@
             next_b = after(next_b, split[k - 2][0])
         mine_a.append(send(next_a, ring_z))
         mine_b.append(send(next_b, ring_z))
-        swap_a = mine_a[k] if k < REACH else after(mine_a[k], split[k - 1][0])
+        swap_a = mine_a[k] if k < REACH else mine_a[k]
         their_a.append(send(swap_a, other_core))
         their_b.append(send(mine_b[k], other_core))
         split.append(split_rows(where, mine_a[k], mine_b[k], their_a[k], their_b[k]))

time: 195 us -> 190 us (0.974)
  waiting for transfers between devices: 52.7 us -> 46.3 us
    ppermute x35, waiting for transfers between devices: 52.7 us -> 46.3 us  [send(): return lax.ppermute(value, AXES, pairs)]
  transfers between devices with their start and end apart: 35 -> 35, of which waited for: 14 -> 12; matrix products, arithmetic and copies ran while one was open for 0% -> 0% of each run, Pallas kernels for 7% -> 7%
where the time goes in v7:
time: 190 us; the launch traced here: 187 us
  starting transfers between devices  112 us (59%)
  waiting for transfers between devices  46.3 us (24%)
  Pallas kernels  25.4 us (13%)
  other arithmetic  1.92 us (1%)
    ppermute x35, starting transfers between devices, send(): return lax.ppermute(value, AXES, pairs)  112 us
    ppermute x35, waiting for transfers between devices, send(): return lax.ppermute(value, AXES, pairs)  46.3 us
    pallas_call x2, Pallas kernels, chunk_products(): pl.pallas_call(functools.partial(chunk_kernel, chunk), out_shape=[jax.Sha...  19.3 us
    pallas_call x5, Pallas kernels, split_rows(): pl.pallas_call(split_kernel, out_shape=[jax.ShapeDtypeStruct((len(panels)...  4.24 us
  transfers between devices with their start and end apart: 35, of which 12 were waited for; matrix products, arithmetic and copies ran while one was open for 0% of the time, Pallas kernels for 7%

profile of v7, /device:TPU:1, one launch (start us, length us, event | category | flops | bytes accessed | tf_op | source)
XLA Modules:
  0.0 186.9 jit_solution(15729830988653922641)
XLA Ops:
  1.9 8.8 %collective-permute-start.3 = (f32[8,128,128]{2,1,0:T(8,128)}, f32[8,128,128]{2,1,0:T(8,128)S(1)}, u32[]{:S(2)}, u32[]{:S(2)}) collective-permute-start(f32[8,128,128]{2,1,0:T(8,128)} %sort_blocks.1.refs_0_), channel_id=1, source_target_pairs={{0,8},{1,9},{2,10},{3,11},{4,12},{5,13},{6,14},{7,15},{8,0},{9,1},... | collective-permute-start | bytes 1572872 | tf_op jit(solution)/shard_map/ppermute | solution.py:37
  12.7 5.1 %collective-permute-start = (s32[64,2]{0,1:T(2,128)S(1)}, s32[64,2]{0,1:T(2,128)S(1)}, u32[]{:S(2)}, u32[]{:S(2)}) collective-permute-start(s32[64,2]{0,1:T(2,128)S(1)} %copy-done.3), channel_id=1, source_target_pairs={{0,0},{1,1},{2,2},{3,3},{4,4},{5,5},{6,6},{7,7},{8,136},{9,137},{1... | collective-permute-start | bytes 1544 | tf_op jit(solution)/shard_map/ppermute | solution.py:37
  17.8 7.6 %collective-permute-done = s32[64,2]{0,1:T(2,128)S(1)} collective-permute-done((s32[64,2]{0,1:T(2,128)S(1)}, s32[64,2]{0,1:T(2,128)S(1)}, u32[]{:S(2)}, u32[]{:S(2)}) %collective-permute-start) | collective-permute-done | bytes 544 | tf_op jit(solution)/shard_map/ppermute | solution.py:37
  38.4 4.0 %collective-permute-start.7 = (f32[8,128,128]{2,1,0:T(8,128)S(1)}, f32[8,128,128]{2,1,0:T(8,128)S(1)}, u32[]{:S(2)}, u32[]{:S(2)}) collective-permute-start(f32[8,128,128]{2,1,0:T(8,128)S(1)} %collective-permute-done.5.refs_1_), channel_id=1, source_target_pairs={{0,8},{1,9},{2,10},{3,11},{4,12},{5,13},{6,14},{7,15},{8,0},{9,1},... | collective-permute-start | bytes 1572872 | tf_op jit(solution)/shard_map/ppermute | solution.py:37
  42.4 5.6 %collective-permute-start.2 = (s32[2,64]{1,0:T(2,128)S(1)}, s32[2,64]{1,0:T(2,128)S(1)}, u32[]{:S(2)}, u32[]{:S(2)}) collective-permute-start(s32[2,64]{1,0:T(2,128)S(1)} %pad_add_fusion.1), channel_id=1, source_target_pairs={{0,16},{1,17},{2,18},{3,19},{4,20},{5,21},{6,22},{7,23},{8,24},{9,... | collective-permute-start | bytes 1544 | tf_op jit(solution)/shard_map/ppermute | solution.py:37
  50.9 4.3 %collective-permute-start.10 = (f32[8,128,128]{2,1,0:T(8,128)S(1)}, f32[8,128,128]{2,1,0:T(8,128)S(1)}, u32[]{:S(2)}, u32[]{:S(2)}) collective-permute-start(f32[8,128,128]{2,1,0:T(8,128)S(1)} %collective-permute-done.8.refs_0_), channel_id=1, source_target_pairs={{0,8},{1,9},{2,10},{3,11},{4,12},{5,13},{6,14},{7,15},{8,0},{9,1},... | collective-permute-start | bytes 1572872 | tf_op jit(solution)/shard_map/ppermute | solution.py:37
  63.5 5.9 %collective-permute-done.13.refs_1_ = f32[8,128,128]{2,1,0:T(8,128)S(1)} collective-permute-done((f32[8,128,128]{2,1,0:T(8,128)S(1)}, f32[8,128,128]{2,1,0:T(8,128)S(1)}, u32[]{:S(2)}, u32[]{:S(2)}) %collective-permute-start.13) | collective-permute-done | bytes 524320 | tf_op jit(solution)/shard_map/ppermute | solution.py:37
  71.3 4.5 %collective-permute-start.14 = (f32[8,128,128]{2,1,0:T(8,128)S(1)}, f32[8,128,128]{2,1,0:T(8,128)S(1)}, u32[]{:S(2)}, u32[]{:S(2)}) collective-permute-start(f32[8,128,128]{2,1,0:T(8,128)S(1)} %collective-permute-done.12.refs_0_), channel_id=1, source_target_pairs={{0,8},{1,9},{2,10},{3,11},{4,12},{5,13},{6,14},{7,15},{8,0},{9,1},... | collective-permute-start | bytes 1572872 | tf_op jit(solution)/shard_map/ppermute | solution.py:37
  85.5 9.6 %products_1.1 = (f32[16,128,128]{2,1,0:T(8,128)S(1)}, f32[16,128,128]{2,1,0:T(8,128)S(1)}, f32[16,128,128]{2,1,0:T(8,128)S(1)}, f32[16,128,128]{2,1,0:T(8,128)S(1)}) custom-call(s32[2]{0:T(128)S(1)} %pad_add_fusion.2.where_ref, s32[4,64]{1,0:T(4,128)S(1)} %pad_add_fusion.codes_ref, bf16[1,512,512]{2,1,0:T(8,128)(2,1)S(1)} %get-tuple-element.37.refs_0_, ...), custom_call_target="tpu_custom_call" | custom-call | tf_op jit(solution)/shard_map/products_1/pallas_call | solution.py:190
  95.1 4.9 %collective-permute-start.22 = (f32[16,128,128]{2,1,0:T(8,128)S(1)}, f32[16,128,128]{2,1,0:T(8,128)S(1)}, u32[]{:S(2)}, u32[]{:S(2)}) collective-permute-start(f32[16,128,128]{2,1,0:T(8,128)S(1)} %get-tuple-element.59), channel_id=1, source_target_pairs={{0,3},{1,0},{2,1},{3,2},{4,7},{5,4},{6,5},{7,6},{8,28},{9,29},{10,... | collective-permute-start | bytes 3145736 | tf_op jit(solution)/shard_map/ppermute | solution.py:37
  105.2 9.6 %products_0.1 = (f32[16,128,128]{2,1,0:T(8,128)S(1)}, f32[16,128,128]{2,1,0:T(8,128)S(1)}, f32[16,128,128]{2,1,0:T(8,128)S(1)}, f32[16,128,128]{2,1,0:T(8,128)S(1)}) custom-call(s32[2]{0:T(128)S(1)} %pad_add_fusion.2.where_ref, s32[4,64]{1,0:T(4,128)S(1)} %pad_add_fusion.codes_ref, bf16[1,512,512]{2,1,0:T(8,128)(2,1)S(1)} %get-tuple-element.37.refs_0_, ...), custom_call_target="tpu_custom_call" | custom-call | tf_op jit(solution)/shard_map/products_0/pallas_call | solution.py:190
  114.8 3.4 %collective-permute-start.26 = (f32[16,128,128]{2,1,0:T(8,128)S(1)}, f32[16,128,128]{2,1,0:T(8,128)S(1)}, u32[]{:S(2)}, u32[]{:S(2)}) collective-permute-start(f32[16,128,128]{2,1,0:T(8,128)S(1)} %get-tuple-element.60), channel_id=1, source_target_pairs={{0,1},{1,2},{2,3},{3,0},{4,5},{5,6},{6,7},{7,4},{8,12},{9,13},{10,... | collective-permute-start | bytes 3145736 | tf_op jit(solution)/shard_map/ppermute | solution.py:37
  118.3 3.4 %collective-permute-start.27 = (f32[16,128,128]{2,1,0:T(8,128)S(1)}, f32[16,128,128]{2,1,0:T(8,128)S(1)}, u32[]{:S(2)}, u32[]{:S(2)}) collective-permute-start(f32[16,128,128]{2,1,0:T(8,128)S(1)} %get-tuple-element.61), channel_id=1, source_target_pairs={{0,2},{1,3},{2,0},{3,1},{4,6},{5,7},{6,4},{7,5},{8,24},{9,25},{10,... | collective-permute-start | bytes 3145736 | tf_op jit(solution)/shard_map/ppermute | solution.py:37
  121.7 12.6 %collective-permute-done.22 = f32[16,128,128]{2,1,0:T(8,128)S(1)} collective-permute-done((f32[16,128,128]{2,1,0:T(8,128)S(1)}, f32[16,128,128]{2,1,0:T(8,128)S(1)}, u32[]{:S(2)}, u32[]{:S(2)}) %collective-permute-start.22) | collective-permute-done | bytes 1048608 | tf_op jit(solution)/shard_map/ppermute | solution.py:37
  134.2 5.3 %collective-permute-start.28 = (f32[16,128,128]{2,1,0:T(8,128)S(1)}, f32[16,128,128]{2,1,0:T(8,128)S(1)}, u32[]{:S(2)}, u32[]{:S(2)}) collective-permute-start(f32[16,128,128]{2,1,0:T(8,128)S(1)} %get-tuple-element.62), channel_id=1, source_target_pairs={{0,3},{1,0},{2,1},{3,2},{4,7},{5,4},{6,5},{7,6},{8,28},{9,29},{10,... | collective-permute-start | bytes 3145736 | tf_op jit(solution)/shard_map/ppermute | solution.py:37
  139.8 3.8 %collective-permute-start.25 = (f32[4,128,128]{2,1,0:T(8,128)S(1)}, f32[4,128,128]{2,1,0:T(8,128)S(1)}, u32[]{:S(2)}, u32[]{:S(2)}) collective-permute-start(f32[4,128,128]{2,1,0:T(8,128)S(1)} %get-tuple-element.75), channel_id=1, source_target_pairs={{0,20},{1,21},{2,22},{3,23},{4,0},{5,1},{6,2},{7,3},{8,11},{9,8},{... | collective-permute-start | bytes 786440 | tf_op jit(solution)/shard_map/ppermute | solution.py:37
  145.6 4.4 %collective-permute-done.25 = f32[4,128,128]{2,1,0:T(8,128)S(1)} collective-permute-done((f32[4,128,128]{2,1,0:T(8,128)S(1)}, f32[4,128,128]{2,1,0:T(8,128)S(1)}, u32[]{:S(2)}, u32[]{:S(2)}) %collective-permute-start.25) | collective-permute-done | bytes 262176 | tf_op jit(solution)/shard_map/ppermute | solution.py:37
  149.9 3.6 %collective-permute-start.23 = (f32[4,128,128]{2,1,0:T(8,128)S(1)}, f32[4,128,128]{2,1,0:T(8,128)S(1)}, u32[]{:S(2)}, u32[]{:S(2)}) collective-permute-start(f32[4,128,128]{2,1,0:T(8,128)S(1)} %get-tuple-element.74), channel_id=1, source_target_pairs={{0,16},{1,17},{2,18},{3,19},{4,20},{5,21},{6,22},{7,23},{8,10},{9,... | collective-permute-start | bytes 786440 | tf_op jit(solution)/shard_map/ppermute | solution.py:37
  155.4 3.2 %collective-permute-done.23 = f32[4,128,128]{2,1,0:T(8,128)S(1)} collective-permute-done((f32[4,128,128]{2,1,0:T(8,128)S(1)}, f32[4,128,128]{2,1,0:T(8,128)S(1)}, u32[]{:S(2)}, u32[]{:S(2)}) %collective-permute-start.23) | collective-permute-done | bytes 262176 | tf_op jit(solution)/shard_map/ppermute | solution.py:37
  158.7 5.2 %collective-permute-start.29 = (f32[4,128,128]{2,1,0:T(8,128)S(1)}, f32[4,128,128]{2,1,0:T(8,128)S(1)}, u32[]{:S(2)}, u32[]{:S(2)}) collective-permute-start(f32[4,128,128]{2,1,0:T(8,128)S(1)} %fusion.2), channel_id=1, source_target_pairs={{8,392},{9,393},{10,394},{11,395},{12,396},{13,397},{14,398},{15,3... | collective-permute-start | bytes 786440 | tf_op jit(solution)/shard_map/ppermute | solution.py:37
  165.4 3.6 %collective-permute-start.31 = (f32[4,128,128]{2,1,0:T(8,128)S(1)}, f32[4,128,128]{2,1,0:T(8,128)S(1)}, u32[]{:S(2)}, u32[]{:S(2)}) collective-permute-start(f32[4,128,128]{2,1,0:T(8,128)S(1)} %get-tuple-element.73), channel_id=1, source_target_pairs={{0,16},{1,17},{2,18},{3,19},{4,20},{5,21},{6,22},{7,23},{8,10},{9,... | collective-permute-start | bytes 786440 | tf_op jit(solution)/shard_map/ppermute | solution.py:37
  169.0 3.2 %collective-permute-start.32 = (f32[4,128,128]{2,1,0:T(8,128)S(1)}, f32[4,128,128]{2,1,0:T(8,128)S(1)}, u32[]{:S(2)}, u32[]{:S(2)}) collective-permute-start(f32[4,128,128]{2,1,0:T(8,128)S(1)} %get-tuple-element.72), channel_id=1, source_target_pairs={{0,4},{1,5},{2,6},{3,7},{4,16},{5,17},{6,18},{7,19},{8,9},{9,10},{... | collective-permute-start | bytes 786440 | tf_op jit(solution)/shard_map/ppermute | solution.py:37
  172.2 3.3 %collective-permute-start.33 = (f32[4,128,128]{2,1,0:T(8,128)S(1)}, f32[4,128,128]{2,1,0:T(8,128)S(1)}, u32[]{:S(2)}, u32[]{:S(2)}) collective-permute-start(f32[4,128,128]{2,1,0:T(8,128)S(1)} %get-tuple-element.71), channel_id=1, source_target_pairs={{0,20},{1,21},{2,22},{3,23},{4,0},{5,1},{6,2},{7,3},{8,11},{9,8},{... | collective-permute-start | bytes 786440 | tf_op jit(solution)/shard_map/ppermute | solution.py:37
  175.5 7.6 %collective-permute-done.29 = f32[4,128,128]{2,1,0:T(8,128)S(1)} collective-permute-done((f32[4,128,128]{2,1,0:T(8,128)S(1)}, f32[4,128,128]{2,1,0:T(8,128)S(1)}, u32[]{:S(2)}, u32[]{:S(2)}) %collective-permute-start.29) | collective-permute-done | bytes 262176 | tf_op jit(solution)/shard_map/ppermute | solution.py:37
  (76 shorter events, 54.0 us)
Async XLA Ops:
  1.9 23.4 %collective-permute-start.3 = (f32[8,128,128]{2,1,0:T(8,128)}, f32[8,128,128]{2,1,0:T(8,128)S(1)}, u32[]{:S(2)}, u32[]{:S(2)}) collective-permute-start(f32[8,128,128]{2,1,0:T(8,128)} %sort_blocks.1.refs_0_), channel_id=1, source_target_pairs={{0,8},{1,9},{2,10},{3,11},{4,12},{5,13},{6,14},{7,15},{8,0},{9,1},... | collective-permute-start | bytes 1572872 | tf_op jit(solution)/shard_map/ppermute | solution.py:37
  10.7 20.2 %collective-permute-start.4 = (f32[8,128,128]{2,1,0:T(8,128)}, f32[8,128,128]{2,1,0:T(8,128)S(1)}, u32[]{:S(2)}, u32[]{:S(2)}) collective-permute-start(f32[8,128,128]{2,1,0:T(8,128)} %sort_blocks.1.refs_0_), channel_id=1, source_target_pairs={{0,480},{1,481},{2,482},{3,483},{4,484},{5,485},{6,486},{7,487},{8... | collective-permute-start | bytes 1572872 | tf_op jit(solution)/shard_map/ppermute | solution.py:37
  12.7 12.6 %collective-permute-start = (s32[64,2]{0,1:T(2,128)S(1)}, s32[64,2]{0,1:T(2,128)S(1)}, u32[]{:S(2)}, u32[]{:S(2)}) collective-permute-start(s32[64,2]{0,1:T(2,128)S(1)} %copy-done.3), channel_id=1, source_target_pairs={{0,0},{1,1},{2,2},{3,3},{4,4},{5,5},{6,6},{7,7},{8,136},{9,137},{1... | collective-permute-start | bytes 1544 | tf_op jit(solution)/shard_map/ppermute | solution.py:37
  25.3 11.1 %collective-permute-start.5 = (f32[8,128,128]{2,1,0:T(8,128)S(1)}, f32[8,128,128]{2,1,0:T(8,128)S(1)}, u32[]{:S(2)}, u32[]{:S(2)}) collective-permute-start(f32[8,128,128]{2,1,0:T(8,128)S(1)} %collective-permute-done.3.refs_1_), channel_id=1, source_target_pairs={{0,480},{1,481},{2,482},{3,483},{4,484},{5,485},{6,486},{7,487},{8... | collective-permute-start | bytes 1572872 | tf_op jit(solution)/shard_map/ppermute | solution.py:37
  30.9 18.0 %collective-permute-start.6 = (f32[8,128,128]{2,1,0:T(8,128)S(1)}, f32[8,128,128]{2,1,0:T(8,128)S(1)}, u32[]{:S(2)}, u32[]{:S(2)}) collective-permute-start(f32[8,128,128]{2,1,0:T(8,128)S(1)} %collective-permute-done.4.refs_0_), channel_id=1, source_target_pairs={{0,8},{1,9},{2,10},{3,11},{4,12},{5,13},{6,14},{7,15},{8,0},{9,1},... | collective-permute-start | bytes 1572872 | tf_op jit(solution)/shard_map/ppermute | solution.py:37
  33.4 15.6 %collective-permute-start.8 = (f32[8,128,128]{2,1,0:T(8,128)S(1)}, f32[8,128,128]{2,1,0:T(8,128)S(1)}, u32[]{:S(2)}, u32[]{:S(2)}) collective-permute-start(f32[8,128,128]{2,1,0:T(8,128)S(1)} %collective-permute-done.4.refs_0_), channel_id=1, source_target_pairs={{0,480},{1,481},{2,482},{3,483},{4,484},{5,485},{6,486},{7,487},{8... | collective-permute-start | bytes 1572872 | tf_op jit(solution)/shard_map/ppermute | solution.py:37
  36.5 18.8 %collective-permute-start.9 = (f32[8,128,128]{2,1,0:T(8,128)S(1)}, f32[8,128,128]{2,1,0:T(8,128)S(1)}, u32[]{:S(2)}, u32[]{:S(2)}) collective-permute-start(f32[8,128,128]{2,1,0:T(8,128)S(1)} %collective-permute-done.5.refs_1_), channel_id=1, source_target_pairs={{0,480},{1,481},{2,482},{3,483},{4,484},{5,485},{6,486},{7,487},{8... | collective-permute-start | bytes 1572872 | tf_op jit(solution)/shard_map/ppermute | solution.py:37
  38.4 16.9 %collective-permute-start.7 = (f32[8,128,128]{2,1,0:T(8,128)S(1)}, f32[8,128,128]{2,1,0:T(8,128)S(1)}, u32[]{:S(2)}, u32[]{:S(2)}) collective-permute-start(f32[8,128,128]{2,1,0:T(8,128)S(1)} %collective-permute-done.5.refs_1_), channel_id=1, source_target_pairs={{0,8},{1,9},{2,10},{3,11},{4,12},{5,13},{6,14},{7,15},{8,0},{9,1},... | collective-permute-start | bytes 1572872 | tf_op jit(solution)/shard_map/ppermute | solution.py:37
  48.9 11.4 %collective-permute-start.12 = (f32[8,128,128]{2,1,0:T(8,128)S(1)}, f32[8,128,128]{2,1,0:T(8,128)S(1)}, u32[]{:S(2)}, u32[]{:S(2)}) collective-permute-start(f32[8,128,128]{2,1,0:T(8,128)S(1)} %collective-permute-done.8.refs_0_), channel_id=1, source_target_pairs={{0,480},{1,481},{2,482},{3,483},{4,484},{5,485},{6,486},{7,487},{8... | collective-permute-start | bytes 1572872 | tf_op jit(solution)/shard_map/ppermute | solution.py:37
  60.3 17.4 %collective-permute-start.16 = (f32[8,128,128]{2,1,0:T(8,128)S(1)}, f32[8,128,128]{2,1,0:T(8,128)S(1)}, u32[]{:S(2)}, u32[]{:S(2)}) collective-permute-start(f32[8,128,128]{2,1,0:T(8,128)S(1)} %collective-permute-done.12.refs_0_), channel_id=1, source_target_pairs={{0,480},{1,481},{2,482},{3,483},{4,484},{5,485},{6,486},{7,487},{8... | collective-permute-start | bytes 1572872 | tf_op jit(solution)/shard_map/ppermute | solution.py:37
  69.4 11.2 %collective-permute-start.17 = (f32[8,128,128]{2,1,0:T(8,128)S(1)}, f32[8,128,128]{2,1,0:T(8,128)S(1)}, u32[]{:S(2)}, u32[]{:S(2)}) collective-permute-start(f32[8,128,128]{2,1,0:T(8,128)S(1)} %collective-permute-done.13.refs_1_), channel_id=1, source_target_pairs={{0,480},{1,481},{2,482},{3,483},{4,484},{5,485},{6,486},{7,487},{8... | collective-permute-start | bytes 1572872 | tf_op jit(solution)/shard_map/ppermute | solution.py:37
  71.3 12.4 %collective-permute-start.14 = (f32[8,128,128]{2,1,0:T(8,128)S(1)}, f32[8,128,128]{2,1,0:T(8,128)S(1)}, u32[]{:S(2)}, u32[]{:S(2)}) collective-permute-start(f32[8,128,128]{2,1,0:T(8,128)S(1)} %collective-permute-done.12.refs_0_), channel_id=1, source_target_pairs={{0,8},{1,9},{2,10},{3,11},{4,12},{5,13},{6,14},{7,15},{8,0},{9,1},... | collective-permute-start | bytes 1572872 | tf_op jit(solution)/shard_map/ppermute | solution.py:37
  95.1 39.1 %collective-permute-start.22 = (f32[16,128,128]{2,1,0:T(8,128)S(1)}, f32[16,128,128]{2,1,0:T(8,128)S(1)}, u32[]{:S(2)}, u32[]{:S(2)}) collective-permute-start(f32[16,128,128]{2,1,0:T(8,128)S(1)} %get-tuple-element.59), channel_id=1, source_target_pairs={{0,3},{1,0},{2,1},{3,2},{4,7},{5,4},{6,5},{7,6},{8,28},{9,29},{10,... | collective-permute-start | bytes 3145736 | tf_op jit(solution)/shard_map/ppermute | solution.py:37
  100.0 39.5 %collective-permute-start.21 = (f32[16,128,128]{2,1,0:T(8,128)S(1)}, f32[16,128,128]{2,1,0:T(8,128)S(1)}, u32[]{:S(2)}, u32[]{:S(2)}) collective-permute-start(f32[16,128,128]{2,1,0:T(8,128)S(1)} %get-tuple-element.58), channel_id=1, source_target_pairs={{0,2},{1,3},{2,0},{3,1},{4,6},{5,7},{6,4},{7,5},{8,24},{9,25},{10,... | collective-permute-start | bytes 3145736 | tf_op jit(solution)/shard_map/ppermute | solution.py:37
  102.2 37.3 %collective-permute-start.20 = (f32[16,128,128]{2,1,0:T(8,128)S(1)}, f32[16,128,128]{2,1,0:T(8,128)S(1)}, u32[]{:S(2)}, u32[]{:S(2)}) collective-permute-start(f32[16,128,128]{2,1,0:T(8,128)S(1)} %get-tuple-element.57), channel_id=1, source_target_pairs={{0,1},{1,2},{2,3},{3,0},{4,5},{5,6},{6,7},{7,4},{8,12},{9,13},{10,... | collective-permute-start | bytes 3145736 | tf_op jit(solution)/shard_map/ppermute | solution.py:37
  114.8 50.3 %collective-permute-start.26 = (f32[16,128,128]{2,1,0:T(8,128)S(1)}, f32[16,128,128]{2,1,0:T(8,128)S(1)}, u32[]{:S(2)}, u32[]{:S(2)}) collective-permute-start(f32[16,128,128]{2,1,0:T(8,128)S(1)} %get-tuple-element.60), channel_id=1, source_target_pairs={{0,1},{1,2},{2,3},{3,0},{4,5},{5,6},{6,7},{7,4},{8,12},{9,13},{10,... | collective-permute-start | bytes 3145736 | tf_op jit(solution)/shard_map/ppermute | solution.py:37
  118.3 46.9 %collective-permute-start.27 = (f32[16,128,128]{2,1,0:T(8,128)S(1)}, f32[16,128,128]{2,1,0:T(8,128)S(1)}, u32[]{:S(2)}, u32[]{:S(2)}) collective-permute-start(f32[16,128,128]{2,1,0:T(8,128)S(1)} %get-tuple-element.61), channel_id=1, source_target_pairs={{0,2},{1,3},{2,0},{3,1},{4,6},{5,7},{6,4},{7,5},{8,24},{9,25},{10,... | collective-permute-start | bytes 3145736 | tf_op jit(solution)/shard_map/ppermute | solution.py:37
  134.2 30.9 %collective-permute-start.28 = (f32[16,128,128]{2,1,0:T(8,128)S(1)}, f32[16,128,128]{2,1,0:T(8,128)S(1)}, u32[]{:S(2)}, u32[]{:S(2)}) collective-permute-start(f32[16,128,128]{2,1,0:T(8,128)S(1)} %get-tuple-element.62), channel_id=1, source_target_pairs={{0,3},{1,0},{2,1},{3,2},{4,7},{5,4},{6,5},{7,6},{8,28},{9,29},{10,... | collective-permute-start | bytes 3145736 | tf_op jit(solution)/shard_map/ppermute | solution.py:37
  143.6 11.7 %collective-permute-start.24 = (f32[4,128,128]{2,1,0:T(8,128)S(1)}, f32[4,128,128]{2,1,0:T(8,128)S(1)}, u32[]{:S(2)}, u32[]{:S(2)}) collective-permute-start(f32[4,128,128]{2,1,0:T(8,128)S(1)} %get-tuple-element.76), channel_id=1, source_target_pairs={{0,4},{1,5},{2,6},{3,7},{4,16},{5,17},{6,18},{7,19},{8,9},{9,10},{... | collective-permute-start | bytes 786440 | tf_op jit(solution)/shard_map/ppermute | solution.py:37
  158.7 24.4 %collective-permute-start.29 = (f32[4,128,128]{2,1,0:T(8,128)S(1)}, f32[4,128,128]{2,1,0:T(8,128)S(1)}, u32[]{:S(2)}, u32[]{:S(2)}) collective-permute-start(f32[4,128,128]{2,1,0:T(8,128)S(1)} %fusion.2), channel_id=1, source_target_pairs={{8,392},{9,393},{10,394},{11,395},{12,396},{13,397},{14,398},{15,3... | collective-permute-start | bytes 786440 | tf_op jit(solution)/shard_map/ppermute | solution.py:37
  163.8 19.6 %collective-permute-start.30 = (f32[4,128,128]{2,1,0:T(8,128)S(1)}, f32[4,128,128]{2,1,0:T(8,128)S(1)}, u32[]{:S(2)}, u32[]{:S(2)}) collective-permute-start(f32[4,128,128]{2,1,0:T(8,128)S(1)} %fusion.2), channel_id=1, source_target_pairs={{0,392},{1,393},{2,394},{3,395},{4,396},{5,397},{6,398},{7,399},{2... | collective-permute-start | bytes 786440 | tf_op jit(solution)/shard_map/ppermute | solution.py:37
  165.4 18.0 %collective-permute-start.31 = (f32[4,128,128]{2,1,0:T(8,128)S(1)}, f32[4,128,128]{2,1,0:T(8,128)S(1)}, u32[]{:S(2)}, u32[]{:S(2)}) collective-permute-start(f32[4,128,128]{2,1,0:T(8,128)S(1)} %get-tuple-element.73), channel_id=1, source_target_pairs={{0,16},{1,17},{2,18},{3,19},{4,20},{5,21},{6,22},{7,23},{8,10},{9,... | collective-permute-start | bytes 786440 | tf_op jit(solution)/shard_map/ppermute | solution.py:37
  169.0 14.4 %collective-permute-start.32 = (f32[4,128,128]{2,1,0:T(8,128)S(1)}, f32[4,128,128]{2,1,0:T(8,128)S(1)}, u32[]{:S(2)}, u32[]{:S(2)}) collective-permute-start(f32[4,128,128]{2,1,0:T(8,128)S(1)} %get-tuple-element.72), channel_id=1, source_target_pairs={{0,4},{1,5},{2,6},{3,7},{4,16},{5,17},{6,18},{7,19},{8,9},{9,10},{... | collective-permute-start | bytes 786440 | tf_op jit(solution)/shard_map/ppermute | solution.py:37
  172.2 11.3 %collective-permute-start.33 = (f32[4,128,128]{2,1,0:T(8,128)S(1)}, f32[4,128,128]{2,1,0:T(8,128)S(1)}, u32[]{:S(2)}, u32[]{:S(2)}) collective-permute-start(f32[4,128,128]{2,1,0:T(8,128)S(1)} %get-tuple-element.71), channel_id=1, source_target_pairs={{0,20},{1,21},{2,22},{3,23},{4,0},{5,1},{6,2},{7,3},{8,11},{9,8},{... | collective-permute-start | bytes 786440 | tf_op jit(solution)/shard_map/ppermute | solution.py:37
  (15 other events, 147.4 us)

commit v8 on v7

--- a/solution.py
+++ b/solution.py
@@ -270,11 +270,11 @@
     their_a, their_b = [None], [None]
     for k in range(1, REACH + 1):
         next_a, next_b = mine_a[-1], mine_b[-1]
-        if k == 1:
+        if k == 2:
             next_b = after(next_b, placed)
-        if k == 2:
+        if k == 3:
             next_b = after(next_b, chip_codes)
-        if k == 3:
+        if k == 4:
             next_b = after(next_b, codes)
         if k > 2:
             next_a = after(next_a, their_a[k - 2])

time: 190 us -> 187 us (0.984)
  waiting for transfers between devices: 46.3 us -> 41.1 us
  starting transfers between devices: 112 us -> 114 us
    ppermute x35, waiting for transfers between devices: 46.3 us -> 41.1 us  [send(): return lax.ppermute(value, AXES, pairs)]
    ppermute x35, starting transfers between devices: 112 us -> 114 us  [send(): return lax.ppermute(value, AXES, pairs)]
  transfers between devices with their start and end apart: 35 -> 35, of which waited for: 12 -> 11; matrix products, arithmetic and copies ran while one was open for 0% -> 0% of each run, Pallas kernels for 7% -> 7%
where the time goes in v8:
time: 187 us; the launch traced here: 184 us
  starting transfers between devices  114 us (61%)
  waiting for transfers between devices  41.1 us (22%)
  Pallas kernels  25.4 us (14%)
  other arithmetic  1.92 us (1%)
    ppermute x35, starting transfers between devices, send(): return lax.ppermute(value, AXES, pairs)  114 us
    ppermute x35, waiting for transfers between devices, send(): return lax.ppermute(value, AXES, pairs)  41.1 us
    pallas_call x2, Pallas kernels, chunk_products(): pl.pallas_call(functools.partial(chunk_kernel, chunk), out_shape=[jax.Sha...  19.3 us
    pallas_call x5, Pallas kernels, split_rows(): pl.pallas_call(split_kernel, out_shape=[jax.ShapeDtypeStruct((len(panels)...  4.24 us
  transfers between devices with their start and end apart: 35, of which 11 were waited for; matrix products, arithmetic and copies ran while one was open for 0% of the time, Pallas kernels for 7%

profile of v8, /device:TPU:1, one launch (start us, length us, event | category | flops | bytes accessed | tf_op | source)
XLA Modules:
  0.0 183.6 jit_solution(14017587514152763987)
XLA Ops:
  1.9 8.8 %collective-permute-start.3 = (f32[8,128,128]{2,1,0:T(8,128)}, f32[8,128,128]{2,1,0:T(8,128)S(1)}, u32[]{:S(2)}, u32[]{:S(2)}) collective-permute-start(f32[8,128,128]{2,1,0:T(8,128)} %sort_blocks.1.refs_0_), channel_id=1, source_target_pairs={{0,8},{1,9},{2,10},{3,11},{4,12},{5,13},{6,14},{7,15},{8,0},{9,1},... | collective-permute-start | bytes 1572872 | tf_op jit(solution)/shard_map/ppermute | solution.py:37
  12.7 5.1 %collective-permute-start = (s32[64,2]{0,1:T(2,128)S(1)}, s32[64,2]{0,1:T(2,128)S(1)}, u32[]{:S(2)}, u32[]{:S(2)}) collective-permute-start(s32[64,2]{0,1:T(2,128)S(1)} %copy-done.1), channel_id=1, source_target_pairs={{0,0},{1,1},{2,2},{3,3},{4,4},{5,5},{6,6},{7,7},{8,136},{9,137},{1... | collective-permute-start | bytes 1544 | tf_op jit(solution)/shard_map/ppermute | solution.py:37
  17.8 3.5 %collective-permute-start.5 = (f32[8,128,128]{2,1,0:T(8,128)S(1)}, f32[8,128,128]{2,1,0:T(8,128)S(1)}, u32[]{:S(2)}, u32[]{:S(2)}) collective-permute-start(f32[8,128,128]{2,1,0:T(8,128)S(1)} %collective-permute-done.3.refs_1_), channel_id=1, source_target_pairs={{0,480},{1,481},{2,482},{3,483},{4,484},{5,485},{6,486},{7,487},{8... | collective-permute-start | bytes 1572872 | tf_op jit(solution)/shard_map/ppermute | solution.py:37
  21.3 4.0 %collective-permute-done = s32[64,2]{0,1:T(2,128)S(1)} collective-permute-done((s32[64,2]{0,1:T(2,128)S(1)}, s32[64,2]{0,1:T(2,128)S(1)}, u32[]{:S(2)}, u32[]{:S(2)}) %collective-permute-start) | collective-permute-done | bytes 544 | tf_op jit(solution)/shard_map/ppermute | solution.py:37
  32.6 4.2 %collective-permute-start.7 = (f32[8,128,128]{2,1,0:T(8,128)S(1)}, f32[8,128,128]{2,1,0:T(8,128)S(1)}, u32[]{:S(2)}, u32[]{:S(2)}) collective-permute-start(f32[8,128,128]{2,1,0:T(8,128)S(1)} %collective-permute-done.5.refs_1_), channel_id=1, source_target_pairs={{0,8},{1,9},{2,10},{3,11},{4,12},{5,13},{6,14},{7,15},{8,0},{9,1},... | collective-permute-start | bytes 1572872 | tf_op jit(solution)/shard_map/ppermute | solution.py:37
  42.7 3.4 %collective-permute-start.10 = (f32[8,128,128]{2,1,0:T(8,128)S(1)}, f32[8,128,128]{2,1,0:T(8,128)S(1)}, u32[]{:S(2)}, u32[]{:S(2)}) collective-permute-start(f32[8,128,128]{2,1,0:T(8,128)S(1)} %collective-permute-done.8.refs_0_), channel_id=1, source_target_pairs={{0,8},{1,9},{2,10},{3,11},{4,12},{5,13},{6,14},{7,15},{8,0},{9,1},... | collective-permute-start | bytes 1572872 | tf_op jit(solution)/shard_map/ppermute | solution.py:37
  48.9 3.7 %collective-permute-start.11 = (f32[8,128,128]{2,1,0:T(8,128)S(1)}, f32[8,128,128]{2,1,0:T(8,128)S(1)}, u32[]{:S(2)}, u32[]{:S(2)}) collective-permute-start(f32[8,128,128]{2,1,0:T(8,128)S(1)} %collective-permute-done.9.refs_1_), channel_id=1, source_target_pairs={{0,8},{1,9},{2,10},{3,11},{4,12},{5,13},{6,14},{7,15},{8,0},{9,1},... | collective-permute-start | bytes 1572872 | tf_op jit(solution)/shard_map/ppermute | solution.py:37
  52.6 6.7 %collective-permute-start.2 = (s32[2,64]{1,0:T(2,128)S(1)}, s32[2,64]{1,0:T(2,128)S(1)}, u32[]{:S(2)}, u32[]{:S(2)}) collective-permute-start(s32[2,64]{1,0:T(2,128)S(1)} %pad_add_fusion.1), channel_id=1, source_target_pairs={{0,16},{1,17},{2,18},{3,19},{4,20},{5,21},{6,22},{7,23},{8,24},{9,... | collective-permute-start | bytes 1544 | tf_op jit(solution)/shard_map/ppermute | solution.py:37
  65.5 4.3 %collective-permute-start.14 = (f32[8,128,128]{2,1,0:T(8,128)S(1)}, f32[8,128,128]{2,1,0:T(8,128)S(1)}, u32[]{:S(2)}, u32[]{:S(2)}) collective-permute-start(f32[8,128,128]{2,1,0:T(8,128)S(1)} %collective-permute-done.12.refs_0_), channel_id=1, source_target_pairs={{0,8},{1,9},{2,10},{3,11},{4,12},{5,13},{6,14},{7,15},{8,0},{9,1},... | collective-permute-start | bytes 1572872 | tf_op jit(solution)/shard_map/ppermute | solution.py:37
  82.5 9.6 %products_1.1 = (f32[16,128,128]{2,1,0:T(8,128)S(1)}, f32[16,128,128]{2,1,0:T(8,128)S(1)}, f32[16,128,128]{2,1,0:T(8,128)S(1)}, f32[16,128,128]{2,1,0:T(8,128)S(1)}) custom-call(s32[2]{0:T(128)S(1)} %pad_add_fusion.2.where_ref, s32[4,64]{1,0:T(4,128)S(1)} %pad_add_fusion.codes_ref, bf16[1,512,512]{2,1,0:T(8,128)(2,1)S(1)} %get-tuple-element.37.refs_0_, ...), custom_call_target="tpu_custom_call" | custom-call | tf_op jit(solution)/shard_map/products_1/pallas_call | solution.py:190
  92.2 4.9 %collective-permute-start.22 = (f32[16,128,128]{2,1,0:T(8,128)S(1)}, f32[16,128,128]{2,1,0:T(8,128)S(1)}, u32[]{:S(2)}, u32[]{:S(2)}) collective-permute-start(f32[16,128,128]{2,1,0:T(8,128)S(1)} %get-tuple-element.59), channel_id=1, source_target_pairs={{0,3},{1,0},{2,1},{3,2},{4,7},{5,4},{6,5},{7,6},{8,28},{9,29},{10,... | collective-permute-start | bytes 3145736 | tf_op jit(solution)/shard_map/ppermute | solution.py:37
  102.2 9.6 %products_0.1 = (f32[16,128,128]{2,1,0:T(8,128)S(1)}, f32[16,128,128]{2,1,0:T(8,128)S(1)}, f32[16,128,128]{2,1,0:T(8,128)S(1)}, f32[16,128,128]{2,1,0:T(8,128)S(1)}) custom-call(s32[2]{0:T(128)S(1)} %pad_add_fusion.2.where_ref, s32[4,64]{1,0:T(4,128)S(1)} %pad_add_fusion.codes_ref, bf16[1,512,512]{2,1,0:T(8,128)(2,1)S(1)} %get-tuple-element.37.refs_0_, ...), custom_call_target="tpu_custom_call" | custom-call | tf_op jit(solution)/shard_map/products_0/pallas_call | solution.py:190
  111.8 3.4 %collective-permute-start.26 = (f32[16,128,128]{2,1,0:T(8,128)S(1)}, f32[16,128,128]{2,1,0:T(8,128)S(1)}, u32[]{:S(2)}, u32[]{:S(2)}) collective-permute-start(f32[16,128,128]{2,1,0:T(8,128)S(1)} %get-tuple-element.60), channel_id=1, source_target_pairs={{0,1},{1,2},{2,3},{3,0},{4,5},{5,6},{6,7},{7,4},{8,12},{9,13},{10,... | collective-permute-start | bytes 3145736 | tf_op jit(solution)/shard_map/ppermute | solution.py:37
  115.3 3.4 %collective-permute-start.27 = (f32[16,128,128]{2,1,0:T(8,128)S(1)}, f32[16,128,128]{2,1,0:T(8,128)S(1)}, u32[]{:S(2)}, u32[]{:S(2)}) collective-permute-start(f32[16,128,128]{2,1,0:T(8,128)S(1)} %get-tuple-element.61), channel_id=1, source_target_pairs={{0,2},{1,3},{2,0},{3,1},{4,6},{5,7},{6,4},{7,5},{8,24},{9,25},{10,... | collective-permute-start | bytes 3145736 | tf_op jit(solution)/shard_map/ppermute | solution.py:37
  118.7 12.6 %collective-permute-done.22 = f32[16,128,128]{2,1,0:T(8,128)S(1)} collective-permute-done((f32[16,128,128]{2,1,0:T(8,128)S(1)}, f32[16,128,128]{2,1,0:T(8,128)S(1)}, u32[]{:S(2)}, u32[]{:S(2)}) %collective-permute-start.22) | collective-permute-done | bytes 1048608 | tf_op jit(solution)/shard_map/ppermute | solution.py:37
  131.2 5.3 %collective-permute-start.28 = (f32[16,128,128]{2,1,0:T(8,128)S(1)}, f32[16,128,128]{2,1,0:T(8,128)S(1)}, u32[]{:S(2)}, u32[]{:S(2)}) collective-permute-start(f32[16,128,128]{2,1,0:T(8,128)S(1)} %get-tuple-element.62), channel_id=1, source_target_pairs={{0,3},{1,0},{2,1},{3,2},{4,7},{5,4},{6,5},{7,6},{8,28},{9,29},{10,... | collective-permute-start | bytes 3145736 | tf_op jit(solution)/shard_map/ppermute | solution.py:37
  136.8 3.8 %collective-permute-start.25 = (f32[4,128,128]{2,1,0:T(8,128)S(1)}, f32[4,128,128]{2,1,0:T(8,128)S(1)}, u32[]{:S(2)}, u32[]{:S(2)}) collective-permute-start(f32[4,128,128]{2,1,0:T(8,128)S(1)} %get-tuple-element.75), channel_id=1, source_target_pairs={{0,20},{1,21},{2,22},{3,23},{4,0},{5,1},{6,2},{7,3},{8,11},{9,8},{... | collective-permute-start | bytes 786440 | tf_op jit(solution)/shard_map/ppermute | solution.py:37
  142.6 4.4 %collective-permute-done.25 = f32[4,128,128]{2,1,0:T(8,128)S(1)} collective-permute-done((f32[4,128,128]{2,1,0:T(8,128)S(1)}, f32[4,128,128]{2,1,0:T(8,128)S(1)}, u32[]{:S(2)}, u32[]{:S(2)}) %collective-permute-start.25) | collective-permute-done | bytes 262176 | tf_op jit(solution)/shard_map/ppermute | solution.py:37
  146.9 3.6 %collective-permute-start.23 = (f32[4,128,128]{2,1,0:T(8,128)S(1)}, f32[4,128,128]{2,1,0:T(8,128)S(1)}, u32[]{:S(2)}, u32[]{:S(2)}) collective-permute-start(f32[4,128,128]{2,1,0:T(8,128)S(1)} %get-tuple-element.74), channel_id=1, source_target_pairs={{0,16},{1,17},{2,18},{3,19},{4,20},{5,21},{6,22},{7,23},{8,10},{9,... | collective-permute-start | bytes 786440 | tf_op jit(solution)/shard_map/ppermute | solution.py:37
  152.4 3.2 %collective-permute-done.23 = f32[4,128,128]{2,1,0:T(8,128)S(1)} collective-permute-done((f32[4,128,128]{2,1,0:T(8,128)S(1)}, f32[4,128,128]{2,1,0:T(8,128)S(1)}, u32[]{:S(2)}, u32[]{:S(2)}) %collective-permute-start.23) | collective-permute-done | bytes 262176 | tf_op jit(solution)/shard_map/ppermute | solution.py:37
  160.2 4.3 %collective-permute-start.31 = (f32[4,128,128]{2,1,0:T(8,128)S(1)}, f32[4,128,128]{2,1,0:T(8,128)S(1)}, u32[]{:S(2)}, u32[]{:S(2)}) collective-permute-start(f32[4,128,128]{2,1,0:T(8,128)S(1)} %get-tuple-element.73), channel_id=1, source_target_pairs={{0,16},{1,17},{2,18},{3,19},{4,20},{5,21},{6,22},{7,23},{8,10},{9,... | collective-permute-start | bytes 786440 | tf_op jit(solution)/shard_map/ppermute | solution.py:37
  164.4 3.2 %collective-permute-start.32 = (f32[4,128,128]{2,1,0:T(8,128)S(1)}, f32[4,128,128]{2,1,0:T(8,128)S(1)}, u32[]{:S(2)}, u32[]{:S(2)}) collective-permute-start(f32[4,128,128]{2,1,0:T(8,128)S(1)} %get-tuple-element.72), channel_id=1, source_target_pairs={{0,4},{1,5},{2,6},{3,7},{4,16},{5,17},{6,18},{7,19},{8,9},{9,10},{... | collective-permute-start | bytes 786440 | tf_op jit(solution)/shard_map/ppermute | solution.py:37
  167.6 3.3 %collective-permute-start.33 = (f32[4,128,128]{2,1,0:T(8,128)S(1)}, f32[4,128,128]{2,1,0:T(8,128)S(1)}, u32[]{:S(2)}, u32[]{:S(2)}) collective-permute-start(f32[4,128,128]{2,1,0:T(8,128)S(1)} %get-tuple-element.71), channel_id=1, source_target_pairs={{0,20},{1,21},{2,22},{3,23},{4,0},{5,1},{6,2},{7,3},{8,11},{9,8},{... | collective-permute-start | bytes 786440 | tf_op jit(solution)/shard_map/ppermute | solution.py:37
  171.0 9.0 %collective-permute-done.29 = f32[4,128,128]{2,1,0:T(8,128)S(1)} collective-permute-done((f32[4,128,128]{2,1,0:T(8,128)S(1)}, f32[4,128,128]{2,1,0:T(8,128)S(1)}, u32[]{:S(2)}, u32[]{:S(2)}) %collective-permute-start.29) | collective-permute-done | bytes 262176 | tf_op jit(solution)/shard_map/ppermute | solution.py:37
  (72 shorter events, 55.8 us)
Async XLA Ops:
  1.9 15.8 %collective-permute-start.3 = (f32[8,128,128]{2,1,0:T(8,128)}, f32[8,128,128]{2,1,0:T(8,128)S(1)}, u32[]{:S(2)}, u32[]{:S(2)}) collective-permute-start(f32[8,128,128]{2,1,0:T(8,128)} %sort_blocks.1.refs_0_), channel_id=1, source_target_pairs={{0,8},{1,9},{2,10},{3,11},{4,12},{5,13},{6,14},{7,15},{8,0},{9,1},... | collective-permute-start | bytes 1572872 | tf_op jit(solution)/shard_map/ppermute | solution.py:37
  10.7 14.6 %collective-permute-start.4 = (f32[8,128,128]{2,1,0:T(8,128)}, f32[8,128,128]{2,1,0:T(8,128)S(1)}, u32[]{:S(2)}, u32[]{:S(2)}) collective-permute-start(f32[8,128,128]{2,1,0:T(8,128)} %sort_blocks.1.refs_0_), channel_id=1, source_target_pairs={{0,480},{1,481},{2,482},{3,483},{4,484},{5,485},{6,486},{7,487},{8... | collective-permute-start | bytes 1572872 | tf_op jit(solution)/shard_map/ppermute | solution.py:37
  12.7 12.7 %collective-permute-start = (s32[64,2]{0,1:T(2,128)S(1)}, s32[64,2]{0,1:T(2,128)S(1)}, u32[]{:S(2)}, u32[]{:S(2)}) collective-permute-start(s32[64,2]{0,1:T(2,128)S(1)} %copy-done.1), channel_id=1, source_target_pairs={{0,0},{1,1},{2,2},{3,3},{4,4},{5,5},{6,6},{7,7},{8,136},{9,137},{1... | collective-permute-start | bytes 1544 | tf_op jit(solution)/shard_map/ppermute | solution.py:37
  25.4 14.7 %collective-permute-start.6 = (f32[8,128,128]{2,1,0:T(8,128)S(1)}, f32[8,128,128]{2,1,0:T(8,128)S(1)}, u32[]{:S(2)}, u32[]{:S(2)}) collective-permute-start(f32[8,128,128]{2,1,0:T(8,128)S(1)} %collective-permute-done.4.refs_0_), channel_id=1, source_target_pairs={{0,8},{1,9},{2,10},{3,11},{4,12},{5,13},{6,14},{7,15},{8,0},{9,1},... | collective-permute-start | bytes 1572872 | tf_op jit(solution)/shard_map/ppermute | solution.py:37
  27.3 12.8 %collective-permute-start.8 = (f32[8,128,128]{2,1,0:T(8,128)S(1)}, f32[8,128,128]{2,1,0:T(8,128)S(1)}, u32[]{:S(2)}, u32[]{:S(2)}) collective-permute-start(f32[8,128,128]{2,1,0:T(8,128)S(1)} %collective-permute-done.4.refs_0_), channel_id=1, source_target_pairs={{0,480},{1,481},{2,482},{3,483},{4,484},{5,485},{6,486},{7,487},{8... | collective-permute-start | bytes 1572872 | tf_op jit(solution)/shard_map/ppermute | solution.py:37
  29.9 16.2 %collective-permute-start.9 = (f32[8,128,128]{2,1,0:T(8,128)S(1)}, f32[8,128,128]{2,1,0:T(8,128)S(1)}, u32[]{:S(2)}, u32[]{:S(2)}) collective-permute-start(f32[8,128,128]{2,1,0:T(8,128)S(1)} %collective-permute-done.5.refs_1_), channel_id=1, source_target_pairs={{0,480},{1,481},{2,482},{3,483},{4,484},{5,485},{6,486},{7,487},{8... | collective-permute-start | bytes 1572872 | tf_op jit(solution)/shard_map/ppermute | solution.py:37
  32.6 13.5 %collective-permute-start.7 = (f32[8,128,128]{2,1,0:T(8,128)S(1)}, f32[8,128,128]{2,1,0:T(8,128)S(1)}, u32[]{:S(2)}, u32[]{:S(2)}) collective-permute-start(f32[8,128,128]{2,1,0:T(8,128)S(1)} %collective-permute-done.5.refs_1_), channel_id=1, source_target_pairs={{0,8},{1,9},{2,10},{3,11},{4,12},{5,13},{6,14},{7,15},{8,0},{9,1},... | collective-permute-start | bytes 1572872 | tf_op jit(solution)/shard_map/ppermute | solution.py:37
  40.0 20.3 %collective-permute-start.12 = (f32[8,128,128]{2,1,0:T(8,128)S(1)}, f32[8,128,128]{2,1,0:T(8,128)S(1)}, u32[]{:S(2)}, u32[]{:S(2)}) collective-permute-start(f32[8,128,128]{2,1,0:T(8,128)S(1)} %collective-permute-done.8.refs_0_), channel_id=1, source_target_pairs={{0,480},{1,481},{2,482},{3,483},{4,484},{5,485},{6,486},{7,487},{8... | collective-permute-start | bytes 1572872 | tf_op jit(solution)/shard_map/ppermute | solution.py:37
  42.7 17.6 %collective-permute-start.10 = (f32[8,128,128]{2,1,0:T(8,128)S(1)}, f32[8,128,128]{2,1,0:T(8,128)S(1)}, u32[]{:S(2)}, u32[]{:S(2)}) collective-permute-start(f32[8,128,128]{2,1,0:T(8,128)S(1)} %collective-permute-done.8.refs_0_), channel_id=1, source_target_pairs={{0,8},{1,9},{2,10},{3,11},{4,12},{5,13},{6,14},{7,15},{8,0},{9,1},... | collective-permute-start | bytes 1572872 | tf_op jit(solution)/shard_map/ppermute | solution.py:37
  47.0 15.4 %collective-permute-start.13 = (f32[8,128,128]{2,1,0:T(8,128)S(1)}, f32[8,128,128]{2,1,0:T(8,128)S(1)}, u32[]{:S(2)}, u32[]{:S(2)}) collective-permute-start(f32[8,128,128]{2,1,0:T(8,128)S(1)} %collective-permute-done.9.refs_1_), channel_id=1, source_target_pairs={{0,480},{1,481},{2,482},{3,483},{4,484},{5,485},{6,486},{7,487},{8... | collective-permute-start | bytes 1572872 | tf_op jit(solution)/shard_map/ppermute | solution.py:37
  48.9 13.5 %collective-permute-start.11 = (f32[8,128,128]{2,1,0:T(8,128)S(1)}, f32[8,128,128]{2,1,0:T(8,128)S(1)}, u32[]{:S(2)}, u32[]{:S(2)}) collective-permute-start(f32[8,128,128]{2,1,0:T(8,128)S(1)} %collective-permute-done.9.refs_1_), channel_id=1, source_target_pairs={{0,8},{1,9},{2,10},{3,11},{4,12},{5,13},{6,14},{7,15},{8,0},{9,1},... | collective-permute-start | bytes 1572872 | tf_op jit(solution)/shard_map/ppermute | solution.py:37
  63.3 13.9 %collective-permute-start.17 = (f32[8,128,128]{2,1,0:T(8,128)S(1)}, f32[8,128,128]{2,1,0:T(8,128)S(1)}, u32[]{:S(2)}, u32[]{:S(2)}) collective-permute-start(f32[8,128,128]{2,1,0:T(8,128)S(1)} %collective-permute-done.13.refs_1_), channel_id=1, source_target_pairs={{0,480},{1,481},{2,482},{3,483},{4,484},{5,485},{6,486},{7,487},{8... | collective-permute-start | bytes 1572872 | tf_op jit(solution)/shard_map/ppermute | solution.py:37
  65.5 15.2 %collective-permute-start.14 = (f32[8,128,128]{2,1,0:T(8,128)S(1)}, f32[8,128,128]{2,1,0:T(8,128)S(1)}, u32[]{:S(2)}, u32[]{:S(2)}) collective-permute-start(f32[8,128,128]{2,1,0:T(8,128)S(1)} %collective-permute-done.12.refs_0_), channel_id=1, source_target_pairs={{0,8},{1,9},{2,10},{3,11},{4,12},{5,13},{6,14},{7,15},{8,0},{9,1},... | collective-permute-start | bytes 1572872 | tf_op jit(solution)/shard_map/ppermute | solution.py:37
  92.2 39.1 %collective-permute-start.22 = (f32[16,128,128]{2,1,0:T(8,128)S(1)}, f32[16,128,128]{2,1,0:T(8,128)S(1)}, u32[]{:S(2)}, u32[]{:S(2)}) collective-permute-start(f32[16,128,128]{2,1,0:T(8,128)S(1)} %get-tuple-element.59), channel_id=1, source_target_pairs={{0,3},{1,0},{2,1},{3,2},{4,7},{5,4},{6,5},{7,6},{8,28},{9,29},{10,... | collective-permute-start | bytes 3145736 | tf_op jit(solution)/shard_map/ppermute | solution.py:37
  97.0 39.5 %collective-permute-start.21 = (f32[16,128,128]{2,1,0:T(8,128)S(1)}, f32[16,128,128]{2,1,0:T(8,128)S(1)}, u32[]{:S(2)}, u32[]{:S(2)}) collective-permute-start(f32[16,128,128]{2,1,0:T(8,128)S(1)} %get-tuple-element.58), channel_id=1, source_target_pairs={{0,2},{1,3},{2,0},{3,1},{4,6},{5,7},{6,4},{7,5},{8,24},{9,25},{10,... | collective-permute-start | bytes 3145736 | tf_op jit(solution)/shard_map/ppermute | solution.py:37
  99.2 37.3 %collective-permute-start.20 = (f32[16,128,128]{2,1,0:T(8,128)S(1)}, f32[16,128,128]{2,1,0:T(8,128)S(1)}, u32[]{:S(2)}, u32[]{:S(2)}) collective-permute-start(f32[16,128,128]{2,1,0:T(8,128)S(1)} %get-tuple-element.57), channel_id=1, source_target_pairs={{0,1},{1,2},{2,3},{3,0},{4,5},{5,6},{6,7},{7,4},{8,12},{9,13},{10,... | collective-permute-start | bytes 3145736 | tf_op jit(solution)/shard_map/ppermute | solution.py:37
  111.8 48.1 %collective-permute-start.26 = (f32[16,128,128]{2,1,0:T(8,128)S(1)}, f32[16,128,128]{2,1,0:T(8,128)S(1)}, u32[]{:S(2)}, u32[]{:S(2)}) collective-permute-start(f32[16,128,128]{2,1,0:T(8,128)S(1)} %get-tuple-element.60), channel_id=1, source_target_pairs={{0,1},{1,2},{2,3},{3,0},{4,5},{5,6},{6,7},{7,4},{8,12},{9,13},{10,... | collective-permute-start | bytes 3145736 | tf_op jit(solution)/shard_map/ppermute | solution.py:37
  115.3 44.6 %collective-permute-start.27 = (f32[16,128,128]{2,1,0:T(8,128)S(1)}, f32[16,128,128]{2,1,0:T(8,128)S(1)}, u32[]{:S(2)}, u32[]{:S(2)}) collective-permute-start(f32[16,128,128]{2,1,0:T(8,128)S(1)} %get-tuple-element.61), channel_id=1, source_target_pairs={{0,2},{1,3},{2,0},{3,1},{4,6},{5,7},{6,4},{7,5},{8,24},{9,25},{10,... | collective-permute-start | bytes 3145736 | tf_op jit(solution)/shard_map/ppermute | solution.py:37
  131.2 28.7 %collective-permute-start.28 = (f32[16,128,128]{2,1,0:T(8,128)S(1)}, f32[16,128,128]{2,1,0:T(8,128)S(1)}, u32[]{:S(2)}, u32[]{:S(2)}) collective-permute-start(f32[16,128,128]{2,1,0:T(8,128)S(1)} %get-tuple-element.62), channel_id=1, source_target_pairs={{0,3},{1,0},{2,1},{3,2},{4,7},{5,4},{6,5},{7,6},{8,28},{9,29},{10,... | collective-permute-start | bytes 3145736 | tf_op jit(solution)/shard_map/ppermute | solution.py:37
  155.7 24.3 %collective-permute-start.29 = (f32[4,128,128]{2,1,0:T(8,128)S(1)}, f32[4,128,128]{2,1,0:T(8,128)S(1)}, u32[]{:S(2)}, u32[]{:S(2)}) collective-permute-start(f32[4,128,128]{2,1,0:T(8,128)S(1)} %fusion.2), channel_id=1, source_target_pairs={{8,392},{9,393},{10,394},{11,395},{12,396},{13,397},{14,398},{15,3... | collective-permute-start | bytes 786440 | tf_op jit(solution)/shard_map/ppermute | solution.py:37
  158.6 21.5 %collective-permute-start.30 = (f32[4,128,128]{2,1,0:T(8,128)S(1)}, f32[4,128,128]{2,1,0:T(8,128)S(1)}, u32[]{:S(2)}, u32[]{:S(2)}) collective-permute-start(f32[4,128,128]{2,1,0:T(8,128)S(1)} %fusion.2), channel_id=1, source_target_pairs={{0,392},{1,393},{2,394},{3,395},{4,396},{5,397},{6,398},{7,399},{2... | collective-permute-start | bytes 786440 | tf_op jit(solution)/shard_map/ppermute | solution.py:37
  160.2 19.9 %collective-permute-start.31 = (f32[4,128,128]{2,1,0:T(8,128)S(1)}, f32[4,128,128]{2,1,0:T(8,128)S(1)}, u32[]{:S(2)}, u32[]{:S(2)}) collective-permute-start(f32[4,128,128]{2,1,0:T(8,128)S(1)} %get-tuple-element.73), channel_id=1, source_target_pairs={{0,16},{1,17},{2,18},{3,19},{4,20},{5,21},{6,22},{7,23},{8,10},{9,... | collective-permute-start | bytes 786440 | tf_op jit(solution)/shard_map/ppermute | solution.py:37
  164.4 15.6 %collective-permute-start.32 = (f32[4,128,128]{2,1,0:T(8,128)S(1)}, f32[4,128,128]{2,1,0:T(8,128)S(1)}, u32[]{:S(2)}, u32[]{:S(2)}) collective-permute-start(f32[4,128,128]{2,1,0:T(8,128)S(1)} %get-tuple-element.72), channel_id=1, source_target_pairs={{0,4},{1,5},{2,6},{3,7},{4,16},{5,17},{6,18},{7,19},{8,9},{9,10},{... | collective-permute-start | bytes 786440 | tf_op jit(solution)/shard_map/ppermute | solution.py:37
  167.6 12.5 %collective-permute-start.33 = (f32[4,128,128]{2,1,0:T(8,128)S(1)}, f32[4,128,128]{2,1,0:T(8,128)S(1)}, u32[]{:S(2)}, u32[]{:S(2)}) collective-permute-start(f32[4,128,128]{2,1,0:T(8,128)S(1)} %get-tuple-element.71), channel_id=1, source_target_pairs={{0,20},{1,21},{2,22},{3,23},{4,0},{5,1},{6,2},{7,3},{8,11},{9,8},{... | collective-permute-start | bytes 786440 | tf_op jit(solution)/shard_map/ppermute | solution.py:37
  (13 other events, 124.7 us)

commit v9 on v8

--- a/solution.py
+++ b/solution.py
@@ -274,16 +274,14 @@
             next_b = after(next_b, placed)
         if k == 3:
             next_b = after(next_b, chip_codes)
-        if k == 4:
-            next_b = after(next_b, codes)
         if k > 2:
             next_a = after(next_a, their_a[k - 2])
             next_b = after(next_b, split[k - 2][0])
         mine_a.append(send(next_a, ring_z))
         mine_b.append(send(next_b, ring_z))
-        swap_a = mine_a[k] if k < REACH else mine_a[k]
-        their_a.append(send(swap_a, other_core))
-        their_b.append(send(mine_b[k], other_core))
+        their_a.append(send(mine_a[k], other_core))
+        swap_b = mine_b[k] if k < REACH else after(mine_b[k], codes)
+        their_b.append(send(swap_b, other_core))
         split.append(split_rows(where, mine_a[k], mine_b[k], their_a[k], their_b[k]))
     split = [part for pair in split for part in pair]
 

time: 187 us -> 191 us (1.021); the launches traced: 184 us -> 190 us
  waiting for transfers between devices: 41.1 us -> 47.7 us
    ppermute x35, waiting for transfers between devices: 41.1 us -> 47.7 us  [send(): return lax.ppermute(value, AXES, pairs)]
  transfers between devices with their start and end apart: 35 -> 35, of which waited for: 11 -> 13; matrix products, arithmetic and copies ran while one was open for 0% -> 0% of each run, Pallas kernels for 7% -> 7%
where the time goes in v9:
time: 191 us; the launch traced here: 190 us
  starting transfers between devices  114 us (60%)
  waiting for transfers between devices  47.7 us (25%)
  Pallas kernels  25.4 us (13%)
  other arithmetic  1.92 us (1%)
    ppermute x35, starting transfers between devices, send(): return lax.ppermute(value, AXES, pairs)  114 us
    ppermute x35, waiting for transfers between devices, send(): return lax.ppermute(value, AXES, pairs)  47.7 us
    pallas_call x2, Pallas kernels, chunk_products(): pl.pallas_call(functools.partial(chunk_kernel, chunk), out_shape=[jax.Sha...  19.3 us
    pallas_call x5, Pallas kernels, split_rows(): pl.pallas_call(split_kernel, out_shape=[jax.ShapeDtypeStruct((len(panels)...  4.24 us
  transfers between devices with their start and end apart: 35, of which 13 were waited for; matrix products, arithmetic and copies ran while one was open for 0% of the time, Pallas kernels for 7%

profile of v9, /device:TPU:1, one launch (start us, length us, event | category | flops | bytes accessed | tf_op | source)
XLA Modules:
  0.0 189.7 jit_solution(5924060263888219502)
XLA Ops:
  1.9 8.8 %collective-permute-start.3 = (f32[8,128,128]{2,1,0:T(8,128)}, f32[8,128,128]{2,1,0:T(8,128)S(1)}, u32[]{:S(2)}, u32[]{:S(2)}) collective-permute-start(f32[8,128,128]{2,1,0:T(8,128)} %sort_blocks.1.refs_0_), channel_id=1, source_target_pairs={{0,8},{1,9},{2,10},{3,11},{4,12},{5,13},{6,14},{7,15},{8,0},{9,1},... | collective-permute-start | bytes 1572872 | tf_op jit(solution)/shard_map/ppermute | solution.py:37
  12.7 5.1 %collective-permute-start = (s32[64,2]{0,1:T(2,128)S(1)}, s32[64,2]{0,1:T(2,128)S(1)}, u32[]{:S(2)}, u32[]{:S(2)}) collective-permute-start(s32[64,2]{0,1:T(2,128)S(1)} %copy-done.1), channel_id=1, source_target_pairs={{0,0},{1,1},{2,2},{3,3},{4,4},{5,5},{6,6},{7,7},{8,136},{9,137},{1... | collective-permute-start | bytes 1544 | tf_op jit(solution)/shard_map/ppermute | solution.py:37
  17.8 3.5 %collective-permute-start.5 = (f32[8,128,128]{2,1,0:T(8,128)S(1)}, f32[8,128,128]{2,1,0:T(8,128)S(1)}, u32[]{:S(2)}, u32[]{:S(2)}) collective-permute-start(f32[8,128,128]{2,1,0:T(8,128)S(1)} %collective-permute-done.3.refs_1_), channel_id=1, source_target_pairs={{0,480},{1,481},{2,482},{3,483},{4,484},{5,485},{6,486},{7,487},{8... | collective-permute-start | bytes 1572872 | tf_op jit(solution)/shard_map/ppermute | solution.py:37
  21.3 4.0 %collective-permute-done = s32[64,2]{0,1:T(2,128)S(1)} collective-permute-done((s32[64,2]{0,1:T(2,128)S(1)}, s32[64,2]{0,1:T(2,128)S(1)}, u32[]{:S(2)}, u32[]{:S(2)}) %collective-permute-start) | collective-permute-done | bytes 544 | tf_op jit(solution)/shard_map/ppermute | solution.py:37
  32.6 4.2 %collective-permute-start.7 = (f32[8,128,128]{2,1,0:T(8,128)S(1)}, f32[8,128,128]{2,1,0:T(8,128)S(1)}, u32[]{:S(2)}, u32[]{:S(2)}) collective-permute-start(f32[8,128,128]{2,1,0:T(8,128)S(1)} %collective-permute-done.5.refs_1_), channel_id=1, source_target_pairs={{0,8},{1,9},{2,10},{3,11},{4,12},{5,13},{6,14},{7,15},{8,0},{9,1},... | collective-permute-start | bytes 1572872 | tf_op jit(solution)/shard_map/ppermute | solution.py:37
  42.7 3.4 %collective-permute-start.10 = (f32[8,128,128]{2,1,0:T(8,128)S(1)}, f32[8,128,128]{2,1,0:T(8,128)S(1)}, u32[]{:S(2)}, u32[]{:S(2)}) collective-permute-start(f32[8,128,128]{2,1,0:T(8,128)S(1)} %collective-permute-done.8.refs_0_), channel_id=1, source_target_pairs={{0,8},{1,9},{2,10},{3,11},{4,12},{5,13},{6,14},{7,15},{8,0},{9,1},... | collective-permute-start | bytes 1572872 | tf_op jit(solution)/shard_map/ppermute | solution.py:37
  55.1 5.1 %collective-permute-done.13.refs_1_ = f32[8,128,128]{2,1,0:T(8,128)S(1)} collective-permute-done((f32[8,128,128]{2,1,0:T(8,128)S(1)}, f32[8,128,128]{2,1,0:T(8,128)S(1)}, u32[]{:S(2)}, u32[]{:S(2)}) %collective-permute-start.13) | collective-permute-done | bytes 524320 | tf_op jit(solution)/shard_map/ppermute | solution.py:37
  62.1 6.1 %collective-permute-start.2 = (s32[2,64]{1,0:T(2,128)S(1)}, s32[2,64]{1,0:T(2,128)S(1)}, u32[]{:S(2)}, u32[]{:S(2)}) collective-permute-start(s32[2,64]{1,0:T(2,128)S(1)} %pad_add_fusion.1), channel_id=1, source_target_pairs={{0,16},{1,17},{2,18},{3,19},{4,20},{5,21},{6,22},{7,23},{8,24},{9,... | collective-permute-start | bytes 1544 | tf_op jit(solution)/shard_map/ppermute | solution.py:37
  69.2 6.4 %collective-permute-start.14 = (f32[8,128,128]{2,1,0:T(8,128)S(1)}, f32[8,128,128]{2,1,0:T(8,128)S(1)}, u32[]{:S(2)}, u32[]{:S(2)}) collective-permute-start(f32[8,128,128]{2,1,0:T(8,128)S(1)} %collective-permute-done.12.refs_0_), channel_id=1, source_target_pairs={{0,8},{1,9},{2,10},{3,11},{4,12},{5,13},{6,14},{7,15},{8,0},{9,1},... | collective-permute-start | bytes 1572872 | tf_op jit(solution)/shard_map/ppermute | solution.py:37
  84.6 9.6 %products_1.1 = (f32[16,128,128]{2,1,0:T(8,128)S(1)}, f32[16,128,128]{2,1,0:T(8,128)S(1)}, f32[16,128,128]{2,1,0:T(8,128)S(1)}, f32[16,128,128]{2,1,0:T(8,128)S(1)}) custom-call(s32[2]{0:T(128)S(1)} %pad_add_fusion.2.where_ref, s32[4,64]{1,0:T(4,128)S(1)} %pad_add_fusion.codes_ref, bf16[1,512,512]{2,1,0:T(8,128)(2,1)S(1)} %get-tuple-element.37.refs_0_, ...), custom_call_target="tpu_custom_call" | custom-call | tf_op jit(solution)/shard_map/products_1/pallas_call | solution.py:190
  94.2 4.9 %collective-permute-start.22 = (f32[16,128,128]{2,1,0:T(8,128)S(1)}, f32[16,128,128]{2,1,0:T(8,128)S(1)}, u32[]{:S(2)}, u32[]{:S(2)}) collective-permute-start(f32[16,128,128]{2,1,0:T(8,128)S(1)} %get-tuple-element.59), channel_id=1, source_target_pairs={{0,3},{1,0},{2,1},{3,2},{4,7},{5,4},{6,5},{7,6},{8,28},{9,29},{10,... | collective-permute-start | bytes 3145736 | tf_op jit(solution)/shard_map/ppermute | solution.py:37
  104.3 9.6 %products_0.1 = (f32[16,128,128]{2,1,0:T(8,128)S(1)}, f32[16,128,128]{2,1,0:T(8,128)S(1)}, f32[16,128,128]{2,1,0:T(8,128)S(1)}, f32[16,128,128]{2,1,0:T(8,128)S(1)}) custom-call(s32[2]{0:T(128)S(1)} %pad_add_fusion.2.where_ref, s32[4,64]{1,0:T(4,128)S(1)} %pad_add_fusion.codes_ref, bf16[1,512,512]{2,1,0:T(8,128)(2,1)S(1)} %get-tuple-element.37.refs_0_, ...), custom_call_target="tpu_custom_call" | custom-call | tf_op jit(solution)/shard_map/products_0/pallas_call | solution.py:190
  113.9 3.4 %collective-permute-start.26 = (f32[16,128,128]{2,1,0:T(8,128)S(1)}, f32[16,128,128]{2,1,0:T(8,128)S(1)}, u32[]{:S(2)}, u32[]{:S(2)}) collective-permute-start(f32[16,128,128]{2,1,0:T(8,128)S(1)} %get-tuple-element.60), channel_id=1, source_target_pairs={{0,1},{1,2},{2,3},{3,0},{4,5},{5,6},{6,7},{7,4},{8,12},{9,13},{10,... | collective-permute-start | bytes 3145736 | tf_op jit(solution)/shard_map/ppermute | solution.py:37
  117.3 3.4 %collective-permute-start.27 = (f32[16,128,128]{2,1,0:T(8,128)S(1)}, f32[16,128,128]{2,1,0:T(8,128)S(1)}, u32[]{:S(2)}, u32[]{:S(2)}) collective-permute-start(f32[16,128,128]{2,1,0:T(8,128)S(1)} %get-tuple-element.61), channel_id=1, source_target_pairs={{0,2},{1,3},{2,0},{3,1},{4,6},{5,7},{6,4},{7,5},{8,24},{9,25},{10,... | collective-permute-start | bytes 3145736 | tf_op jit(solution)/shard_map/ppermute | solution.py:37
  120.7 12.6 %collective-permute-done.22 = f32[16,128,128]{2,1,0:T(8,128)S(1)} collective-permute-done((f32[16,128,128]{2,1,0:T(8,128)S(1)}, f32[16,128,128]{2,1,0:T(8,128)S(1)}, u32[]{:S(2)}, u32[]{:S(2)}) %collective-permute-start.22) | collective-permute-done | bytes 1048608 | tf_op jit(solution)/shard_map/ppermute | solution.py:37
  133.3 5.3 %collective-permute-start.28 = (f32[16,128,128]{2,1,0:T(8,128)S(1)}, f32[16,128,128]{2,1,0:T(8,128)S(1)}, u32[]{:S(2)}, u32[]{:S(2)}) collective-permute-start(f32[16,128,128]{2,1,0:T(8,128)S(1)} %get-tuple-element.62), channel_id=1, source_target_pairs={{0,3},{1,0},{2,1},{3,2},{4,7},{5,4},{6,5},{7,6},{8,28},{9,29},{10,... | collective-permute-start | bytes 3145736 | tf_op jit(solution)/shard_map/ppermute | solution.py:37
  138.9 3.9 %collective-permute-start.25 = (f32[4,128,128]{2,1,0:T(8,128)S(1)}, f32[4,128,128]{2,1,0:T(8,128)S(1)}, u32[]{:S(2)}, u32[]{:S(2)}) collective-permute-start(f32[4,128,128]{2,1,0:T(8,128)S(1)} %get-tuple-element.75), channel_id=1, source_target_pairs={{0,20},{1,21},{2,22},{3,23},{4,0},{5,1},{6,2},{7,3},{8,11},{9,8},{... | collective-permute-start | bytes 786440 | tf_op jit(solution)/shard_map/ppermute | solution.py:37
  144.7 4.4 %collective-permute-done.25 = f32[4,128,128]{2,1,0:T(8,128)S(1)} collective-permute-done((f32[4,128,128]{2,1,0:T(8,128)S(1)}, f32[4,128,128]{2,1,0:T(8,128)S(1)}, u32[]{:S(2)}, u32[]{:S(2)}) %collective-permute-start.25) | collective-permute-done | bytes 262176 | tf_op jit(solution)/shard_map/ppermute | solution.py:37
  149.1 3.6 %collective-permute-start.23 = (f32[4,128,128]{2,1,0:T(8,128)S(1)}, f32[4,128,128]{2,1,0:T(8,128)S(1)}, u32[]{:S(2)}, u32[]{:S(2)}) collective-permute-start(f32[4,128,128]{2,1,0:T(8,128)S(1)} %get-tuple-element.74), channel_id=1, source_target_pairs={{0,16},{1,17},{2,18},{3,19},{4,20},{5,21},{6,22},{7,23},{8,10},{9,... | collective-permute-start | bytes 786440 | tf_op jit(solution)/shard_map/ppermute | solution.py:37
  154.5 3.2 %collective-permute-done.23 = f32[4,128,128]{2,1,0:T(8,128)S(1)} collective-permute-done((f32[4,128,128]{2,1,0:T(8,128)S(1)}, f32[4,128,128]{2,1,0:T(8,128)S(1)}, u32[]{:S(2)}, u32[]{:S(2)}) %collective-permute-start.23) | collective-permute-done | bytes 262176 | tf_op jit(solution)/shard_map/ppermute | solution.py:37
  162.2 4.4 %collective-permute-start.31 = (f32[4,128,128]{2,1,0:T(8,128)S(1)}, f32[4,128,128]{2,1,0:T(8,128)S(1)}, u32[]{:S(2)}, u32[]{:S(2)}) collective-permute-start(f32[4,128,128]{2,1,0:T(8,128)S(1)} %get-tuple-element.73), channel_id=1, source_target_pairs={{0,16},{1,17},{2,18},{3,19},{4,20},{5,21},{6,22},{7,23},{8,10},{9,... | collective-permute-start | bytes 786440 | tf_op jit(solution)/shard_map/ppermute | solution.py:37
  166.6 3.2 %collective-permute-start.32 = (f32[4,128,128]{2,1,0:T(8,128)S(1)}, f32[4,128,128]{2,1,0:T(8,128)S(1)}, u32[]{:S(2)}, u32[]{:S(2)}) collective-permute-start(f32[4,128,128]{2,1,0:T(8,128)S(1)} %get-tuple-element.72), channel_id=1, source_target_pairs={{0,4},{1,5},{2,6},{3,7},{4,16},{5,17},{6,18},{7,19},{8,9},{9,10},{... | collective-permute-start | bytes 786440 | tf_op jit(solution)/shard_map/ppermute | solution.py:37
  169.8 3.3 %collective-permute-start.33 = (f32[4,128,128]{2,1,0:T(8,128)S(1)}, f32[4,128,128]{2,1,0:T(8,128)S(1)}, u32[]{:S(2)}, u32[]{:S(2)}) collective-permute-start(f32[4,128,128]{2,1,0:T(8,128)S(1)} %get-tuple-element.71), channel_id=1, source_target_pairs={{0,20},{1,21},{2,22},{3,23},{4,0},{5,1},{6,2},{7,3},{8,11},{9,8},{... | collective-permute-start | bytes 786440 | tf_op jit(solution)/shard_map/ppermute | solution.py:37
  173.1 13.0 %collective-permute-done.29 = f32[4,128,128]{2,1,0:T(8,128)S(1)} collective-permute-done((f32[4,128,128]{2,1,0:T(8,128)S(1)}, f32[4,128,128]{2,1,0:T(8,128)S(1)}, u32[]{:S(2)}, u32[]{:S(2)}) %collective-permute-start.29) | collective-permute-done | bytes 262176 | tf_op jit(solution)/shard_map/ppermute | solution.py:37
  (72 shorter events, 55.0 us)
Async XLA Ops:
  1.9 15.8 %collective-permute-start.3 = (f32[8,128,128]{2,1,0:T(8,128)}, f32[8,128,128]{2,1,0:T(8,128)S(1)}, u32[]{:S(2)}, u32[]{:S(2)}) collective-permute-start(f32[8,128,128]{2,1,0:T(8,128)} %sort_blocks.1.refs_0_), channel_id=1, source_target_pairs={{0,8},{1,9},{2,10},{3,11},{4,12},{5,13},{6,14},{7,15},{8,0},{9,1},... | collective-permute-start | bytes 1572872 | tf_op jit(solution)/shard_map/ppermute | solution.py:37
  10.7 14.6 %collective-permute-start.4 = (f32[8,128,128]{2,1,0:T(8,128)}, f32[8,128,128]{2,1,0:T(8,128)S(1)}, u32[]{:S(2)}, u32[]{:S(2)}) collective-permute-start(f32[8,128,128]{2,1,0:T(8,128)} %sort_blocks.1.refs_0_), channel_id=1, source_target_pairs={{0,480},{1,481},{2,482},{3,483},{4,484},{5,485},{6,486},{7,487},{8... | collective-permute-start | bytes 1572872 | tf_op jit(solution)/shard_map/ppermute | solution.py:37
  12.7 12.7 %collective-permute-start = (s32[64,2]{0,1:T(2,128)S(1)}, s32[64,2]{0,1:T(2,128)S(1)}, u32[]{:S(2)}, u32[]{:S(2)}) collective-permute-start(s32[64,2]{0,1:T(2,128)S(1)} %copy-done.1), channel_id=1, source_target_pairs={{0,0},{1,1},{2,2},{3,3},{4,4},{5,5},{6,6},{7,7},{8,136},{9,137},{1... | collective-permute-start | bytes 1544 | tf_op jit(solution)/shard_map/ppermute | solution.py:37
  17.8 12.2 %collective-permute-start.5 = (f32[8,128,128]{2,1,0:T(8,128)S(1)}, f32[8,128,128]{2,1,0:T(8,128)S(1)}, u32[]{:S(2)}, u32[]{:S(2)}) collective-permute-start(f32[8,128,128]{2,1,0:T(8,128)S(1)} %collective-permute-done.3.refs_1_), channel_id=1, source_target_pairs={{0,480},{1,481},{2,482},{3,483},{4,484},{5,485},{6,486},{7,487},{8... | collective-permute-start | bytes 1572872 | tf_op jit(solution)/shard_map/ppermute | solution.py:37
  25.4 14.7 %collective-permute-start.6 = (f32[8,128,128]{2,1,0:T(8,128)S(1)}, f32[8,128,128]{2,1,0:T(8,128)S(1)}, u32[]{:S(2)}, u32[]{:S(2)}) collective-permute-start(f32[8,128,128]{2,1,0:T(8,128)S(1)} %collective-permute-done.4.refs_0_), channel_id=1, source_target_pairs={{0,8},{1,9},{2,10},{3,11},{4,12},{5,13},{6,14},{7,15},{8,0},{9,1},... | collective-permute-start | bytes 1572872 | tf_op jit(solution)/shard_map/ppermute | solution.py:37
  27.3 12.8 %collective-permute-start.8 = (f32[8,128,128]{2,1,0:T(8,128)S(1)}, f32[8,128,128]{2,1,0:T(8,128)S(1)}, u32[]{:S(2)}, u32[]{:S(2)}) collective-permute-start(f32[8,128,128]{2,1,0:T(8,128)S(1)} %collective-permute-done.4.refs_0_), channel_id=1, source_target_pairs={{0,480},{1,481},{2,482},{3,483},{4,484},{5,485},{6,486},{7,487},{8... | collective-permute-start | bytes 1572872 | tf_op jit(solution)/shard_map/ppermute | solution.py:37
  29.9 16.2 %collective-permute-start.9 = (f32[8,128,128]{2,1,0:T(8,128)S(1)}, f32[8,128,128]{2,1,0:T(8,128)S(1)}, u32[]{:S(2)}, u32[]{:S(2)}) collective-permute-start(f32[8,128,128]{2,1,0:T(8,128)S(1)} %collective-permute-done.5.refs_1_), channel_id=1, source_target_pairs={{0,480},{1,481},{2,482},{3,483},{4,484},{5,485},{6,486},{7,487},{8... | collective-permute-start | bytes 1572872 | tf_op jit(solution)/shard_map/ppermute | solution.py:37
  32.6 13.5 %collective-permute-start.7 = (f32[8,128,128]{2,1,0:T(8,128)S(1)}, f32[8,128,128]{2,1,0:T(8,128)S(1)}, u32[]{:S(2)}, u32[]{:S(2)}) collective-permute-start(f32[8,128,128]{2,1,0:T(8,128)S(1)} %collective-permute-done.5.refs_1_), channel_id=1, source_target_pairs={{0,8},{1,9},{2,10},{3,11},{4,12},{5,13},{6,14},{7,15},{8,0},{9,1},... | collective-permute-start | bytes 1572872 | tf_op jit(solution)/shard_map/ppermute | solution.py:37
  40.0 11.1 %collective-permute-start.12 = (f32[8,128,128]{2,1,0:T(8,128)S(1)}, f32[8,128,128]{2,1,0:T(8,128)S(1)}, u32[]{:S(2)}, u32[]{:S(2)}) collective-permute-start(f32[8,128,128]{2,1,0:T(8,128)S(1)} %collective-permute-done.8.refs_0_), channel_id=1, source_target_pairs={{0,480},{1,481},{2,482},{3,483},{4,484},{5,485},{6,486},{7,487},{8... | collective-permute-start | bytes 1572872 | tf_op jit(solution)/shard_map/ppermute | solution.py:37
  51.2 26.3 %collective-permute-start.16 = (f32[8,128,128]{2,1,0:T(8,128)S(1)}, f32[8,128,128]{2,1,0:T(8,128)S(1)}, u32[]{:S(2)}, u32[]{:S(2)}) collective-permute-start(f32[8,128,128]{2,1,0:T(8,128)S(1)} %collective-permute-done.12.refs_0_), channel_id=1, source_target_pairs={{0,480},{1,481},{2,482},{3,483},{4,484},{5,485},{6,486},{7,487},{8... | collective-permute-start | bytes 1572872 | tf_op jit(solution)/shard_map/ppermute | solution.py:37
  60.2 19.7 %collective-permute-start.17 = (f32[8,128,128]{2,1,0:T(8,128)S(1)}, f32[8,128,128]{2,1,0:T(8,128)S(1)}, u32[]{:S(2)}, u32[]{:S(2)}) collective-permute-start(f32[8,128,128]{2,1,0:T(8,128)S(1)} %collective-permute-done.13.refs_1_), channel_id=1, source_target_pairs={{0,480},{1,481},{2,482},{3,483},{4,484},{5,485},{6,486},{7,487},{8... | collective-permute-start | bytes 1572872 | tf_op jit(solution)/shard_map/ppermute | solution.py:37
  69.2 13.4 %collective-permute-start.14 = (f32[8,128,128]{2,1,0:T(8,128)S(1)}, f32[8,128,128]{2,1,0:T(8,128)S(1)}, u32[]{:S(2)}, u32[]{:S(2)}) collective-permute-start(f32[8,128,128]{2,1,0:T(8,128)S(1)} %collective-permute-done.12.refs_0_), channel_id=1, source_target_pairs={{0,8},{1,9},{2,10},{3,11},{4,12},{5,13},{6,14},{7,15},{8,0},{9,1},... | collective-permute-start | bytes 1572872 | tf_op jit(solution)/shard_map/ppermute | solution.py:37
  94.2 39.1 %collective-permute-start.22 = (f32[16,128,128]{2,1,0:T(8,128)S(1)}, f32[16,128,128]{2,1,0:T(8,128)S(1)}, u32[]{:S(2)}, u32[]{:S(2)}) collective-permute-start(f32[16,128,128]{2,1,0:T(8,128)S(1)} %get-tuple-element.59), channel_id=1, source_target_pairs={{0,3},{1,0},{2,1},{3,2},{4,7},{5,4},{6,5},{7,6},{8,28},{9,29},{10,... | collective-permute-start | bytes 3145736 | tf_op jit(solution)/shard_map/ppermute | solution.py:37
  99.1 39.5 %collective-permute-start.21 = (f32[16,128,128]{2,1,0:T(8,128)S(1)}, f32[16,128,128]{2,1,0:T(8,128)S(1)}, u32[]{:S(2)}, u32[]{:S(2)}) collective-permute-start(f32[16,128,128]{2,1,0:T(8,128)S(1)} %get-tuple-element.58), channel_id=1, source_target_pairs={{0,2},{1,3},{2,0},{3,1},{4,6},{5,7},{6,4},{7,5},{8,24},{9,25},{10,... | collective-permute-start | bytes 3145736 | tf_op jit(solution)/shard_map/ppermute | solution.py:37
  101.3 37.3 %collective-permute-start.20 = (f32[16,128,128]{2,1,0:T(8,128)S(1)}, f32[16,128,128]{2,1,0:T(8,128)S(1)}, u32[]{:S(2)}, u32[]{:S(2)}) collective-permute-start(f32[16,128,128]{2,1,0:T(8,128)S(1)} %get-tuple-element.57), channel_id=1, source_target_pairs={{0,1},{1,2},{2,3},{3,0},{4,5},{5,6},{6,7},{7,4},{8,12},{9,13},{10,... | collective-permute-start | bytes 3145736 | tf_op jit(solution)/shard_map/ppermute | solution.py:37
  113.9 48.1 %collective-permute-start.26 = (f32[16,128,128]{2,1,0:T(8,128)S(1)}, f32[16,128,128]{2,1,0:T(8,128)S(1)}, u32[]{:S(2)}, u32[]{:S(2)}) collective-permute-start(f32[16,128,128]{2,1,0:T(8,128)S(1)} %get-tuple-element.60), channel_id=1, source_target_pairs={{0,1},{1,2},{2,3},{3,0},{4,5},{5,6},{6,7},{7,4},{8,12},{9,13},{10,... | collective-permute-start | bytes 3145736 | tf_op jit(solution)/shard_map/ppermute | solution.py:37
  117.3 44.6 %collective-permute-start.27 = (f32[16,128,128]{2,1,0:T(8,128)S(1)}, f32[16,128,128]{2,1,0:T(8,128)S(1)}, u32[]{:S(2)}, u32[]{:S(2)}) collective-permute-start(f32[16,128,128]{2,1,0:T(8,128)S(1)} %get-tuple-element.61), channel_id=1, source_target_pairs={{0,2},{1,3},{2,0},{3,1},{4,6},{5,7},{6,4},{7,5},{8,24},{9,25},{10,... | collective-permute-start | bytes 3145736 | tf_op jit(solution)/shard_map/ppermute | solution.py:37
  133.3 28.7 %collective-permute-start.28 = (f32[16,128,128]{2,1,0:T(8,128)S(1)}, f32[16,128,128]{2,1,0:T(8,128)S(1)}, u32[]{:S(2)}, u32[]{:S(2)}) collective-permute-start(f32[16,128,128]{2,1,0:T(8,128)S(1)} %get-tuple-element.62), channel_id=1, source_target_pairs={{0,3},{1,0},{2,1},{3,2},{4,7},{5,4},{6,5},{7,6},{8,28},{9,29},{10,... | collective-permute-start | bytes 3145736 | tf_op jit(solution)/shard_map/ppermute | solution.py:37
  142.8 11.7 %collective-permute-start.24 = (f32[4,128,128]{2,1,0:T(8,128)S(1)}, f32[4,128,128]{2,1,0:T(8,128)S(1)}, u32[]{:S(2)}, u32[]{:S(2)}) collective-permute-start(f32[4,128,128]{2,1,0:T(8,128)S(1)} %get-tuple-element.76), channel_id=1, source_target_pairs={{0,4},{1,5},{2,6},{3,7},{4,16},{5,17},{6,18},{7,19},{8,9},{9,10},{... | collective-permute-start | bytes 786440 | tf_op jit(solution)/shard_map/ppermute | solution.py:37
  157.8 28.3 %collective-permute-start.29 = (f32[4,128,128]{2,1,0:T(8,128)S(1)}, f32[4,128,128]{2,1,0:T(8,128)S(1)}, u32[]{:S(2)}, u32[]{:S(2)}) collective-permute-start(f32[4,128,128]{2,1,0:T(8,128)S(1)} %fusion.2), channel_id=1, source_target_pairs={{8,392},{9,393},{10,394},{11,395},{12,396},{13,397},{14,398},{15,3... | collective-permute-start | bytes 786440 | tf_op jit(solution)/shard_map/ppermute | solution.py:37
  160.7 25.6 %collective-permute-start.30 = (f32[4,128,128]{2,1,0:T(8,128)S(1)}, f32[4,128,128]{2,1,0:T(8,128)S(1)}, u32[]{:S(2)}, u32[]{:S(2)}) collective-permute-start(f32[4,128,128]{2,1,0:T(8,128)S(1)} %fusion.2), channel_id=1, source_target_pairs={{0,392},{1,393},{2,394},{3,395},{4,396},{5,397},{6,398},{7,399},{2... | collective-permute-start | bytes 786440 | tf_op jit(solution)/shard_map/ppermute | solution.py:37
  162.2 24.1 %collective-permute-start.31 = (f32[4,128,128]{2,1,0:T(8,128)S(1)}, f32[4,128,128]{2,1,0:T(8,128)S(1)}, u32[]{:S(2)}, u32[]{:S(2)}) collective-permute-start(f32[4,128,128]{2,1,0:T(8,128)S(1)} %get-tuple-element.73), channel_id=1, source_target_pairs={{0,16},{1,17},{2,18},{3,19},{4,20},{5,21},{6,22},{7,23},{8,10},{9,... | collective-permute-start | bytes 786440 | tf_op jit(solution)/shard_map/ppermute | solution.py:37
  166.6 19.7 %collective-permute-start.32 = (f32[4,128,128]{2,1,0:T(8,128)S(1)}, f32[4,128,128]{2,1,0:T(8,128)S(1)}, u32[]{:S(2)}, u32[]{:S(2)}) collective-permute-start(f32[4,128,128]{2,1,0:T(8,128)S(1)} %get-tuple-element.72), channel_id=1, source_target_pairs={{0,4},{1,5},{2,6},{3,7},{4,16},{5,17},{6,18},{7,19},{8,9},{9,10},{... | collective-permute-start | bytes 786440 | tf_op jit(solution)/shard_map/ppermute | solution.py:37
  169.8 16.5 %collective-permute-start.33 = (f32[4,128,128]{2,1,0:T(8,128)S(1)}, f32[4,128,128]{2,1,0:T(8,128)S(1)}, u32[]{:S(2)}, u32[]{:S(2)}) collective-permute-start(f32[4,128,128]{2,1,0:T(8,128)S(1)} %get-tuple-element.71), channel_id=1, source_target_pairs={{0,20},{1,21},{2,22},{3,23},{4,0},{5,1},{6,2},{7,3},{8,11},{9,8},{... | collective-permute-start | bytes 786440 | tf_op jit(solution)/shard_map/ppermute | solution.py:37
  (13 other events, 122.3 us)
